TPU v7x, 256 devices: a whole 4x4x8 slice. The times are simulated.
256 devices in a mesh: energy: 64 (over y_lo, z, x), tile: 4 (over y_hi, core).
Axes of the slice: x: 4, y: 4 (y_hi: 2, y_lo: 2; y = y_hi * 2 + y_lo), z: 8, core: 2. Of those that a mesh axis runs over, the one named last changes fastest.
Arguments:
- material_maps: float32 [2, 4, 256, 1024], P(None, None, 'energy', 'tile'), may hold values from -0.3 to 0.3
- spectra: float32 [64, 4, 2], replicated, may hold values from -0.3 to 0.3
- probes: float32 [64, 128, 256], P('energy'), may hold values from -1 to 1, as said below
- offsets: int32 [4, 32, 2], P('tile'), may hold values from 0 to 128
- measured: float32 [64, 4, 32, 128, 128], P('energy', 'tile'), may hold values from 0 to 4
Outputs:
- refined_maps: float32 [2, 4, 256, 1024], P(None, None, 'energy', 'tile')
Inputs may be any that keep to these rules, and one draw needn't show every extreme that they name: `probes`: each probe entry has modulus between 0.5 and 1.
All inputs are finite; a program needn't handle non-finite values.
Results may differ from a plain program's by a relative error of at most 0.0024.
The roundings to bfloat16 on the way count: a program that leaves them out, or rounds other values in their place, can miss the bound.
Values sent between devices are 32-bit elements; how exact they have to be, the bound alone decides.
No kernel may reach another device: no remote copies, remote signals or barrier semaphores. Data moves between devices by JAX's collectives and lax.ppermute only.
A program may use at most 64 MiB of HBM per device.

v0:
```python
import math

import jax
import jax.numpy as jnp
from jax import lax
from jax.sharding import PartitionSpec as P

ITERS = 2
TV_STEPS = 3


DATA_STEP = 0.05
TV_STEP = 0.05
TV_EPS = 0.01


def with_halo(block, sides, width):
    for axis, dim in sides:
        count = lax.axis_size(axis)
        forward = [(i, i + 1) for i in range(count - 1)]
        backward = [(target, source) for source, target in forward]
        low = lax.ppermute(
            lax.slice_in_dim(block, block.shape[dim] - width, None, axis=dim), axis, forward
        )
        high = lax.ppermute(lax.slice_in_dim(block, 0, width, axis=dim), axis, backward)
        block = jnp.concatenate([low, block, high], axis=dim)
    return block


def dft_tables(length):
    index = jnp.arange(length, dtype=jnp.int32)
    phase = index[:, None] * index[None, :] % length
    angle = phase.astype(jnp.float32) * (-2.0 * math.pi / length)
    scale = 1.0 / math.sqrt(length)
    return (
        (jnp.cos(angle) * scale).astype(jnp.bfloat16),
        (jnp.sin(angle) * scale).astype(jnp.bfloat16),
    )


def dft_blocks(real_table, imag_table):
    right_fwd = jnp.concatenate(
        [
            jnp.concatenate([real_table, imag_table], 1),
            jnp.concatenate([-imag_table, real_table], 1),
        ],
        0,
    )
    right_back = jnp.concatenate(
        [
            jnp.concatenate([real_table, -imag_table], 1),
            jnp.concatenate([imag_table, real_table], 1),
        ],
        0,
    )
    stacked = jnp.concatenate([real_table, imag_table], 0)
    return (right_fwd, right_back, stacked)


def mix_all(strips, spectra):
    coeff_real = spectra[:, :, 0]
    coeff_imag = spectra[:, :, 1]
    weights = jnp.stack(
        [jnp.stack([coeff_real, -coeff_imag], 1), jnp.stack([coeff_imag, coeff_real], 1)], 1
    )
    return jnp.einsum(
        "eopm,pmrc->eorc",
        weights,
        strips,
        precision=lax.Precision.HIGHEST,
        preferred_element_type=jnp.float32,
    )


def unmix_all(energy_grads, spectra):
    coeff_real = spectra[:, :, 0]
    coeff_imag = spectra[:, :, 1]
    weights = jnp.stack(
        [jnp.stack([coeff_real, coeff_imag], 1), jnp.stack([-coeff_imag, coeff_real], 1)], 1
    )
    return jnp.einsum(
        "eopm,eprc->omrc",
        weights,
        energy_grads,
        precision=lax.Precision.HIGHEST,
        preferred_element_type=jnp.float32,
    )


def exponent(real_part, imag_part):
    growth = jnp.exp(real_part)
    return jnp.stack([growth * jnp.cos(imag_part), growth * jnp.sin(imag_part)], axis=0)


def conj_times(wave, other):
    return jnp.stack(
        [wave[0] * other[0] + wave[1] * other[1], wave[0] * other[1] - wave[1] * other[0]], axis=0
    )


def tv_div(extended):
    base = extended[:, :, :-1, :-1]
    down = extended[:, :, 1:, :-1] - base
    across = extended[:, :, :-1, 1:] - base
    magnitude = jnp.sqrt(jnp.sum(down * down + across * across, axis=0) + TV_EPS)
    norm_down = down / magnitude
    norm_across = across / magnitude
    return (
        norm_down[:, :, 1:, 1:]
        - norm_down[:, :, :-1, 1:]
        + norm_across[:, :, 1:, 1:]
        - norm_across[:, :, 1:, :-1]
    )


def patch_gradients(pieces, my_probe, counts, blocks):
    right_fwd, right_back, stacked = blocks
    length = my_probe.shape[0]
    probe_real = my_probe[:, :length]
    probe_imag = my_probe[:, length:]
    wave_real = pieces[:, 0]
    wave_imag = pieces[:, 1]
    exit_wave = jnp.concatenate(
        [
            probe_real * wave_real - probe_imag * wave_imag,
            probe_real * wave_imag + probe_imag * wave_real,
        ],
        axis=-1,
    ).astype(jnp.bfloat16)
    first_pass = jnp.einsum(
        "bij,jk->bik", exit_wave, right_fwd, preferred_element_type=jnp.float32
    ).astype(jnp.bfloat16)
    second_pass = jnp.einsum("ij,bjk->bik", stacked, first_pass, preferred_element_type=jnp.float32)
    far_real = second_pass[:, :length, :length] - second_pass[:, length:, length:]
    far_imag = second_pass[:, :length, length:] + second_pass[:, length:, :length]
    misfit = far_real * far_real + far_imag * far_imag - counts
    weighted = jnp.concatenate([misfit * far_real, misfit * far_imag], axis=-1).astype(jnp.bfloat16)
    third_pass = jnp.einsum(
        "bij,jk->bik", weighted, right_back, preferred_element_type=jnp.float32
    ).astype(jnp.bfloat16)
    fourth_pass = jnp.einsum("ij,bjk->bik", stacked, third_pass, preferred_element_type=jnp.float32)
    grad_real = fourth_pass[:, :length, :length] + fourth_pass[:, length:, length:]
    grad_imag = fourth_pass[:, :length, length:] - fourth_pass[:, length:, :length]
    return jnp.stack(
        [
            probe_real * grad_real + probe_imag * grad_imag,
            probe_real * grad_imag - probe_imag * grad_real,
        ],
        axis=1,
    )


def object_gradient(tile_wave, my_probe, my_spots, my_data, blocks):
    length = my_probe.shape[0]
    tile_rows = tile_wave.shape[1]
    tile_cols = tile_wave.shape[2]
    group_size = 8
    patch_index = jnp.arange(length, dtype=jnp.int32)
    row_index = jnp.arange(tile_rows, dtype=jnp.int32)
    col_index = jnp.arange(tile_cols, dtype=jnp.int32)

    def one_group(block_index, running):
        first_patch = block_index * group_size
        where_rows = lax.dynamic_slice_in_dim(my_spots, first_patch, group_size, 0)
        counts = lax.dynamic_slice_in_dim(my_data, first_patch, group_size, 0)
        pieces = jax.vmap(
            lambda location: lax.dynamic_slice(
                tile_wave, (location[0] * 0, location[0], location[1]), (2, length, length)
            )
        )(where_rows)
        updates = patch_gradients(pieces, my_probe, counts, blocks)
        rows_hot = (
            row_index[None, :, None] == where_rows[:, 0][:, None, None] + patch_index[None, None, :]
        ).astype(jnp.float32)
        cols_hot = (
            col_index[None, :, None] == where_rows[:, 1][:, None, None] + patch_index[None, None, :]
        ).astype(jnp.float32)
        shifted = jnp.einsum(
            "gta,gcab->gctb",
            rows_hot,
            updates,
            precision=lax.Precision.HIGHEST,
            preferred_element_type=jnp.float32,
        )
        placed = jnp.einsum(
            "gctb,gsb->cts",
            shifted,
            cols_hot,
            precision=lax.Precision.HIGHEST,
            preferred_element_type=jnp.float32,
        )
        return running + placed

    return lax.fori_loop(
        0, my_spots.shape[0] // group_size, one_group, jnp.zeros(tile_wave.shape, jnp.float32)
    )


def shards(material_maps, spectra, probes, offsets, measured):
    patch_len = probes.shape[1]
    energy_count = spectra.shape[0]
    my_probe = probes[0]
    my_spots = offsets[0]
    my_data = measured[0, 0]
    blocks = dft_blocks(*dft_tables(patch_len))
    factor = DATA_STEP / math.sqrt(energy_count)
    current = material_maps
    for repeat in range(ITERS):
        strip_mix = mix_all(current, spectra)
        mixed_rows = lax.all_to_all(strip_mix, "energy", split_axis=0, concat_axis=2, tiled=True)[0]
        tile_wave = exponent(mixed_rows[0], mixed_rows[1])
        grad_wave = object_gradient(tile_wave, my_probe, my_spots, my_data, blocks)
        grad_exp = conj_times(tile_wave, grad_wave)
        energy_grads = lax.all_to_all(
            grad_exp[None], "energy", split_axis=2, concat_axis=0, tiled=True
        )
        map_grad = unmix_all(energy_grads, spectra)
        current = current - factor * map_grad
        for smooth_pass in range(TV_STEPS):
            extended = with_halo(current, (("energy", 2), ("tile", 3)), 1)
            current = current + TV_STEP * tv_div(extended)
    return current


def solution(mesh):
    in_specs = (
        P(None, None, "energy", "tile"),
        P(),
        P("energy", None, None),
        P("tile", None, None),
        P("energy", "tile", None, None, None),
    )
    out_specs = P(None, None, "energy", "tile")
    return jax.shard_map(shards, mesh=mesh, in_specs=in_specs, out_specs=out_specs, check_vma=False)
```

profile of v0, /device:TPU:8, one launch (start us, length us, event | category | flops | bytes accessed | tf_op | source)
XLA Modules:
  0.0 446.6 jit_solution(1108326021738510749)
XLA Ops:
  1.5 1.4 convolution_bitcast_fusion.5
  4.0 13.0 %all-to-all-start = ((f32[64,2,4,256]{3,2,1,0:T(4,128)}), f32[64,2,4,256]{3,2,1,0:T(4,128)S(1)}, u32[]{:S(2)}, u32[]{:S(2)}) async-start(f32[64,2,4,256]{3,2,1,0:T(4,128)} %copy.61), calls=%async_computation | async-start | bytes 1048576 | tf_op jit(solution)/shard_map/all_to_all | solution.py:210
  17.1 1.8 copy.62
  19.5 13.8 %all-to-all-done = f32[64,2,4,256]{3,2,1,0:T(4,128)S(1)} async-done(((f32[64,2,4,256]{3,2,1,0:T(4,128)}), f32[64,2,4,256]{3,2,1,0:T(4,128)S(1)}, u32[]{:S(2)}, u32[]{:S(2)}) %all-to-all-start) | async-done | bytes 524320 | tf_op jit(solution)/shard_map/all_to_all | solution.py:210
  33.3 2.0 cosine_multiply_fusion.1
  37.2 103.0 %while.41 = (s32[]{:T(128)}, f32[2,256,256]{2,1,0:T(8,128)}, f32[128,256]{1,0:T(8,128)S(1)}, s32[32,2]{0,1:T(2,128)S(1)}, f32[2,256,256]{2,1,0:T(8,128)S(1)}, /*...) while((s32[]{:T(128)}, f32[2,256,256]{2,1,0:T(8,128)}, ...), condition=%wide.region_1.2_spmd.clone.clone, body=%wide.region_0.1_spmd.clone.clone.sunk | while | flops 2959869952 | bytes 21382156 | solution.py:194
  37.3 16.6 %while.44 = (s32[]{:T(128)}, f32[2,256,256]{2,1,0:T(8,128)S(1)}, s32[8,3]{0,1:T(4,128)S(1)}, f32[8,2,128,128]{3,2,0,1:T(8,128)S(1)}, s32[]{:T(128)}) while((s32[]{:T(128)}, f32[2,256,256]{2,1,0:T(8,128)S(1)}, s32[8,3]{0,1:T(4,128)S(1)}, f32[8,2,128,128]{3,2,0,1:T(8,128)S(1)}, s32[]{:T(128)}) %tuple.187), condition=%wide.while_cond, body=%wide.while_body.sunk | while | flops 2 | bytes 262261 | solution.py:167
  59.5 2.7 fusion.205
  62.3 16.6 %while.44 = (s32[]{:T(128)}, f32[2,256,256]{2,1,0:T(8,128)S(1)}, s32[8,3]{0,1:T(4,128)S(1)}, f32[8,2,128,128]{3,2,0,1:T(8,128)S(1)}, s32[]{:T(128)}) while((s32[]{:T(128)}, f32[2,256,256]{2,1,0:T(8,128)S(1)}, s32[8,3]{0,1:T(4,128)S(1)}, f32[8,2,128,128]{3,2,0,1:T(8,128)S(1)}, s32[]{:T(128)}) %tuple.187), condition=%wide.while_cond, body=%wide.while_body.sunk | while | flops 2 | bytes 262261 | solution.py:167
  84.5 3.7 fusion.205
  88.3 16.6 %while.44 = (s32[]{:T(128)}, f32[2,256,256]{2,1,0:T(8,128)S(1)}, s32[8,3]{0,1:T(4,128)S(1)}, f32[8,2,128,128]{3,2,0,1:T(8,128)S(1)}, s32[]{:T(128)}) while((s32[]{:T(128)}, f32[2,256,256]{2,1,0:T(8,128)S(1)}, s32[8,3]{0,1:T(4,128)S(1)}, f32[8,2,128,128]{3,2,0,1:T(8,128)S(1)}, s32[]{:T(128)}) %tuple.187), condition=%wide.while_cond, body=%wide.while_body.sunk | while | flops 2 | bytes 262261 | solution.py:167
  110.5 3.7 fusion.205
  114.3 16.6 %while.44 = (s32[]{:T(128)}, f32[2,256,256]{2,1,0:T(8,128)S(1)}, s32[8,3]{0,1:T(4,128)S(1)}, f32[8,2,128,128]{3,2,0,1:T(8,128)S(1)}, s32[]{:T(128)}) while((s32[]{:T(128)}, f32[2,256,256]{2,1,0:T(8,128)S(1)}, s32[8,3]{0,1:T(4,128)S(1)}, f32[8,2,128,128]{3,2,0,1:T(8,128)S(1)}, s32[]{:T(128)}) %tuple.187), condition=%wide.while_cond, body=%wide.while_body.sunk | while | flops 2 | bytes 262261 | solution.py:167
  136.5 3.7 fusion.205
  140.2 1.4 copy.64
  141.7 1.6 multiply_add_fusion.1
  143.8 23.0 %all_to_all.66 = f32[1,2,256,256]{3,1,0,2:T(2,128)S(1)} all-to-all(f32[1,2,256,256]{3,1,0,2:T(2,128)S(1)} %maximum_bitcast_fusion), channel_id=1, replica_groups=mesh['energy'=64,'tile'=4] {'energy'}, dimensions={2} | all-to-all | bytes 1048576 | tf_op jit(solution)/shard_map/all_to_all | solution.py:214
  167.4 2.6 collective-permute-start
  170.0 7.5 %collective-permute-start.1 = (f32[2,4,1,256]{3,1,2,0:T(4,128)S(1)}, f32[2,4,1,256]{3,1,2,0:T(4,128)S(1)}, u32[]{:S(2)}, u32[]{:S(2)}) collective-permute-start(f32[2,4,1,256]{3,1,2,0:T(4,128)S(1)} %get-tuple-element.762), channel_id=1, source_target_pairs={{4,0},{8,4},{12,8},{16,12},{20,16},{24,20},{28,24},{32,28},{36,32}... | collective-permute-start | bytes 24584 | tf_op jit(solution)/shard_map/ppermute | solution.py:25
  181.6 4.2 collective-permute-done.3
  186.1 1.9 collective-permute-start.4
  188.0 9.0 %collective-permute-start.5 = (f32[2,4,1,256]{3,1,2,0:T(4,128)S(1)}, f32[2,4,1,256]{3,1,2,0:T(4,128)S(1)}, u32[]{:S(2)}, u32[]{:S(2)}) collective-permute-start(f32[2,4,1,256]{3,1,2,0:T(4,128)S(1)} %get-tuple-element.760), channel_id=1, source_target_pairs={{4,0},{8,4},{12,8},{16,12},{20,16},{24,20},{28,24},{32,28},{36,32}... | collective-permute-start | bytes 24584 | tf_op jit(solution)/shard_map/ppermute | solution.py:25
  198.5 5.1 %collective-permute-start.6 = (f32[2,4,6,1]{3,1,2,0:T(4,128)S(1)}, f32[2,4,6,1]{3,1,2,0:T(4,128)S(1)}, u32[]{:S(2)}, u32[]{:S(2)}) collective-permute-start(f32[2,4,6,1]{3,1,2,0:T(4,128)S(1)} %get-tuple-element.748), channel_id=1, source_target_pairs={{0,1},{1,2},{2,3},{4,5},{5,6},{6,7},{8,9},{9,10},{10,11},{12,13},{... | collective-permute-start | bytes 584 | tf_op jit(solution)/shard_map/ppermute | solution.py:22
  205.0 1.7 collective-permute-done.7
  206.9 1.9 collective-permute-start.8
  208.8 8.8 %collective-permute-start.9 = (f32[2,4,1,256]{3,1,2,0:T(4,128)S(1)}, f32[2,4,1,256]{3,1,2,0:T(4,128)S(1)}, u32[]{:S(2)}, u32[]{:S(2)}) collective-permute-start(f32[2,4,1,256]{3,1,2,0:T(4,128)S(1)} %get-tuple-element.758), channel_id=1, source_target_pairs={{4,0},{8,4},{12,8},{16,12},{20,16},{24,20},{28,24},{32,28},{36,32}... | collective-permute-start | bytes 24584 | tf_op jit(solution)/shard_map/ppermute | solution.py:25
  219.1 5.1 %collective-permute-start.10 = (f32[2,4,6,1]{3,1,2,0:T(4,128)S(1)}, f32[2,4,6,1]{3,1,2,0:T(4,128)S(1)}, u32[]{:S(2)}, u32[]{:S(2)}) collective-permute-start(f32[2,4,6,1]{3,1,2,0:T(4,128)S(1)} %get-tuple-element.746), channel_id=1, source_target_pairs={{0,1},{1,2},{2,3},{4,5},{5,6},{6,7},{8,9},{9,10},{10,11},{12,13},{... | collective-permute-start | bytes 584 | tf_op jit(solution)/shard_map/ppermute | solution.py:22
  225.6 1.7 collective-permute-done.11
  229.4 9.4 %all-to-all-start.2 = ((f32[64,2,4,256]{3,2,1,0:T(4,128)}), f32[64,2,4,256]{3,2,1,0:T(4,128)S(1)}, u32[]{:S(2)}, u32[]{:S(2)}) async-start(f32[64,2,4,256]{3,2,1,0:T(4,128)} %copy.70), calls=%async_computation.2 | async-start | bytes 1048576 | tf_op jit(solution)/shard_map/all_to_all | solution.py:210
  238.7 14.1 %all-to-all-done.2 = f32[64,2,4,256]{3,2,1,0:T(4,128)S(1)} async-done(((f32[64,2,4,256]{3,2,1,0:T(4,128)}), f32[64,2,4,256]{3,2,1,0:T(4,128)S(1)}, u32[]{:S(2)}, u32[]{:S(2)}) %all-to-all-start.2) | async-done | bytes 524320 | tf_op jit(solution)/shard_map/all_to_all | solution.py:210
  252.9 2.0 cosine_multiply_fusion
  256.8 102.6 %while.43 = (s32[]{:T(128)}, f32[2,256,256]{2,1,0:T(8,128)}, f32[128,256]{1,0:T(8,128)S(1)}, s32[32,2]{0,1:T(2,128)S(1)}, f32[2,256,256]{2,1,0:T(8,128)S(1)}, /*...) while((s32[]{:T(128)}, f32[2,256,256]{2,1,0:T(8,128)}, ...), condition=%wide.region_6.7_spmd.clone.clone, body=%wide.region_5.6_spmd.clone.clone.sunk | while | flops 2959869952 | bytes 21906464 | solution.py:194
  256.9 16.4 %while.45 = (s32[]{:T(128)}, f32[2,256,256]{2,1,0:T(8,128)S(1)}, s32[8,3]{0,1:T(4,128)S(1)}, f32[8,2,128,128]{3,2,0,1:T(8,128)S(1)}, s32[]{:T(128)}) while((s32[]{:T(128)}, f32[2,256,256]{2,1,0:T(8,128)S(1)}, s32[8,3]{0,1:T(4,128)S(1)}, f32[8,2,128,128]{3,2,0,1:T(8,128)S(1)}, s32[]{:T(128)}) %tuple.184), condition=%wide.while_cond.1, body=%wide.while_body.1.sunk | while | flops 2 | bytes 262261 | solution.py:167
  261.7 1.4 bitcast_dynamic-update-slice_fusion.4
  263.7 1.4 bitcast_dynamic-update-slice_fusion.4
  265.8 1.4 bitcast_dynamic-update-slice_fusion.4
  267.8 1.4 bitcast_dynamic-update-slice_fusion.4
  279.0 2.7 fusion.219
  281.7 16.4 %while.45 = (s32[]{:T(128)}, f32[2,256,256]{2,1,0:T(8,128)S(1)}, s32[8,3]{0,1:T(4,128)S(1)}, f32[8,2,128,128]{3,2,0,1:T(8,128)S(1)}, s32[]{:T(128)}) while((s32[]{:T(128)}, f32[2,256,256]{2,1,0:T(8,128)S(1)}, s32[8,3]{0,1:T(4,128)S(1)}, f32[8,2,128,128]{3,2,0,1:T(8,128)S(1)}, s32[]{:T(128)}) %tuple.184), condition=%wide.while_cond.1, body=%wide.while_body.1.sunk | while | flops 2 | bytes 262261 | solution.py:167
  282.4 1.4 bitcast_dynamic-update-slice_fusion.4
  284.5 1.4 bitcast_dynamic-update-slice_fusion.4
  286.5 1.4 bitcast_dynamic-update-slice_fusion.4
  288.6 1.4 bitcast_dynamic-update-slice_fusion.4
  294.7 1.4 bitcast_dynamic-update-slice_fusion.4
  303.8 3.7 fusion.219
  307.6 16.4 %while.45 = (s32[]{:T(128)}, f32[2,256,256]{2,1,0:T(8,128)S(1)}, s32[8,3]{0,1:T(4,128)S(1)}, f32[8,2,128,128]{3,2,0,1:T(8,128)S(1)}, s32[]{:T(128)}) while((s32[]{:T(128)}, f32[2,256,256]{2,1,0:T(8,128)S(1)}, s32[8,3]{0,1:T(4,128)S(1)}, f32[8,2,128,128]{3,2,0,1:T(8,128)S(1)}, s32[]{:T(128)}) %tuple.184), condition=%wide.while_cond.1, body=%wide.while_body.1.sunk | while | flops 2 | bytes 262261 | solution.py:167
  329.7 3.7 fusion.219
  333.5 16.4 %while.45 = (s32[]{:T(128)}, f32[2,256,256]{2,1,0:T(8,128)S(1)}, s32[8,3]{0,1:T(4,128)S(1)}, f32[8,2,128,128]{3,2,0,1:T(8,128)S(1)}, s32[]{:T(128)}) while((s32[]{:T(128)}, f32[2,256,256]{2,1,0:T(8,128)S(1)}, s32[8,3]{0,1:T(4,128)S(1)}, f32[8,2,128,128]{3,2,0,1:T(8,128)S(1)}, s32[]{:T(128)}) %tuple.184), condition=%wide.while_cond.1, body=%wide.while_body.1.sunk | while | flops 2 | bytes 262261 | solution.py:167
  355.6 3.7 fusion.219
  359.4 1.4 copy.72
  360.8 1.6 multiply_add_fusion
  362.9 24.9 %all_to_all.67 = f32[1,2,256,256]{3,1,0,2:T(2,128)S(1)} all-to-all(f32[1,2,256,256]{3,1,0,2:T(2,128)S(1)} %maximum_bitcast_fusion.1), channel_id=1, replica_groups=mesh['energy'=64,'tile'=4] {'energy'}, dimensions={2} | all-to-all | bytes 1048576 | tf_op jit(solution)/shard_map/all_to_all | solution.py:214
  388.3 2.3 collective-permute-start.12
  390.6 7.8 %collective-permute-start.13 = (f32[2,4,1,256]{3,1,2,0:T(4,128)S(1)}, f32[2,4,1,256]{3,1,2,0:T(4,128)S(1)}, u32[]{:S(2)}, u32[]{:S(2)}) collective-permute-start(f32[2,4,1,256]{3,1,2,0:T(4,128)S(1)} %get-tuple-element.756), channel_id=1, source_target_pairs={{4,0},{8,4},{12,8},{16,12},{20,16},{24,20},{28,24},{32,28},{36,32}... | collective-permute-start | bytes 24584 | tf_op jit(solution)/shard_map/ppermute | solution.py:25
  399.8 2.1 collective-permute-start.14
  403.3 1.7 collective-permute-done.15
  405.3 1.9 collective-permute-start.16
  407.2 8.4 %collective-permute-start.17 = (f32[2,4,1,256]{3,1,2,0:T(4,128)S(1)}, f32[2,4,1,256]{3,1,2,0:T(4,128)S(1)}, u32[]{:S(2)}, u32[]{:S(2)}) collective-permute-start(f32[2,4,1,256]{3,1,2,0:T(4,128)S(1)} %get-tuple-element.754), channel_id=1, source_target_pairs={{4,0},{8,4},{12,8},{16,12},{20,16},{24,20},{28,24},{32,28},{36,32}... | collective-permute-start | bytes 24584 | tf_op jit(solution)/shard_map/ppermute | solution.py:25
  417.0 4.6 %collective-permute-start.18 = (f32[2,4,6,1]{3,1,2,0:T(4,128)S(1)}, f32[2,4,6,1]{3,1,2,0:T(4,128)S(1)}, u32[]{:S(2)}, u32[]{:S(2)}) collective-permute-start(f32[2,4,6,1]{3,1,2,0:T(4,128)S(1)} %get-tuple-element.742), channel_id=1, source_target_pairs={{0,1},{1,2},{2,3},{4,5},{5,6},{6,7},{8,9},{9,10},{10,11},{12,13},{... | collective-permute-start | bytes 584 | tf_op jit(solution)/shard_map/ppermute | solution.py:22
  423.1 1.8 collective-permute-done.19
  425.1 1.9 collective-permute-start.20
  427.1 9.0 %collective-permute-start.21 = (f32[2,4,1,256]{3,1,2,0:T(4,128)S(1)}, f32[2,4,1,256]{3,1,2,0:T(4,128)S(1)}, u32[]{:S(2)}, u32[]{:S(2)}) collective-permute-start(f32[2,4,1,256]{3,1,2,0:T(4,128)S(1)} %get-tuple-element.752), channel_id=1, source_target_pairs={{4,0},{8,4},{12,8},{16,12},{20,16},{24,20},{28,24},{32,28},{36,32}... | collective-permute-start | bytes 24584 | tf_op jit(solution)/shard_map/ppermute | solution.py:25
  437.5 5.1 %collective-permute-start.22 = (f32[2,4,6,1]{3,1,2,0:T(4,128)S(1)}, f32[2,4,6,1]{3,1,2,0:T(4,128)S(1)}, u32[]{:S(2)}, u32[]{:S(2)}) collective-permute-start(f32[2,4,6,1]{3,1,2,0:T(4,128)S(1)} %get-tuple-element.740), channel_id=1, source_target_pairs={{0,1},{1,2},{2,3},{4,5},{5,6},{6,7},{8,9},{9,10},{10,11},{12,13},{... | collective-permute-start | bytes 584 | tf_op jit(solution)/shard_map/ppermute | solution.py:22
  444.1 1.7 collective-permute-done.23
  (457 shorter events, 194.4 us)
Async XLA Ops:
  0.0 17.1 %copy-start.10 = (f32[1,1,32,128,128]{4,3,2,1,0:T(8,128)S(1)}, f32[1,1,32,128,128]{4,3,2,1,0:T(8,128)}, u32[]{:S(2)}) copy-start(f32[1,1,32,128,128]{4,3,2,1,0:T(8,128)} %param.13) | copy-start | bytes 6291460
  1.5 17.5 %copy-start.17 = (f32[64,1,2,4]{0,3,2,1:T(4,128)}, f32[64,1,2,4]{0,3,2,1:T(4,128)S(1)}, u32[]{:S(2)}) copy-start(f32[64,1,2,4]{0,3,2,1:T(4,128)S(1)} %get-tuple-element.764) | copy-start | bytes 6148
  1.5 17.5 %copy-start.19 = (f32[64,1,2,4]{0,3,2,1:T(4,128)}, f32[64,1,2,4]{0,3,2,1:T(4,128)S(1)}, u32[]{:S(2)}) copy-start(f32[64,1,2,4]{0,3,2,1:T(4,128)S(1)} %get-tuple-element.769) | copy-start | bytes 6148
  4.0 29.3 %all-to-all-start = ((f32[64,2,4,256]{3,2,1,0:T(4,128)}), f32[64,2,4,256]{3,2,1,0:T(4,128)S(1)}, u32[]{:S(2)}, u32[]{:S(2)}) async-start(f32[64,2,4,256]{3,2,1,0:T(4,128)} %copy.61), calls=%async_computation | async-start | bytes 1048576 | tf_op jit(solution)/shard_map/all_to_all | solution.py:210
  33.3 3.9 copy-start.2
  33.3 3.9 copy-start.14
  35.6 1.6 copy-start.8
  35.9 0.7 copy-start.9
  53.9 0.6 copy-start
  59.5 2.7 copy-start.3
  78.9 0.6 copy-start
  84.5 3.7 copy-start.3
  104.9 0.6 copy-start
  110.5 3.7 copy-start.3
  130.9 0.6 copy-start
  136.5 3.7 copy-start.3
  141.7 25.1 %copy-start.13 = (f32[2,4,4,256]{3,2,1,0:T(4,128)S(1)}, f32[2,4,4,256]{3,2,1,0:T(4,128)}, u32[]{:S(2)}) copy-start(f32[2,4,4,256]{3,2,1,0:T(4,128)} %param.9) | copy-start | bytes 98308
  141.7 25.1 %copy-start.15 = (f32[64,1,2,4]{0,3,2,1:T(4,128)S(1)}, f32[64,1,2,4]{0,3,2,1:T(4,128)}, u32[]{:S(2)}) copy-start(f32[64,1,2,4]{0,3,2,1:T(4,128)} %get-tuple-element.770) | copy-start | bytes 6148
  166.8 60.7 %copy-start.18 = (f32[64,1,2,4]{0,3,2,1:T(4,128)S(1)}, f32[64,1,2,4]{0,3,2,1:T(4,128)}, u32[]{:S(2)}) copy-start(f32[64,1,2,4]{0,3,2,1:T(4,128)} %copy-done.17) | copy-start | bytes 6148
  166.8 60.7 %copy-start.20 = (f32[64,1,2,4]{0,3,2,1:T(4,128)S(1)}, f32[64,1,2,4]{0,3,2,1:T(4,128)}, u32[]{:S(2)}) copy-start(f32[64,1,2,4]{0,3,2,1:T(4,128)} %copy-done.19) | copy-start | bytes 6148
  167.4 10.1 %collective-permute-start = (f32[2,4,1,256]{3,1,2,0:T(4,128)S(1)}, f32[2,4,1,256]{3,1,2,0:T(4,128)S(1)}, u32[]{:S(2)}, u32[]{:S(2)}) collective-permute-start(f32[2,4,1,256]{3,1,2,0:T(4,128)S(1)} %get-tuple-element.761), channel_id=1, source_target_pairs={{0,4},{4,8},{8,12},{12,16},{16,20},{20,24},{24,28},{28,32},{32,36}... | collective-permute-start | bytes 24584 | tf_op jit(solution)/shard_map/ppermute | solution.py:22
  170.0 8.8 %collective-permute-start.1 = (f32[2,4,1,256]{3,1,2,0:T(4,128)S(1)}, f32[2,4,1,256]{3,1,2,0:T(4,128)S(1)}, u32[]{:S(2)}, u32[]{:S(2)}) collective-permute-start(f32[2,4,1,256]{3,1,2,0:T(4,128)S(1)} %get-tuple-element.762), channel_id=1, source_target_pairs={{4,0},{8,4},{12,8},{16,12},{20,16},{24,20},{28,24},{32,28},{36,32}... | collective-permute-start | bytes 24584 | tf_op jit(solution)/shard_map/ppermute | solution.py:25
  178.9 2.6 collective-permute-start.2
  180.2 5.6 %collective-permute-start.3 = (f32[2,4,6,1]{3,1,2,0:T(4,128)S(1)}, f32[2,4,6,1]{3,1,2,0:T(4,128)S(1)}, u32[]{:S(2)}, u32[]{:S(2)}) collective-permute-start(f32[2,4,6,1]{3,1,2,0:T(4,128)S(1)} %get-tuple-element.749), channel_id=1, source_target_pairs={{1,0},{2,1},{3,2},{5,4},{6,5},{7,6},{9,8},{10,9},{11,10},{13,12},{... | collective-permute-start | bytes 584 | tf_op jit(solution)/shard_map/ppermute | solution.py:25
  186.1 11.0 %collective-permute-start.4 = (f32[2,4,1,256]{3,1,2,0:T(4,128)S(1)}, f32[2,4,1,256]{3,1,2,0:T(4,128)S(1)}, u32[]{:S(2)}, u32[]{:S(2)}) collective-permute-start(f32[2,4,1,256]{3,1,2,0:T(4,128)S(1)} %get-tuple-element.759), channel_id=1, source_target_pairs={{0,4},{4,8},{8,12},{12,16},{16,20},{20,24},{24,28},{28,32},{32,36}... | collective-permute-start | bytes 24584 | tf_op jit(solution)/shard_map/ppermute | solution.py:22
  188.0 10.4 %collective-permute-start.5 = (f32[2,4,1,256]{3,1,2,0:T(4,128)S(1)}, f32[2,4,1,256]{3,1,2,0:T(4,128)S(1)}, u32[]{:S(2)}, u32[]{:S(2)}) collective-permute-start(f32[2,4,1,256]{3,1,2,0:T(4,128)S(1)} %get-tuple-element.760), channel_id=1, source_target_pairs={{4,0},{8,4},{12,8},{16,12},{20,16},{24,20},{28,24},{32,28},{36,32}... | collective-permute-start | bytes 24584 | tf_op jit(solution)/shard_map/ppermute | solution.py:25
  198.5 6.4 %collective-permute-start.6 = (f32[2,4,6,1]{3,1,2,0:T(4,128)S(1)}, f32[2,4,6,1]{3,1,2,0:T(4,128)S(1)}, u32[]{:S(2)}, u32[]{:S(2)}) collective-permute-start(f32[2,4,6,1]{3,1,2,0:T(4,128)S(1)} %get-tuple-element.748), channel_id=1, source_target_pairs={{0,1},{1,2},{2,3},{4,5},{5,6},{6,7},{8,9},{9,10},{10,11},{12,13},{... | collective-permute-start | bytes 584 | tf_op jit(solution)/shard_map/ppermute | solution.py:22
  203.6 3.1 collective-permute-start.7
  206.9 10.7 %collective-permute-start.8 = (f32[2,4,1,256]{3,1,2,0:T(4,128)S(1)}, f32[2,4,1,256]{3,1,2,0:T(4,128)S(1)}, u32[]{:S(2)}, u32[]{:S(2)}) collective-permute-start(f32[2,4,1,256]{3,1,2,0:T(4,128)S(1)} %get-tuple-element.757), channel_id=1, source_target_pairs={{0,4},{4,8},{8,12},{12,16},{16,20},{20,24},{24,28},{28,32},{32,36}... | collective-permute-start | bytes 24584 | tf_op jit(solution)/shard_map/ppermute | solution.py:22
  208.8 10.1 %collective-permute-start.9 = (f32[2,4,1,256]{3,1,2,0:T(4,128)S(1)}, f32[2,4,1,256]{3,1,2,0:T(4,128)S(1)}, u32[]{:S(2)}, u32[]{:S(2)}) collective-permute-start(f32[2,4,1,256]{3,1,2,0:T(4,128)S(1)} %get-tuple-element.758), channel_id=1, source_target_pairs={{4,0},{8,4},{12,8},{16,12},{20,16},{24,20},{28,24},{32,28},{36,32}... | collective-permute-start | bytes 24584 | tf_op jit(solution)/shard_map/ppermute | solution.py:25
  219.1 6.4 %collective-permute-start.10 = (f32[2,4,6,1]{3,1,2,0:T(4,128)S(1)}, f32[2,4,6,1]{3,1,2,0:T(4,128)S(1)}, u32[]{:S(2)}, u32[]{:S(2)}) collective-permute-start(f32[2,4,6,1]{3,1,2,0:T(4,128)S(1)} %get-tuple-element.746), channel_id=1, source_target_pairs={{0,1},{1,2},{2,3},{4,5},{5,6},{6,7},{8,9},{9,10},{10,11},{12,13},{... | collective-permute-start | bytes 584 | tf_op jit(solution)/shard_map/ppermute | solution.py:22
  224.2 3.1 collective-permute-start.11
  227.6 27.3 %copy-start.11 = (f32[2,4,4,256]{3,1,2,0:T(4,128)}, f32[2,4,4,256]{3,1,2,0:T(4,128)S(1)}, u32[]{:S(2)}) copy-start(f32[2,4,4,256]{3,1,2,0:T(4,128)S(1)} %fusion.127) | copy-start | bytes 98308
  229.4 23.5 %all-to-all-start.2 = ((f32[64,2,4,256]{3,2,1,0:T(4,128)}), f32[64,2,4,256]{3,2,1,0:T(4,128)S(1)}, u32[]{:S(2)}, u32[]{:S(2)}) async-start(f32[64,2,4,256]{3,2,1,0:T(4,128)} %copy.70), calls=%async_computation.2 | async-start | bytes 1048576 | tf_op jit(solution)/shard_map/all_to_all | solution.py:210
  255.2 1.6 copy-start.6
  255.5 0.7 copy-start.7
  256.8 16.6 %copy-start.4 = (f32[128,256]{1,0:T(8,128)}, f32[128,256]{1,0:T(8,128)S(1)}, u32[]{:S(2)}) copy-start(f32[128,256]{1,0:T(8,128)S(1)} %get-tuple-element.1121) | copy-start | bytes 393220 | tf_op jit(solution)/shard_map/while
  273.4 0.6 copy-start.1
  278.9 2.7 copy-start.5
  281.6 16.6 %copy-start.4 = (f32[128,256]{1,0:T(8,128)}, f32[128,256]{1,0:T(8,128)S(1)}, u32[]{:S(2)}) copy-start(f32[128,256]{1,0:T(8,128)S(1)} %get-tuple-element.1121) | copy-start | bytes 393220 | tf_op jit(solution)/shard_map/while
  298.2 0.6 copy-start.1
  303.8 3.7 copy-start.5
  307.5 16.6 %copy-start.4 = (f32[128,256]{1,0:T(8,128)}, f32[128,256]{1,0:T(8,128)S(1)}, u32[]{:S(2)}) copy-start(f32[128,256]{1,0:T(8,128)S(1)} %get-tuple-element.1121) | copy-start | bytes 393220 | tf_op jit(solution)/shard_map/while
  324.1 0.6 copy-start.1
  329.7 3.7 copy-start.5
  333.4 16.6 %copy-start.4 = (f32[128,256]{1,0:T(8,128)}, f32[128,256]{1,0:T(8,128)S(1)}, u32[]{:S(2)}) copy-start(f32[128,256]{1,0:T(8,128)S(1)} %get-tuple-element.1121) | copy-start | bytes 393220 | tf_op jit(solution)/shard_map/while
  350.0 0.6 copy-start.1
  355.6 3.7 copy-start.5
  360.8 27.0 %copy-start.12 = (f32[2,4,4,256]{3,1,2,0:T(4,128)S(1)}, f32[2,4,4,256]{3,1,2,0:T(4,128)}, u32[]{:S(2)}) copy-start(f32[2,4,4,256]{3,1,2,0:T(4,128)} %copy-done.11) | copy-start | bytes 98308
  360.8 27.0 %copy-start.16 = (f32[64,1,2,4]{0,3,2,1:T(4,128)S(1)}, f32[64,1,2,4]{0,3,2,1:T(4,128)}, u32[]{:S(2)}) copy-start(f32[64,1,2,4]{0,3,2,1:T(4,128)} %get-tuple-element.770) | copy-start | bytes 6148
  388.3 10.1 %collective-permute-start.12 = (f32[2,4,1,256]{3,1,2,0:T(4,128)S(1)}, f32[2,4,1,256]{3,1,2,0:T(4,128)S(1)}, u32[]{:S(2)}, u32[]{:S(2)}) collective-permute-start(f32[2,4,1,256]{3,1,2,0:T(4,128)S(1)} %get-tuple-element.755), channel_id=1, source_target_pairs={{0,4},{4,8},{8,12},{12,16},{16,20},{20,24},{24,28},{28,32},{32,36}... | collective-permute-start | bytes 24584 | tf_op jit(solution)/shard_map/ppermute | solution.py:22
  390.6 9.1 %collective-permute-start.13 = (f32[2,4,1,256]{3,1,2,0:T(4,128)S(1)}, f32[2,4,1,256]{3,1,2,0:T(4,128)S(1)}, u32[]{:S(2)}, u32[]{:S(2)}) collective-permute-start(f32[2,4,1,256]{3,1,2,0:T(4,128)S(1)} %get-tuple-element.756), channel_id=1, source_target_pairs={{4,0},{8,4},{12,8},{16,12},{20,16},{24,20},{28,24},{32,28},{36,32}... | collective-permute-start | bytes 24584 | tf_op jit(solution)/shard_map/ppermute | solution.py:25
  399.8 3.4 collective-permute-start.14
  401.9 3.1 collective-permute-start.15
  405.3 10.3 %collective-permute-start.16 = (f32[2,4,1,256]{3,1,2,0:T(4,128)S(1)}, f32[2,4,1,256]{3,1,2,0:T(4,128)S(1)}, u32[]{:S(2)}, u32[]{:S(2)}) collective-permute-start(f32[2,4,1,256]{3,1,2,0:T(4,128)S(1)} %get-tuple-element.753), channel_id=1, source_target_pairs={{0,4},{4,8},{8,12},{12,16},{16,20},{20,24},{24,28},{28,32},{32,36}... | collective-permute-start | bytes 24584 | tf_op jit(solution)/shard_map/ppermute | solution.py:22
  407.2 9.7 %collective-permute-start.17 = (f32[2,4,1,256]{3,1,2,0:T(4,128)S(1)}, f32[2,4,1,256]{3,1,2,0:T(4,128)S(1)}, u32[]{:S(2)}, u32[]{:S(2)}) collective-permute-start(f32[2,4,1,256]{3,1,2,0:T(4,128)S(1)} %get-tuple-element.754), channel_id=1, source_target_pairs={{4,0},{8,4},{12,8},{16,12},{20,16},{24,20},{28,24},{32,28},{36,32}... | collective-permute-start | bytes 24584 | tf_op jit(solution)/shard_map/ppermute | solution.py:25
  417.0 5.9 %collective-permute-start.18 = (f32[2,4,6,1]{3,1,2,0:T(4,128)S(1)}, f32[2,4,6,1]{3,1,2,0:T(4,128)S(1)}, u32[]{:S(2)}, u32[]{:S(2)}) collective-permute-start(f32[2,4,6,1]{3,1,2,0:T(4,128)S(1)} %get-tuple-element.742), channel_id=1, source_target_pairs={{0,1},{1,2},{2,3},{4,5},{5,6},{6,7},{8,9},{9,10},{10,11},{12,13},{... | collective-permute-start | bytes 584 | tf_op jit(solution)/shard_map/ppermute | solution.py:22
  421.7 3.2 collective-permute-start.19
  425.1 11.0 %collective-permute-start.20 = (f32[2,4,1,256]{3,1,2,0:T(4,128)S(1)}, f32[2,4,1,256]{3,1,2,0:T(4,128)S(1)}, u32[]{:S(2)}, u32[]{:S(2)}) collective-permute-start(f32[2,4,1,256]{3,1,2,0:T(4,128)S(1)} %get-tuple-element.751), channel_id=1, source_target_pairs={{0,4},{4,8},{8,12},{12,16},{16,20},{20,24},{24,28},{28,32},{32,36}... | collective-permute-start | bytes 24584 | tf_op jit(solution)/shard_map/ppermute | solution.py:22
  427.1 10.4 %collective-permute-start.21 = (f32[2,4,1,256]{3,1,2,0:T(4,128)S(1)}, f32[2,4,1,256]{3,1,2,0:T(4,128)S(1)}, u32[]{:S(2)}, u32[]{:S(2)}) collective-permute-start(f32[2,4,1,256]{3,1,2,0:T(4,128)S(1)} %get-tuple-element.752), channel_id=1, source_target_pairs={{4,0},{8,4},{12,8},{16,12},{20,16},{24,20},{28,24},{32,28},{36,32}... | collective-permute-start | bytes 24584 | tf_op jit(solution)/shard_map/ppermute | solution.py:25
  437.5 6.4 %collective-permute-start.22 = (f32[2,4,6,1]{3,1,2,0:T(4,128)S(1)}, f32[2,4,6,1]{3,1,2,0:T(4,128)S(1)}, u32[]{:S(2)}, u32[]{:S(2)}) collective-permute-start(f32[2,4,6,1]{3,1,2,0:T(4,128)S(1)} %get-tuple-element.740), channel_id=1, source_target_pairs={{0,1},{1,2},{2,3},{4,5},{5,6},{6,7},{8,9},{9,10},{10,11},{12,13},{... | collective-permute-start | bytes 584 | tf_op jit(solution)/shard_map/ppermute | solution.py:22
  442.6 3.1 collective-permute-start.23
where the time goes:
time: 454 us; the launch traced here: 447 us
  local copies, waits for them, and re-layouts  147 us (32%)
  starting transfers between devices  116 us (26%)
  matrix products  51.8 us (11%)
  waiting for transfers between devices  48.7 us (11%)
  blocking collectives  47.9 us (11%)
  other arithmetic  32.2 us (7%)
    gather x192, local copies, waits for them, and re-layouts  131 us
    ppermute x12, starting transfers between devices, with_halo(): lax.ppermute(lax.slice_in_dim(block, 0, width, axis=dim), axis, backward)  58.2 us
    all_to_all x2, blocking collectives, shards(): lax.all_to_all(grad_exp[None], 'energy', split_axis=2, concat_axis=0, til...  47.9 us
    ppermute x12, starting transfers between devices, with_halo(): lax.ppermute(lax.slice_in_dim(block, block.shape[dim] - width, None, axis...  35.8 us
    all_to_all x2, waiting for transfers between devices, shards(): lax.all_to_all(strip_mix, 'energy', split_axis=0, concat_axis=2, tiled=True)  27.9 us
    dot_general x8, matrix products, one_group(): jnp.einsum('gctb,gsb->cts', shifted, cols_hot, precision=lax.Precision.HI...  27.7 us
    all_to_all x2, starting transfers between devices, shards(): lax.all_to_all(strip_mix, 'energy', split_axis=0, concat_axis=2, tiled=True)  22.4 us
    ppermute x12, waiting for transfers between devices, with_halo(): lax.ppermute(lax.slice_in_dim(block, 0, width, axis=dim), axis, backward)  20.7 us
  transfers between devices with their start and end apart: 26, of which 14 were waited for; matrix products, arithmetic and copies ran while one was open for 1% of the time, Pallas kernels for 0%

commit v1 on v0

v1 whole, which is shorter than its diff:
```python
import functools
import math

import jax
import jax.numpy as jnp
from jax import lax
from jax.experimental import pallas as pl
from jax.experimental.pallas import tpu as pltpu
from jax.sharding import PartitionSpec as P

ITERS = 2
TV_STEPS = 3
DATA_STEP = 0.05
TV_STEP = 0.05
TV_EPS = 0.01

LEN = 128
GROUP = 8

def dft_tables(length):
    index = jnp.arange(length, dtype=jnp.int32)
    phase = index[:, None] * index[None, :] % length
    angle = phase.astype(jnp.float32) * (-2.0 * math.pi / length)
    scale = 1.0 / math.sqrt(length)
    return (
        (jnp.cos(angle) * scale).astype(jnp.bfloat16),
        (jnp.sin(angle) * scale).astype(jnp.bfloat16),
    )

def dft_blocks(fr, fi):
    ahead = jnp.concatenate([jnp.concatenate([fr, fi], 1), jnp.concatenate([-fi, fr], 1)], 0)
    back = jnp.concatenate([jnp.concatenate([fr, -fi], 1), jnp.concatenate([fi, fr], 1)], 0)
    return ahead, back

def dot(left, right):
    return jnp.dot(left, right, preferred_element_type=jnp.float32)

def pair_up(both):
    one, two = both
    return jnp.concatenate([
        jnp.concatenate([one[:, :LEN], two[:, :LEN]], 1),
        jnp.concatenate([one[:, LEN:], two[:, LEN:]], 1)], 0)

def patch_kernel(group, spots, z_ref, probe_ref, counts_hbm, ahead_ref, back_ref, out_ref, wave, total, counts, sem):
    copy = pltpu.make_async_copy(counts_hbm, counts, sem)
    copy.start()
    patches = counts.shape[0]
    blocks = z_ref.shape[0]
    step = 4
    upper = lax.broadcasted_iota(jnp.int32, (step, 8, LEN), 1) < 4

    def expand(i, carry):
        at = pl.multiple_of(i * step, step)
        rows = pl.ds(pl.multiple_of(i * step * 8, step * 8), step * 8)
        for half in range(2):
            def part(c):
                low = z_ref[pl.ds(at, step), 8 * c + 4 * half : 8 * c + 4 * half + 8, :]
                high = z_ref[pl.ds(at, step), 8 * c + 4 * half + 12 : 8 * c + 4 * half + 20, :]
                return jnp.where(upper, low, high).reshape(step * 8, LEN)
            growth = jnp.exp(part(0))
            angle = part(1)
            wave[half, rows, :] = growth * jnp.cos(angle)
            wave[2 + half, rows, :] = growth * jnp.sin(angle)
            total[half, rows, :] = jnp.zeros((step * 8, LEN), jnp.float32)
            total[2 + half, rows, :] = jnp.zeros((step * 8, LEN), jnp.float32)
        return carry

    lax.fori_loop(0, blocks // step, expand, 0)
    copy.wait()
    lane = lax.broadcasted_iota(jnp.int32, (LEN, LEN), 1)

    def one_group(g, carry):
        first = g * group
        exits = []
        for j in range(group):
            a = spots[first + j, 0]
            b = spots[first + j, 1]
            rows = pl.ds(a, LEN)
            keep = lane >= b
            shift = jnp.bitwise_and(LEN - b, LEN - 1)
            wr = pltpu.roll(jnp.where(keep, wave[0, rows, :], wave[1, rows, :]), shift, 1)
            wi = pltpu.roll(jnp.where(keep, wave[2, rows, :], wave[3, rows, :]), shift, 1)
            pr = probe_ref[:, :LEN]
            pi = probe_ref[:, LEN:]
            exits.append(jnp.concatenate([pr * wr - pi * wi, pr * wi + pi * wr], 1).astype(jnp.bfloat16))
        first_pass = dot(jnp.concatenate(exits, 0), ahead_ref[...]).astype(jnp.bfloat16)
        weighted = []
        for j in range(0, group, 2):
            far = dot(back_ref[...], pair_up([first_pass[k * LEN : (k + 1) * LEN] for k in (j, j + 1)]))
            for k in range(2):
                fr = far[:LEN, k * LEN : (k + 1) * LEN]
                fi = far[LEN:, k * LEN : (k + 1) * LEN]
                misfit = fr * fr + fi * fi - counts[first + j + k]
                weighted.append(jnp.concatenate([misfit * fr, misfit * fi], 1).astype(jnp.bfloat16))
        third_pass = dot(jnp.concatenate(weighted, 0), back_ref[...]).astype(jnp.bfloat16)
        for j in range(0, group, 2):
            grad = dot(ahead_ref[...], pair_up([third_pass[k * LEN : (k + 1) * LEN] for k in (j, j + 1)]))
            for k in range(2):
                a = spots[first + j + k, 0]
                b = spots[first + j + k, 1]
                rows = pl.ds(a, LEN)
                keep = lane >= jnp.bitwise_and(b, LEN - 1)
                wrap = b == LEN
                gr = grad[:LEN, k * LEN : (k + 1) * LEN]
                gi = grad[LEN:, k * LEN : (k + 1) * LEN]
                pr = probe_ref[:, :LEN]
                pi = probe_ref[:, LEN:]
                keep = lane >= b
                shift = jnp.bitwise_and(b, LEN - 1)
                ur = pltpu.roll(pr * gr + pi * gi, shift, 1)
                ui = pltpu.roll(pr * gi - pi * gr, shift, 1)
                total[0, rows, :] += jnp.where(keep, ur, 0.0)
                total[1, rows, :] += jnp.where(keep, 0.0, ur)
                total[2, rows, :] += jnp.where(keep, ui, 0.0)
                total[3, rows, :] += jnp.where(keep, 0.0, ui)
        return carry

    lax.fori_loop(0, patches // group, one_group, 0)

    def finish(i, carry):
        at = pl.multiple_of(i * step, step)
        rows = pl.ds(pl.multiple_of(i * step * 8, step * 8), step * 8)
        for half in range(2):
            orr = wave[half, rows, :]
            oi = wave[2 + half, rows, :]
            tr = total[half, rows, :]
            ti = total[2 + half, rows, :]
            for c, value in ((0, orr * tr + oi * ti), (1, orr * ti - oi * tr)):
                value = value.reshape(step, 8, LEN)
                lo = 8 * c + 4 * half
                out_ref[pl.ds(at, step), lo : lo + 4, :] = value[:, :4]
                out_ref[pl.ds(at, step), lo + 16 : lo + 20, :] = value[:, 4:]
        return carry

    lax.fori_loop(0, blocks // step, finish, 0)


def patch_gradient(z, probe, spots, counts, tables, group=GROUP):
    strips = z.shape[0]
    vmem = pl.BlockSpec(memory_space=pltpu.VMEM)
    out = pl.pallas_call(
        functools.partial(patch_kernel, group),
        out_shape=jax.ShapeDtypeStruct((strips // 2, 32, LEN), jnp.float32),
        in_specs=[pl.BlockSpec(memory_space=pltpu.SMEM), vmem, vmem, pl.BlockSpec(memory_space=pl.ANY), vmem, vmem],
        out_specs=vmem,
        scratch_shapes=[
            pltpu.VMEM((4, 4 * strips, LEN), jnp.float32),
            pltpu.VMEM((4, 4 * strips, LEN), jnp.float32),
            pltpu.VMEM(counts.shape, jnp.float32),
            pltpu.SemaphoreType.DMA,
        ],
    )(spots, z.reshape(strips // 2, 32, LEN), probe, counts, *tables)
    return out.reshape(z.shape)


def mixed(planes, spectra, out_ref):
    materials = len(planes) // 2

    def one(e, carry):
        re = jnp.zeros_like(planes[0])
        im = jnp.zeros_like(planes[0])
        for m in range(materials):
            cr = spectra[e, 2 * m]
            ci = spectra[e, 2 * m + 1]
            re = re + cr * planes[m] - ci * planes[materials + m]
            im = im + cr * planes[materials + m] + ci * planes[m]
        out_ref[e, 0:8, :] = re
        out_ref[e, 8:16, :] = im
        return carry

    lax.fori_loop(0, out_ref.shape[0], one, 0, unroll=8)


def mix_kernel(spectra, maps_ref, out_ref, rows_ref):
    for half in range(2):
        rows_ref[:, 4 * half : 4 * half + 4, :] = maps_ref[:, :, half * LEN : (half + 1) * LEN]
    mixed([rows_ref[p] for p in range(rows_ref.shape[0])], spectra, out_ref)


def unmix_kernel(factor, spectra, grads_ref, rows_ref, out_ref):
    materials = rows_ref.shape[0] // 2

    def one(e, sums):
        gr = grads_ref[e, 0:8, :]
        gi = grads_ref[e, 8:16, :]
        reals, imags = [], []
        for m in range(materials):
            cr = spectra[e, 2 * m]
            ci = spectra[e, 2 * m + 1]
            reals.append(sums[m] + cr * gr + ci * gi)
            imags.append(sums[materials + m] + cr * gi - ci * gr)
        return tuple(reals + imags)

    zero = jnp.zeros(rows_ref.shape[1:], jnp.float32)
    sums = lax.fori_loop(0, grads_ref.shape[0], one, (zero,) * (2 * materials), unroll=8)
    for p in range(2 * materials):
        out_ref[p] = rows_ref[p] - factor * sums[p]


def smooth(place, last, mine_ref, before_ref, after_ref, field):
    planes = mine_ref.shape[0]
    for j in range(3):
        lanes = slice(j * LEN, (j + 1) * LEN)
        field[:, 0:4, lanes] = before_ref[:, 4 * j : 4 * j + 4, :]
        field[:, 4:8, lanes] = mine_ref[:, 4 * j : 4 * j + 4, :]
        field[:, 8:12, lanes] = after_ref[:, 4 * j : 4 * j + 4, :]
        field[:, 12:16, lanes] = jnp.zeros((planes, 4, LEN), jnp.float32)
    shape = (16, 3 * LEN)
    row = lax.broadcasted_iota(jnp.int32, shape, 0)
    lane = lax.broadcasted_iota(jnp.int32, shape, 1)
    low_row = jnp.where(place[0] == 0, 4, 0)
    high_row = jnp.where(place[0] == last[0], 8, 16)
    low_edge = jnp.where(place[1] == last[1], 2 * LEN + LEN // 2, 0)
    high_edge = jnp.where(place[1] == 0, 2 * LEN + LEN // 2, 3 * LEN)
    inside = (row >= low_row) & (row < high_row)
    inside = inside & ((lane < 2 * LEN) | ((lane >= low_edge) & (lane < high_edge)))
    results = [None] * planes
    for m in range(planes // 2):
        pair = [field[m], field[planes // 2 + m]]
        for _ in range(TV_STEPS):
            down = [pltpu.roll(x, 15, 0) - x for x in pair]
            across = [pltpu.roll(x, 3 * LEN - 1, 1) - x for x in pair]
            square = down[0] * down[0] + across[0] * across[0] + down[1] * down[1] + across[1] * across[1]
            scale = lax.rsqrt(square + TV_EPS)
            fresh = []
            for x, d, c in zip(pair, down, across):
                d = d * scale
                c = c * scale
                moved = x + TV_STEP * (d - pltpu.roll(d, 1, 0) + c - pltpu.roll(c, 1, 1))
                fresh.append(jnp.where(inside, moved, 0.0))
            pair = fresh
        results[m], results[planes // 2 + m] = pair
    return results


def smooth_mix_kernel(last, place, spectra, mine_ref, before_ref, after_ref, rows_ref, out_ref, field):
    results = smooth(place, last, mine_ref, before_ref, after_ref, field)
    for p, value in enumerate(results):
        rows_ref[p, 0:4, :] = value[4:8, :LEN]
        rows_ref[p, 4:8, :] = value[4:8, LEN : 2 * LEN]
    mixed([rows_ref[p] for p in range(rows_ref.shape[0])], spectra, out_ref)


def smooth_kernel(last, place, mine_ref, before_ref, after_ref, out_ref, field):
    results = smooth(place, last, mine_ref, before_ref, after_ref, field)
    for p, value in enumerate(results):
        out_ref[p] = value[4:8, : 2 * LEN]


def on_chip(kernel, out_shape, scalars, arrays, scratch=()):
    vmem = pl.BlockSpec(memory_space=pltpu.VMEM)
    smem = pl.BlockSpec(memory_space=pltpu.SMEM)
    return pl.pallas_call(
        kernel,
        out_shape=out_shape,
        in_specs=[smem] * len(scalars) + [vmem] * len(arrays),
        out_specs=jax.tree.map(lambda _: vmem, out_shape),
        scratch_shapes=list(scratch),
    )(*scalars, *arrays)


def with_edges(rows):
    count = lax.axis_size("tile")
    right = [(i, i + 1) for i in range(count - 1)]
    left = [(b, a) for a, b in right]
    from_left = lax.ppermute(rows[:, 4:8], "tile", right)
    from_right = lax.ppermute(rows[:, 0:4], "tile", left)
    lane = lax.broadcasted_iota(jnp.int32, from_left.shape, 2)
    return jnp.concatenate([rows, jnp.where(lane < LEN // 2, from_right, from_left)], 1)


def from_neighbours(strip):
    count = lax.axis_size("energy")
    ahead = [(i, i + 1) for i in range(count - 1)]
    back = [(b, a) for a, b in ahead]
    return lax.ppermute(strip, "energy", ahead), lax.ppermute(strip, "energy", back)


def shards(material_maps, spectra, probes, offsets, measured):
    energies, materials, _ = spectra.shape
    planes = 2 * materials
    rows, columns = material_maps.shape[2:]
    assert rows == 4 and columns == 2 * LEN
    probe = probes[0]
    spots = offsets[0]
    counts = measured[0, 0]
    tables = dft_blocks(*dft_tables(LEN))
    weights = spectra.reshape(energies, 2 * materials)
    factor = DATA_STEP / math.sqrt(energies)
    place = jnp.stack([lax.axis_index("energy"), lax.axis_index("tile")]).astype(jnp.int32)
    last = (lax.axis_size("energy") - 1, lax.axis_size("tile") - 1)
    strip = jax.ShapeDtypeStruct((planes, 2 * rows, LEN), jnp.float32)
    spread = jax.ShapeDtypeStruct((energies, 4 * rows, LEN), jnp.float32)
    field = pltpu.VMEM((planes, 16, 3 * LEN), jnp.float32)
    maps = material_maps.reshape(planes, rows, columns)
    current = maps.reshape(planes, rows, 2, LEN).transpose(0, 2, 1, 3).reshape(planes, 2 * rows, LEN)
    mixes = on_chip(mix_kernel, spread, (weights,), (maps,), [pltpu.VMEM((planes, 2 * rows, LEN), jnp.float32)])
    for repeat in range(ITERS):
        tile = lax.all_to_all(mixes, "energy", split_axis=0, concat_axis=0, tiled=True)
        grads = patch_gradient(tile, probe, spots, counts, tables)
        grads = lax.all_to_all(grads, "energy", split_axis=0, concat_axis=0, tiled=True)
        current = on_chip(functools.partial(unmix_kernel, factor), strip, (weights,), (grads, current))
        mine = with_edges(current)
        before, after = from_neighbours(mine)
        if repeat < ITERS - 1:
            current, mixes = on_chip(
                functools.partial(smooth_mix_kernel, last), (strip, spread), (place, weights), (mine, before, after), [field]
            )
    result = jax.ShapeDtypeStruct((planes, rows, columns), jnp.float32)
    out = on_chip(functools.partial(smooth_kernel, last), result, (place,), (mine, before, after), [field])
    return out.reshape(material_maps.shape)


def solution(mesh):
    in_specs = (
        P(None, None, "energy", "tile"),
        P(),
        P("energy", None, None),
        P("tile", None, None),
        P("energy", "tile", None, None, None),
    )
    out_specs = P(None, None, "energy", "tile")
    return jax.shard_map(shards, mesh=mesh, in_specs=in_specs, out_specs=out_specs, check_vma=False)
```

time: 454 us -> 182 us (0.40)
  local copies, waits for them, and re-layouts: 147 us -> 6.47 us
  starting transfers between devices: 116 us -> 34.1 us
  matrix products: 51.8 us -> 0 us
  Pallas kernels: 0 us -> 29.6 us
  other arithmetic: 32.2 us -> 3.48 us
  blocking collectives: 47.9 us -> 69.4 us
  waiting for transfers between devices: 48.7 us -> 35.9 us
    gather x192 -> x0, local copies, waits for them, and re-layouts: 131 us -> none
    ppermute x24 -> x8, starting transfers between devices: 94 us -> 21.1 us  [the longest x2 12.1 us: from_neighbours(): lax.ppermute(strip, 'energy', back)]
    dot_general x36 -> x0, matrix products: 51.8 us -> none  [the longest x8 27.7 us: one_group(): jnp.einsum('gctb,gsb->cts', shifted, cols_hot, precision=lax.Precision.HI...]
    pallas_call x0 -> x7, Pallas kernels: none -> 29.6 us  [the longest x2 17.4 us: patch_gradient(): pl.pallas_call(functools.partial(patch_kernel, group), out_shape=jax.Shap...]
    all_to_all x2 -> x3, blocking collectives: 47.9 us -> 69.4 us  [the longest x2 49 us: shards(): lax.all_to_all(grads, 'energy', split_axis=0, concat_axis=0, tiled=True)]
    another operation x27 -> x1, other arithmetic: 20.8 us -> 0.65 us  [shards(): jnp.stack([lax.axis_index('energy'), lax.axis_index('tile')])]
    all_to_all x2 -> x1, waiting for transfers between devices: 27.9 us -> 13.6 us  [shards(): lax.all_to_all(mixes, 'energy', split_axis=0, concat_axis=0, tiled=True)]
    all_to_all x2 -> x1, starting transfers between devices: 22.4 us -> 13 us  [shards(): lax.all_to_all(mixes, 'energy', split_axis=0, concat_axis=0, tiled=True)]
  transfers between devices with their start and end apart: 26 -> 9, of which waited for: 14 -> 5; matrix products, arithmetic and copies ran while one was open for 1% -> 2% of each run, Pallas kernels for 0% -> 0%
where the time goes in v1:
time: 182 us; the launch traced here: 179 us
  blocking collectives  69.4 us (38%)
  waiting for transfers between devices  35.9 us (20%)
  starting transfers between devices  34.1 us (19%)
  Pallas kernels  29.6 us (16%)
  local copies, waits for them, and re-layouts  6.47 us (4%)
  other arithmetic  3.48 us (2%)
    all_to_all x2, blocking collectives, shards(): lax.all_to_all(grads, 'energy', split_axis=0, concat_axis=0, tiled=True)  49 us
    all_to_all x1, blocking collectives, shards(): lax.all_to_all(mixes, 'energy', split_axis=0, concat_axis=0, tiled=True)  20.4 us
    pallas_call x2, Pallas kernels, patch_gradient(): pl.pallas_call(functools.partial(patch_kernel, group), out_shape=jax.Shap...  17.4 us
    ppermute x2, waiting for transfers between devices, from_neighbours(): lax.ppermute(strip, 'energy', ahead)  16.2 us
    all_to_all x1, waiting for transfers between devices, shards(): lax.all_to_all(mixes, 'energy', split_axis=0, concat_axis=0, tiled=True)  13.6 us
    all_to_all x1, starting transfers between devices, shards(): lax.all_to_all(mixes, 'energy', split_axis=0, concat_axis=0, tiled=True)  13 us
    pallas_call x5, Pallas kernels, on_chip(): pl.pallas_call(kernel, out_shape=out_shape, in_specs=[smem] * len(scalars...  12.2 us
    ppermute x2, starting transfers between devices, from_neighbours(): lax.ppermute(strip, 'energy', back)  12.1 us
  transfers between devices with their start and end apart: 9, of which 5 were waited for; matrix products, arithmetic and copies ran while one was open for 2% of the time, Pallas kernels for 0%

profile of v1, /device:TPU:8, one launch (start us, length us, event | category | flops | bytes accessed | tf_op | source)
XLA Modules:
  0.0 179.1 jit_solution(5789869894104488244)
XLA Ops:
  0.0 1.4 copy.16.spectra
  1.4 2.4 %shard_map.55 = f32[64,16,128]{2,1,0:T(8,128)} custom-call(f32[64,8]{1,0:T(8,128)} %copy.16.spectra, f32[8,4,256]{2,1,0:T(4,128)} %bitcast.25), custom_call_target="tpu_custom_call" | custom-call | tf_op jit(solution)/shard_map/pallas_call | solution.py:253
  3.8 13.0 %all-to-all-start = ((f32[64,16,128]{2,1,0:T(8,128)}), f32[64,16,128]{2,1,0:T(8,128)S(1)}, u32[]{:S(2)}, u32[]{:S(2)}) async-start(f32[64,16,128]{2,1,0:T(8,128)} %shard_map.55), calls=%async_computation | async-start | bytes 1048576 | tf_op jit(solution)/shard_map/all_to_all | solution.py:299
  16.8 1.4 copy.15.spots
  18.2 0.3 fusion.8
  18.5 0.3 multiply_convert_fusion
  18.8 0.7 fusion.1
  19.5 13.6 %all-to-all-done = f32[64,16,128]{2,1,0:T(8,128)S(1)} async-done(((f32[64,16,128]{2,1,0:T(8,128)}), f32[64,16,128]{2,1,0:T(8,128)S(1)}, u32[]{:S(2)}, u32[]{:S(2)}) %all-to-all-start) | async-done | bytes 524320 | tf_op jit(solution)/shard_map/all_to_all | solution.py:299
  33.1 0.0 copy-start
  33.1 0.8 copy-done
  33.9 8.7 %shard_map.56 = f32[32,32,128]{2,1,0:T(8,128)} custom-call(s32[32,2]{1,0:T(8,128)} %copy.15.spots, f32[32,32,128]{2,1,0:T(8,128)} %bitcast.19, f32[128,256]{1,0:T(8,128)} %bitcast.23, f32[32,128,128]{2,1,0:T(8,128)} %bitcast.17, bf16[256,256]{1,0:T(8,128)(2,1)} %get-tuple-element.10.ahead_ref, bf16[256,256]{1,0:T(8,128)(2,1)} %get-tuple-element.9.back_ref), custom_call_target="tpu_custom_call" | custom-call | tf_op jit(solution)/shard_map/pallas_call | solution.py:141
  42.6 23.3 %all_to_all.20.grads_ref = f32[64,16,128]{2,1,0:T(8,128)} all-to-all(f32[64,16,128]{2,1,0:T(8,128)} %bitcast.22), channel_id=1, replica_groups=mesh['energy'=64,'tile'=4] {'energy'}, dimensions={0} | all-to-all | bytes 1048576 | tf_op jit(solution)/shard_map/all_to_all | solution.py:301
  65.9 2.2 %shard_map.57 = f32[8,8,128]{2,1,0:T(8,128)} custom-call(f32[64,8]{1,0:T(8,128)} %copy.16.spectra, f32[64,16,128]{2,1,0:T(8,128)} %all_to_all.20.grads_ref, f32[8,8,128]{2,1,0:T(8,128)} %bitcast.26), custom_call_target="tpu_custom_call" | custom-call | tf_op jit(solution)/shard_map/pallas_call | solution.py:253
  68.1 0.8 fusion.10
  69.0 1.3 collective-permute-start.1
  70.3 1.3 collective-permute-start
  71.6 0.0 collective-permute-done.1
  71.6 4.3 %collective-permute-done = f32[8,4,128]{2,1,0:T(4,128)S(1)} collective-permute-done((f32[8,4,128]{2,1,0:T(4,128)S(1)}, f32[8,4,128]{2,1,0:T(4,128)S(1)}, u32[]{:S(2)}, u32[]{:S(2)}) %collective-permute-start) | collective-permute-done | bytes 16416 | tf_op jit(solution)/shard_map/ppermute | solution.py:267
  75.9 0.8 pad_maximum_fusion.4.mine_ref
  76.7 0.0 copy-start.1
  76.7 6.3 %collective-permute-start.3 = (f32[8,12,128]{2,1,0:T(8,128)S(1)}, f32[8,12,128]{2,1,0:T(8,128)S(1)}, u32[]{:S(2)}, u32[]{:S(2)}) collective-permute-start(f32[8,12,128]{2,1,0:T(8,128)S(1)} %pad_maximum_fusion.4.mine_ref), channel_id=1, source_target_pairs={{4,0},{8,4},{12,8},{16,12},{20,16},{24,20},{28,24},{32,28},{36,32}... | collective-permute-start | bytes 147464 | tf_op jit(solution)/shard_map/ppermute | solution.py:276
  82.9 1.9 %collective-permute-start.2 = (f32[8,12,128]{2,1,0:T(8,128)S(1)}, f32[8,12,128]{2,1,0:T(8,128)S(1)}, u32[]{:S(2)}, u32[]{:S(2)}) collective-permute-start(f32[8,12,128]{2,1,0:T(8,128)S(1)} %pad_maximum_fusion.4.mine_ref), channel_id=1, source_target_pairs={{0,4},{4,8},{8,12},{12,16},{16,20},{20,24},{24,28},{28,32},{32,36}... | collective-permute-start | bytes 147464 | tf_op jit(solution)/shard_map/ppermute | solution.py:276
  84.8 0.7 pad_add_fusion.place
  85.5 0.0 collective-permute-done.3.after_ref
  85.5 0.0 copy-start.3
  85.5 7.8 %collective-permute-done.2.before_ref = f32[8,12,128]{2,1,0:T(8,128)S(1)} collective-permute-done((f32[8,12,128]{2,1,0:T(8,128)S(1)}, f32[8,12,128]{2,1,0:T(8,128)S(1)}, u32[]{:S(2)}, u32[]{:S(2)}) %collective-permute-start.2) | collective-permute-done | bytes 49184 | tf_op jit(solution)/shard_map/ppermute | solution.py:276
  93.3 0.0 copy-done.1
  93.3 0.0 copy-done.3
  93.3 0.0 copy-start.4
  93.3 0.6 copy-done.4
  93.9 3.2 %shard_map.58 = (f32[8,8,128]{2,1,0:T(8,128)}, f32[64,16,128]{2,1,0:T(8,128)}) custom-call(s32[2]{0:T(128)} %pad_add_fusion.place, f32[64,8]{1,0:T(8,128)} %copy.16.spectra, f32[8,12,128]{2,1,0:T(8,128)} %copy-done.1, f32[8,12,128]{2,1,0:T(8,128)} %copy-done.4, f32[8,12,128]{2,1,0:T(8,128)} %copy-done.3), custom_call_target="tpu_custom_call" | custom-call | tf_op jit(solution)/shard_map/pallas_call | solution.py:253
  97.1 20.4 %all_to_all.21 = f32[64,16,128]{2,1,0:T(8,128)} all-to-all(f32[64,16,128]{2,1,0:T(8,128)} %get-tuple-element.7), channel_id=1, replica_groups=mesh['energy'=64,'tile'=4] {'energy'}, dimensions={0} | all-to-all | bytes 1048576 | tf_op jit(solution)/shard_map/all_to_all | solution.py:299
  117.5 8.7 %shard_map.59 = f32[32,32,128]{2,1,0:T(8,128)} custom-call(s32[32,2]{1,0:T(8,128)} %copy.15.spots, f32[32,32,128]{2,1,0:T(8,128)} %bitcast.20, f32[128,256]{1,0:T(8,128)} %bitcast.24, f32[32,128,128]{2,1,0:T(8,128)} %bitcast.18, bf16[256,256]{1,0:T(8,128)(2,1)} %get-tuple-element.10.ahead_ref, bf16[256,256]{1,0:T(8,128)(2,1)} %get-tuple-element.9.back_ref), custom_call_target="tpu_custom_call" | custom-call | tf_op jit(solution)/shard_map/pallas_call | solution.py:141
  126.2 25.7 %all_to_all.22.grads_ref = f32[64,16,128]{2,1,0:T(8,128)} all-to-all(f32[64,16,128]{2,1,0:T(8,128)} %bitcast.21), channel_id=1, replica_groups=mesh['energy'=64,'tile'=4] {'energy'}, dimensions={0} | all-to-all | bytes 1048576 | tf_op jit(solution)/shard_map/all_to_all | solution.py:301
  151.9 2.2 %shard_map.60 = f32[8,8,128]{2,1,0:T(8,128)} custom-call(f32[64,8]{1,0:T(8,128)} %copy.16.spectra, f32[64,16,128]{2,1,0:T(8,128)} %all_to_all.22.grads_ref, f32[8,8,128]{2,1,0:T(8,128)} %get-tuple-element.8.rows_ref), custom_call_target="tpu_custom_call" | custom-call | tf_op jit(solution)/shard_map/pallas_call | solution.py:253
  154.1 0.8 fusion.9
  154.9 1.3 collective-permute-start.5
  156.2 1.3 collective-permute-start.4
  157.5 0.0 collective-permute-done.5
  157.5 1.8 collective-permute-done.4
  159.3 0.8 pad_maximum_fusion.5.mine_ref
  160.1 0.0 copy-start.2
  160.1 5.8 %collective-permute-start.7 = (f32[8,12,128]{2,1,0:T(8,128)S(1)}, f32[8,12,128]{2,1,0:T(8,128)S(1)}, u32[]{:S(2)}, u32[]{:S(2)}) collective-permute-start(f32[8,12,128]{2,1,0:T(8,128)S(1)} %pad_maximum_fusion.5.mine_ref), channel_id=1, source_target_pairs={{4,0},{8,4},{12,8},{16,12},{20,16},{24,20},{28,24},{32,28},{36,32}... | collective-permute-start | bytes 147464 | tf_op jit(solution)/shard_map/ppermute | solution.py:276
  165.9 1.9 %collective-permute-start.6 = (f32[8,12,128]{2,1,0:T(8,128)S(1)}, f32[8,12,128]{2,1,0:T(8,128)S(1)}, u32[]{:S(2)}, u32[]{:S(2)}) collective-permute-start(f32[8,12,128]{2,1,0:T(8,128)S(1)} %pad_maximum_fusion.5.mine_ref), channel_id=1, source_target_pairs={{0,4},{4,8},{8,12},{12,16},{16,20},{20,24},{24,28},{28,32},{32,36}... | collective-permute-start | bytes 147464 | tf_op jit(solution)/shard_map/ppermute | solution.py:276
  167.8 0.0 collective-permute-done.7.after_ref
  167.8 0.0 copy-start.5
  167.9 8.4 %collective-permute-done.6.before_ref = f32[8,12,128]{2,1,0:T(8,128)S(1)} collective-permute-done((f32[8,12,128]{2,1,0:T(8,128)S(1)}, f32[8,12,128]{2,1,0:T(8,128)S(1)}, u32[]{:S(2)}, u32[]{:S(2)}) %collective-permute-start.6) | collective-permute-done | bytes 49184 | tf_op jit(solution)/shard_map/ppermute | solution.py:276
  176.3 0.0 copy-done.2
  176.3 0.0 copy-done.5
  176.3 0.0 copy-start.6
  176.3 0.6 copy-done.6
  176.9 2.2 %shard_map.61 = f32[8,4,256]{2,1,0:T(4,128)} custom-call(s32[2]{0:T(128)} %pad_add_fusion.place, f32[8,12,128]{2,1,0:T(8,128)} %copy-done.2, f32[8,12,128]{2,1,0:T(8,128)} %copy-done.6, f32[8,12,128]{2,1,0:T(8,128)} %copy-done.5), custom_call_target="tpu_custom_call" | custom-call | tf_op jit(solution)/shard_map/pallas_call | solution.py:253
  (3 shorter events, 0.0 us)
Async XLA Ops:
  3.8 29.3 %all-to-all-start = ((f32[64,16,128]{2,1,0:T(8,128)}), f32[64,16,128]{2,1,0:T(8,128)S(1)}, u32[]{:S(2)}, u32[]{:S(2)}) async-start(f32[64,16,128]{2,1,0:T(8,128)} %shard_map.55), calls=%async_computation | async-start | bytes 1048576 | tf_op jit(solution)/shard_map/all_to_all | solution.py:299
  33.1 0.8 copy-start
  69.0 2.6 %collective-permute-start.1 = (f32[8,4,128]{2,1,0:T(4,128)S(1)}, f32[8,4,128]{2,1,0:T(4,128)S(1)}, u32[]{:S(2)}, u32[]{:S(2)}) collective-permute-start(f32[8,4,128]{2,1,0:T(4,128)S(1)} %get-tuple-element.13), channel_id=1, source_target_pairs={{0,1},{1,2},{2,3},{4,5},{5,6},{6,7},{8,9},{9,10},{10,11},{12,13},{... | collective-permute-start | bytes 49160 | tf_op jit(solution)/shard_map/ppermute | solution.py:266
  70.3 5.6 %collective-permute-start = (f32[8,4,128]{2,1,0:T(4,128)S(1)}, f32[8,4,128]{2,1,0:T(4,128)S(1)}, u32[]{:S(2)}, u32[]{:S(2)}) collective-permute-start(f32[8,4,128]{2,1,0:T(4,128)S(1)} %get-tuple-element.14), channel_id=1, source_target_pairs={{1,0},{2,1},{3,2},{5,4},{6,5},{7,6},{9,8},{10,9},{11,10},{13,12},{... | collective-permute-start | bytes 49160 | tf_op jit(solution)/shard_map/ppermute | solution.py:267
  76.7 16.6 %copy-start.1 = (f32[8,12,128]{2,1,0:T(8,128)}, f32[8,12,128]{2,1,0:T(8,128)S(1)}, u32[]{:S(2)}) copy-start(f32[8,12,128]{2,1,0:T(8,128)S(1)} %pad_maximum_fusion.4.mine_ref) | copy-start | bytes 147460
  76.7 8.8 %collective-permute-start.3 = (f32[8,12,128]{2,1,0:T(8,128)S(1)}, f32[8,12,128]{2,1,0:T(8,128)S(1)}, u32[]{:S(2)}, u32[]{:S(2)}) collective-permute-start(f32[8,12,128]{2,1,0:T(8,128)S(1)} %pad_maximum_fusion.4.mine_ref), channel_id=1, source_target_pairs={{4,0},{8,4},{12,8},{16,12},{20,16},{24,20},{28,24},{32,28},{36,32}... | collective-permute-start | bytes 147464 | tf_op jit(solution)/shard_map/ppermute | solution.py:276
  82.9 10.4 %collective-permute-start.2 = (f32[8,12,128]{2,1,0:T(8,128)S(1)}, f32[8,12,128]{2,1,0:T(8,128)S(1)}, u32[]{:S(2)}, u32[]{:S(2)}) collective-permute-start(f32[8,12,128]{2,1,0:T(8,128)S(1)} %pad_maximum_fusion.4.mine_ref), channel_id=1, source_target_pairs={{0,4},{4,8},{8,12},{12,16},{16,20},{20,24},{24,28},{28,32},{32,36}... | collective-permute-start | bytes 147464 | tf_op jit(solution)/shard_map/ppermute | solution.py:276
  85.5 7.8 %copy-start.3 = (f32[8,12,128]{2,1,0:T(8,128)}, f32[8,12,128]{2,1,0:T(8,128)S(1)}, u32[]{:S(2)}) copy-start(f32[8,12,128]{2,1,0:T(8,128)S(1)} %collective-permute-done.3.after_ref) | copy-start | bytes 147460
  93.3 0.6 copy-start.4
  154.9 2.6 %collective-permute-start.5 = (f32[8,4,128]{2,1,0:T(4,128)S(1)}, f32[8,4,128]{2,1,0:T(4,128)S(1)}, u32[]{:S(2)}, u32[]{:S(2)}) collective-permute-start(f32[8,4,128]{2,1,0:T(4,128)S(1)} %get-tuple-element.11), channel_id=1, source_target_pairs={{0,1},{1,2},{2,3},{4,5},{5,6},{6,7},{8,9},{9,10},{10,11},{12,13},{... | collective-permute-start | bytes 49160 | tf_op jit(solution)/shard_map/ppermute | solution.py:266
  156.2 3.1 %collective-permute-start.4 = (f32[8,4,128]{2,1,0:T(4,128)S(1)}, f32[8,4,128]{2,1,0:T(4,128)S(1)}, u32[]{:S(2)}, u32[]{:S(2)}) collective-permute-start(f32[8,4,128]{2,1,0:T(4,128)S(1)} %get-tuple-element.12), channel_id=1, source_target_pairs={{1,0},{2,1},{3,2},{5,4},{6,5},{7,6},{9,8},{10,9},{11,10},{13,12},{... | collective-permute-start | bytes 49160 | tf_op jit(solution)/shard_map/ppermute | solution.py:267
  160.1 16.2 %copy-start.2 = (f32[8,12,128]{2,1,0:T(8,128)}, f32[8,12,128]{2,1,0:T(8,128)S(1)}, u32[]{:S(2)}) copy-start(f32[8,12,128]{2,1,0:T(8,128)S(1)} %pad_maximum_fusion.5.mine_ref) | copy-start | bytes 147460
  160.1 7.8 %collective-permute-start.7 = (f32[8,12,128]{2,1,0:T(8,128)S(1)}, f32[8,12,128]{2,1,0:T(8,128)S(1)}, u32[]{:S(2)}, u32[]{:S(2)}) collective-permute-start(f32[8,12,128]{2,1,0:T(8,128)S(1)} %pad_maximum_fusion.5.mine_ref), channel_id=1, source_target_pairs={{4,0},{8,4},{12,8},{16,12},{20,16},{24,20},{28,24},{32,28},{36,32}... | collective-permute-start | bytes 147464 | tf_op jit(solution)/shard_map/ppermute | solution.py:276
  165.9 10.4 %collective-permute-start.6 = (f32[8,12,128]{2,1,0:T(8,128)S(1)}, f32[8,12,128]{2,1,0:T(8,128)S(1)}, u32[]{:S(2)}, u32[]{:S(2)}) collective-permute-start(f32[8,12,128]{2,1,0:T(8,128)S(1)} %pad_maximum_fusion.5.mine_ref), channel_id=1, source_target_pairs={{0,4},{4,8},{8,12},{12,16},{16,20},{20,24},{24,28},{28,32},{32,36}... | collective-permute-start | bytes 147464 | tf_op jit(solution)/shard_map/ppermute | solution.py:276
  167.8 8.4 %copy-start.5 = (f32[8,12,128]{2,1,0:T(8,128)}, f32[8,12,128]{2,1,0:T(8,128)S(1)}, u32[]{:S(2)}) copy-start(f32[8,12,128]{2,1,0:T(8,128)S(1)} %collective-permute-done.7.after_ref) | copy-start | bytes 147460
  176.3 0.6 copy-start.6

commit v2 on v1

--- a/solution.py
+++ b/solution.py
@@ -73,8 +73,8 @@
         first = g * group
         exits = []
         for j in range(group):
-            a = spots[first + j, 0]
-            b = spots[first + j, 1]
+            a = spots[0, first + j]
+            b = spots[1, first + j]
             rows = pl.ds(a, LEN)
             keep = lane >= b
             shift = jnp.bitwise_and(LEN - b, LEN - 1)
@@ -96,11 +96,9 @@
         for j in range(0, group, 2):
             grad = dot(ahead_ref[...], pair_up([third_pass[k * LEN : (k + 1) * LEN] for k in (j, j + 1)]))
             for k in range(2):
-                a = spots[first + j + k, 0]
-                b = spots[first + j + k, 1]
+                a = spots[0, first + j + k]
+                b = spots[1, first + j + k]
                 rows = pl.ds(a, LEN)
-                keep = lane >= jnp.bitwise_and(b, LEN - 1)
-                wrap = b == LEN
                 gr = grad[:LEN, k * LEN : (k + 1) * LEN]
                 gi = grad[LEN:, k * LEN : (k + 1) * LEN]
                 pr = probe_ref[:, :LEN]
@@ -149,6 +147,7 @@
             pltpu.VMEM(counts.shape, jnp.float32),
             pltpu.SemaphoreType.DMA,
         ],
+        compiler_params=pltpu.CompilerParams(vmem_limit_bytes=16 << 20),
     )(spots, z.reshape(strips // 2, 32, LEN), probe, counts, *tables)
     return out.reshape(z.shape)
 
@@ -160,8 +159,8 @@
         re = jnp.zeros_like(planes[0])
         im = jnp.zeros_like(planes[0])
         for m in range(materials):
-            cr = spectra[e, 2 * m]
-            ci = spectra[e, 2 * m + 1]
+            cr = spectra[2 * m, e]
+            ci = spectra[2 * m + 1, e]
             re = re + cr * planes[m] - ci * planes[materials + m]
             im = im + cr * planes[materials + m] + ci * planes[m]
         out_ref[e, 0:8, :] = re
@@ -177,7 +176,7 @@
     mixed([rows_ref[p] for p in range(rows_ref.shape[0])], spectra, out_ref)
 
 
-def unmix_kernel(factor, spectra, grads_ref, rows_ref, out_ref):
+def unmix_kernel(factor, spectra, grads_ref, rows_ref, out_ref, low_ref, high_ref):
     materials = rows_ref.shape[0] // 2
 
     def one(e, sums):
@@ -185,8 +184,8 @@
         gi = grads_ref[e, 8:16, :]
         reals, imags = [], []
         for m in range(materials):
-            cr = spectra[e, 2 * m]
-            ci = spectra[e, 2 * m + 1]
+            cr = spectra[2 * m, e]
+            ci = spectra[2 * m + 1, e]
             reals.append(sums[m] + cr * gr + ci * gi)
             imags.append(sums[materials + m] + cr * gi - ci * gr)
         return tuple(reals + imags)
@@ -194,7 +193,10 @@
     zero = jnp.zeros(rows_ref.shape[1:], jnp.float32)
     sums = lax.fori_loop(0, grads_ref.shape[0], one, (zero,) * (2 * materials), unroll=8)
     for p in range(2 * materials):
-        out_ref[p] = rows_ref[p] - factor * sums[p]
+        value = rows_ref[p] - factor * sums[p]
+        out_ref[p] = value
+        low_ref[p] = value[:4]
+        high_ref[p] = value[4:]
 
 
 def smooth(place, last, mine_ref, before_ref, after_ref, field):
@@ -216,7 +218,7 @@
     inside = inside & ((lane < 2 * LEN) | ((lane >= low_edge) & (lane < high_edge)))
     results = [None] * planes
     for m in range(planes // 2):
-        pair = [field[m], field[planes // 2 + m]]
+        pair = [jnp.where(inside, field[p], 0.0) for p in (m, planes // 2 + m)]
         for _ in range(TV_STEPS):
             down = [pltpu.roll(x, 15, 0) - x for x in pair]
             across = [pltpu.roll(x, 3 * LEN - 1, 1) - x for x in pair]
@@ -256,23 +258,26 @@
         in_specs=[smem] * len(scalars) + [vmem] * len(arrays),
         out_specs=jax.tree.map(lambda _: vmem, out_shape),
         scratch_shapes=list(scratch),
+        compiler_params=pltpu.CompilerParams(vmem_limit_bytes=8 << 20),
     )(*scalars, *arrays)
 
 
-def with_edges(rows):
-    count = lax.axis_size("tile")
-    right = [(i, i + 1) for i in range(count - 1)]
-    left = [(b, a) for a, b in right]
-    from_left = lax.ppermute(rows[:, 4:8], "tile", right)
-    from_right = lax.ppermute(rows[:, 0:4], "tile", left)
+def ring(axis):
+    count = lax.axis_size(axis)
+    ahead = [(i, (i + 1) % count) for i in range(count)]
+    return ahead, [(b, a) for a, b in ahead]
+
+
+def with_edges(rows, low, high):
+    ahead, back = ring("tile")
+    from_left = lax.ppermute(high, "tile", ahead)
+    from_right = lax.ppermute(low, "tile", back)
     lane = lax.broadcasted_iota(jnp.int32, from_left.shape, 2)
     return jnp.concatenate([rows, jnp.where(lane < LEN // 2, from_right, from_left)], 1)
 
 
 def from_neighbours(strip):
-    count = lax.axis_size("energy")
-    ahead = [(i, i + 1) for i in range(count - 1)]
-    back = [(b, a) for a, b in ahead]
+    ahead, back = ring("energy")
     return lax.ppermute(strip, "energy", ahead), lax.ppermute(strip, "energy", back)
 
 
@@ -282,14 +287,15 @@
     rows, columns = material_maps.shape[2:]
     assert rows == 4 and columns == 2 * LEN
     probe = probes[0]
-    spots = offsets[0]
+    spots = offsets[0].T
     counts = measured[0, 0]
     tables = dft_blocks(*dft_tables(LEN))
-    weights = spectra.reshape(energies, 2 * materials)
+    weights = spectra.transpose(1, 2, 0).reshape(2 * materials, energies)
     factor = DATA_STEP / math.sqrt(energies)
     place = jnp.stack([lax.axis_index("energy"), lax.axis_index("tile")]).astype(jnp.int32)
     last = (lax.axis_size("energy") - 1, lax.axis_size("tile") - 1)
     strip = jax.ShapeDtypeStruct((planes, 2 * rows, LEN), jnp.float32)
+    part = jax.ShapeDtypeStruct((planes, rows, LEN), jnp.float32)
     spread = jax.ShapeDtypeStruct((energies, 4 * rows, LEN), jnp.float32)
     field = pltpu.VMEM((planes, 16, 3 * LEN), jnp.float32)
     maps = material_maps.reshape(planes, rows, columns)
@@ -299,8 +305,10 @@
         tile = lax.all_to_all(mixes, "energy", split_axis=0, concat_axis=0, tiled=True)
         grads = patch_gradient(tile, probe, spots, counts, tables)
         grads = lax.all_to_all(grads, "energy", split_axis=0, concat_axis=0, tiled=True)
-        current = on_chip(functools.partial(unmix_kernel, factor), strip, (weights,), (grads, current))
-        mine = with_edges(current)
+        current, low, high = on_chip(
+            functools.partial(unmix_kernel, factor), (strip, part, part), (weights,), (grads, current)
+        )
+        mine = with_edges(current, low, high)
         before, after = from_neighbours(mine)
         if repeat < ITERS - 1:
             current, mixes = on_chip(

time: 182 us -> 153 us (0.84); the launches traced: 179 us -> 152 us
  starting transfers between devices: 34.1 us -> 22.1 us
  Pallas kernels: 29.6 us -> 21.4 us
  blocking collectives: 69.4 us -> 63.2 us
  waiting for transfers between devices: 35.9 us -> 41 us
  other arithmetic: 3.48 us -> 0.68 us
  local copies, waits for them, and re-layouts: 6.47 us -> 3.77 us
    all_to_all x2, blocking collectives: 49 us -> 44.2 us  [shards(): lax.all_to_all(grads, 'energy', split_axis=0, concat_axis=0, tiled=True)]
    pallas_call x5, Pallas kernels: 12.2 us -> 7.58 us  [on_chip(): pl.pallas_call(kernel, out_shape=out_shape, in_specs=[smem] * len(scalars...]
    ppermute x2, starting transfers between devices: 12.1 us -> 7.75 us  [from_neighbours(): lax.ppermute(strip, 'energy', back)]
    ppermute x2, starting transfers between devices: 3.84 us -> 0.01 us  [from_neighbours(): lax.ppermute(strip, 'energy', ahead)]
    ppermute x4, starting transfers between devices: 5.14 us -> 1.34 us  [the longest x2 0.99 us: with_edges(): from_left = lax.ppermute(high, 'tile', ahead)]
    ppermute x2, waiting for transfers between devices: 0.01 us -> 3.73 us  [from_neighbours(): lax.ppermute(strip, 'energy', back)]
    pallas_call x2, Pallas kernels: 17.4 us -> 13.8 us  [patch_gradient(): pl.pallas_call(functools.partial(patch_kernel, group), out_shape=jax.Shap...]
    ppermute x2, waiting for transfers between devices: 16.2 us -> 13.2 us  [from_neighbours(): lax.ppermute(strip, 'energy', ahead)]
  transfers between devices with their start and end apart: 9 -> 9, of which waited for: 5 -> 9; matrix products, arithmetic and copies ran while one was open for 2% -> 0% of each run, Pallas kernels for 0% -> 0%
where the time goes in v2:
time: 153 us; the launch traced here: 152 us
  blocking collectives  63.2 us (41%)
  waiting for transfers between devices  41 us (27%)
  starting transfers between devices  22.1 us (14%)
  Pallas kernels  21.4 us (14%)
  local copies, waits for them, and re-layouts  3.77 us (2%)
    all_to_all x2, blocking collectives, shards(): lax.all_to_all(grads, 'energy', split_axis=0, concat_axis=0, tiled=True)  44.2 us
    all_to_all x1, blocking collectives, shards(): lax.all_to_all(mixes, 'energy', split_axis=0, concat_axis=0, tiled=True)  19.1 us
    all_to_all x1, waiting for transfers between devices, shards(): lax.all_to_all(mixes, 'energy', split_axis=0, concat_axis=0, tiled=True)  15.7 us
    pallas_call x2, Pallas kernels, patch_gradient(): pl.pallas_call(functools.partial(patch_kernel, group), out_shape=jax.Shap...  13.8 us
    ppermute x2, waiting for transfers between devices, from_neighbours(): lax.ppermute(strip, 'energy', ahead)  13.2 us
    all_to_all x1, starting transfers between devices, shards(): lax.all_to_all(mixes, 'energy', split_axis=0, concat_axis=0, tiled=True)  13 us
    ppermute x2, starting transfers between devices, from_neighbours(): lax.ppermute(strip, 'energy', back)  7.75 us
    pallas_call x5, Pallas kernels, on_chip(): pl.pallas_call(kernel, out_shape=out_shape, in_specs=[smem] * len(scalars...  7.58 us
  transfers between devices with their start and end apart: 9, of which 9 were waited for; matrix products, arithmetic and copies ran while one was open for 0% of the time, Pallas kernels for 0%

profile of v2, /device:TPU:8, one launch (start us, length us, event | category | flops | bytes accessed | tf_op | source)
XLA Modules:
  0.0 152.4 jit_solution(1768833255648943574)
XLA Ops:
  0.0 0.0 copy-start.2
  0.0 0.0 copy-start.3
  0.0 0.8 copy-done.3
  0.8 0.0 copy-start.5
  0.8 0.7 copy-done.5
  1.5 1.9 %shard_map.55 = f32[64,16,128]{2,1,0:T(8,128)} custom-call(f32[8,64]{1,0:T(8,128)S(1)} %bitcast.31, f32[8,4,256]{2,1,0:T(4,128)S(1)} %bitcast.29), custom_call_target="tpu_custom_call" | custom-call | tf_op jit(solution)/shard_map/pallas_call | solution.py:255
  3.4 13.0 %all-to-all-start = ((f32[64,16,128]{2,1,0:T(8,128)}), f32[64,16,128]{2,1,0:T(8,128)S(1)}, u32[]{:S(2)}, u32[]{:S(2)}) async-start(f32[64,16,128]{2,1,0:T(8,128)} %shard_map.55), calls=%async_computation | async-start | bytes 1048576 | tf_op jit(solution)/shard_map/all_to_all | solution.py:305
  16.4 0.3 fusion.8
  16.7 0.3 multiply_convert_fusion
  17.0 15.7 %all-to-all-done = f32[64,16,128]{2,1,0:T(8,128)S(1)} async-done(((f32[64,16,128]{2,1,0:T(8,128)}), f32[64,16,128]{2,1,0:T(8,128)S(1)}, u32[]{:S(2)}, u32[]{:S(2)}) %all-to-all-start) | async-done | bytes 524320 | tf_op jit(solution)/shard_map/all_to_all | solution.py:305
  32.7 0.0 copy-done.2
  32.7 0.0 copy-start
  32.7 1.6 %copy-done = f32[1,1,32,128,128]{4,3,2,1,0:T(8,128)S(1)} copy-done((f32[1,1,32,128,128]{4,3,2,1,0:T(8,128)S(1)}, f32[1,1,32,128,128]{4,3,2,1,0:T(8,128)}, u32[]{:S(2)}) %copy-start) | copy-done | bytes 2097176
  34.3 0.0 copy-start.7
  34.3 0.7 copy-done.7
  35.0 0.0 copy-start.4
  35.0 0.0 copy-start.6
  35.0 6.9 %shard_map.56 = f32[32,32,128]{2,1,0:T(8,128)S(1)} custom-call(s32[2,32]{1,0:T(2,128)S(1)} %bitcast.35, f32[32,32,128]{2,1,0:T(8,128)S(1)} %bitcast.23, f32[128,256]{1,0:T(8,128)S(1)} %bitcast.27, f32[32,128,128]{2,1,0:T(8,128)S(1)} %bitcast.21, bf16[256,256]{1,0:T(8,128)(2,1)S(1)} %get-tuple-element.22.ahead_ref, ...), custom_call_target="tpu_custom_call" | custom-call | tf_op jit(solution)/shard_map/pallas_call | solution.py:139
  41.9 0.0 copy-start.1
  41.9 0.0 copy-start.8
  41.9 23.1 %all_to_all.20.grads_ref = f32[64,16,128]{2,1,0:T(8,128)S(1)} all-to-all(f32[64,16,128]{2,1,0:T(8,128)S(1)} %bitcast.26), channel_id=1, replica_groups=mesh['energy'=64,'tile'=4] {'energy'}, dimensions={0} | all-to-all | bytes 1048576 | tf_op jit(solution)/shard_map/all_to_all | solution.py:307
  65.1 0.0 copy-done.4
  65.1 0.0 copy-done.6
  65.1 1.1 shard_map.57
  66.2 0.1 collective-permute-start
  66.3 0.5 collective-permute-start.1
  66.8 0.9 collective-permute-done
  67.7 3.3 %collective-permute-done.1 = f32[8,4,128]{2,1,0:T(4,128)S(1)} collective-permute-done((f32[8,4,128]{2,1,0:T(4,128)S(1)}, f32[8,4,128]{2,1,0:T(4,128)S(1)}, u32[]{:S(2)}, u32[]{:S(2)}) %collective-permute-start.1) | collective-permute-done | bytes 16416 | tf_op jit(solution)/shard_map/ppermute | solution.py:273
  71.0 3.9 %collective-permute-start.3 = (f32[8,12,128]{2,1,0:T(8,128)S(1)}, f32[8,12,128]{2,1,0:T(8,128)S(1)}, u32[]{:S(2)}, u32[]{:S(2)}) collective-permute-start(f32[8,12,128]{2,1,0:T(8,128)S(1)} %pad_maximum_fusion.4.mine_ref), channel_id=1, source_target_pairs={{4,0},{8,4},{12,8},{16,12},{20,16},{24,20},{28,24},{32,28},{36,32}... | collective-permute-start | bytes 147464 | tf_op jit(solution)/shard_map/ppermute | solution.py:281
  74.9 0.0 collective-permute-start.2
  74.9 0.1 pad_add_fusion.place
  75.0 1.8 %collective-permute-done.3.after_ref = f32[8,12,128]{2,1,0:T(8,128)S(1)} collective-permute-done((f32[8,12,128]{2,1,0:T(8,128)S(1)}, f32[8,12,128]{2,1,0:T(8,128)S(1)}, u32[]{:S(2)}, u32[]{:S(2)}) %collective-permute-start.3) | collective-permute-done | bytes 49184 | tf_op jit(solution)/shard_map/ppermute | solution.py:281
  76.8 6.6 %collective-permute-done.2.before_ref = f32[8,12,128]{2,1,0:T(8,128)S(1)} collective-permute-done((f32[8,12,128]{2,1,0:T(8,128)S(1)}, f32[8,12,128]{2,1,0:T(8,128)S(1)}, u32[]{:S(2)}, u32[]{:S(2)}) %collective-permute-start.2) | collective-permute-done | bytes 49184 | tf_op jit(solution)/shard_map/ppermute | solution.py:281
  83.4 1.7 %shard_map.58 = (f32[8,8,128]{2,1,0:T(8,128)S(1)}, f32[64,16,128]{2,1,0:T(8,128)S(1)}) custom-call(s32[2]{0:T(128)S(1)} %pad_add_fusion.place, f32[8,64]{1,0:T(8,128)S(1)} %bitcast.33, f32[8,12,128]{2,1,0:T(8,128)S(1)} %pad_maximum_fusion.4.mine_ref, f32[8,12,128]{2,1,0:T(8,128)S(1)} %collective-permute-done.2.before_ref, ...), custom_call_target="tpu_custom_call" | custom-call | tf_op jit(solution)/shard_map/pallas_call | solution.py:255
  85.1 19.1 %all_to_all.21 = f32[64,16,128]{2,1,0:T(8,128)S(1)} all-to-all(f32[64,16,128]{2,1,0:T(8,128)S(1)} %get-tuple-element.16), channel_id=1, replica_groups=mesh['energy'=64,'tile'=4] {'energy'}, dimensions={0} | all-to-all | bytes 1048576 | tf_op jit(solution)/shard_map/all_to_all | solution.py:305
  104.1 0.0 copy-done.1
  104.2 0.0 copy-done.8
  104.2 6.9 %shard_map.59 = f32[32,32,128]{2,1,0:T(8,128)S(1)} custom-call(s32[2,32]{1,0:T(2,128)S(1)} %bitcast.36, f32[32,32,128]{2,1,0:T(8,128)S(1)} %bitcast.24, f32[128,256]{1,0:T(8,128)S(1)} %bitcast.28, f32[32,128,128]{2,1,0:T(8,128)S(1)} %bitcast.22, bf16[256,256]{1,0:T(8,128)(2,1)S(1)} %get-tuple-element.22.ahead_ref, ...), custom_call_target="tpu_custom_call" | custom-call | tf_op jit(solution)/shard_map/pallas_call | solution.py:139
  111.1 21.0 %all_to_all.22.grads_ref = f32[64,16,128]{2,1,0:T(8,128)S(1)} all-to-all(f32[64,16,128]{2,1,0:T(8,128)S(1)} %bitcast.25), channel_id=1, replica_groups=mesh['energy'=64,'tile'=4] {'energy'}, dimensions={0} | all-to-all | bytes 1048576 | tf_op jit(solution)/shard_map/all_to_all | solution.py:307
  132.1 1.1 shard_map.60
  133.2 0.3 collective-permute-start.4
  133.5 0.5 collective-permute-start.5
  134.0 0.9 collective-permute-done.4
  134.9 3.3 %collective-permute-done.5 = f32[8,4,128]{2,1,0:T(4,128)S(1)} collective-permute-done((f32[8,4,128]{2,1,0:T(4,128)S(1)}, f32[8,4,128]{2,1,0:T(4,128)S(1)}, u32[]{:S(2)}, u32[]{:S(2)}) %collective-permute-start.5) | collective-permute-done | bytes 16416 | tf_op jit(solution)/shard_map/ppermute | solution.py:273
  138.2 3.9 %collective-permute-start.7 = (f32[8,12,128]{2,1,0:T(8,128)S(1)}, f32[8,12,128]{2,1,0:T(8,128)S(1)}, u32[]{:S(2)}, u32[]{:S(2)}) collective-permute-start(f32[8,12,128]{2,1,0:T(8,128)S(1)} %pad_maximum_fusion.5.mine_ref), channel_id=1, source_target_pairs={{4,0},{8,4},{12,8},{16,12},{20,16},{24,20},{28,24},{32,28},{36,32}... | collective-permute-start | bytes 147464 | tf_op jit(solution)/shard_map/ppermute | solution.py:281
  142.1 0.0 collective-permute-start.6
  142.1 1.9 %collective-permute-done.7.after_ref = f32[8,12,128]{2,1,0:T(8,128)S(1)} collective-permute-done((f32[8,12,128]{2,1,0:T(8,128)S(1)}, f32[8,12,128]{2,1,0:T(8,128)S(1)}, u32[]{:S(2)}, u32[]{:S(2)}) %collective-permute-start.7) | collective-permute-done | bytes 49184 | tf_op jit(solution)/shard_map/ppermute | solution.py:281
  144.0 6.6 %collective-permute-done.6.before_ref = f32[8,12,128]{2,1,0:T(8,128)S(1)} collective-permute-done((f32[8,12,128]{2,1,0:T(8,128)S(1)}, f32[8,12,128]{2,1,0:T(8,128)S(1)}, u32[]{:S(2)}, u32[]{:S(2)}) %collective-permute-start.6) | collective-permute-done | bytes 49184 | tf_op jit(solution)/shard_map/ppermute | solution.py:281
  150.6 1.8 %shard_map.61 = f32[8,4,256]{2,1,0:T(4,128)} custom-call(s32[2]{0:T(128)S(1)} %pad_add_fusion.place, f32[8,12,128]{2,1,0:T(8,128)S(1)} %pad_maximum_fusion.5.mine_ref, f32[8,12,128]{2,1,0:T(8,128)S(1)} %collective-permute-done.6.before_ref, f32[8,12,128]{2,1,0:T(8,128)S(1)} %collective-permute-done.7.after_ref), custom_call_target="tpu_custom_call" | custom-call | tf_op jit(solution)/shard_map/pallas_call | solution.py:255
  (6 shorter events, 0.1 us)
Async XLA Ops:
  0.0 32.7 %copy-start.2 = (f32[1,128,256]{2,1,0:T(8,128)S(1)}, f32[1,128,256]{2,1,0:T(8,128)}, u32[]{:S(2)}) copy-start(f32[1,128,256]{2,1,0:T(8,128)} %param.7) | copy-start | bytes 393220
  0.0 0.8 copy-start.3
  0.8 0.7 copy-start.5
  3.4 29.3 %all-to-all-start = ((f32[64,16,128]{2,1,0:T(8,128)}), f32[64,16,128]{2,1,0:T(8,128)S(1)}, u32[]{:S(2)}, u32[]{:S(2)}) async-start(f32[64,16,128]{2,1,0:T(8,128)} %shard_map.55), calls=%async_computation | async-start | bytes 1048576 | tf_op jit(solution)/shard_map/all_to_all | solution.py:305
  32.7 1.6 %copy-start = (f32[1,1,32,128,128]{4,3,2,1,0:T(8,128)S(1)}, f32[1,1,32,128,128]{4,3,2,1,0:T(8,128)}, u32[]{:S(2)}) copy-start(f32[1,1,32,128,128]{4,3,2,1,0:T(8,128)} %param.9) | copy-start | bytes 6291460
  34.3 0.7 copy-start.7
  35.0 30.1 %copy-start.4 = (f32[2,4,4,256]{3,2,1,0:T(4,128)S(1)}, f32[2,4,4,256]{3,2,1,0:T(4,128)}, u32[]{:S(2)}) copy-start(f32[2,4,4,256]{3,2,1,0:T(4,128)} %param.5) | copy-start | bytes 98308
  35.0 30.1 %copy-start.6 = (f32[64,4,2]{0,2,1:T(2,128)S(1)}, f32[64,4,2]{0,2,1:T(2,128)}, u32[]{:S(2)}) copy-start(f32[64,4,2]{0,2,1:T(2,128)} %param.6) | copy-start | bytes 6148
  41.9 62.3 %copy-start.1 = (f32[1,1,32,128,128]{4,3,2,1,0:T(8,128)S(1)}, f32[1,1,32,128,128]{4,3,2,1,0:T(8,128)}, u32[]{:S(2)}) copy-start(f32[1,1,32,128,128]{4,3,2,1,0:T(8,128)} %param.9) | copy-start | bytes 6291460
  41.9 62.3 %copy-start.8 = (s32[1,32,2]{1,2,0:T(2,128)S(1)}, s32[1,32,2]{1,2,0:T(2,128)}, u32[]{:S(2)}) copy-start(s32[1,32,2]{1,2,0:T(2,128)} %param.8) | copy-start | bytes 772
  66.2 1.5 %collective-permute-start = (f32[8,4,128]{2,1,0:T(4,128)S(1)}, f32[8,4,128]{2,1,0:T(4,128)S(1)}, u32[]{:S(2)}, u32[]{:S(2)}) collective-permute-start(f32[8,4,128]{2,1,0:T(4,128)S(1)} %get-tuple-element.14), channel_id=1, source_target_pairs={{1,0},{2,1},{3,2},{0,3},{5,4},{6,5},{7,6},{4,7},{9,8},{10,9},{11,1... | collective-permute-start | bytes 49160 | tf_op jit(solution)/shard_map/ppermute | solution.py:274
  66.3 4.7 %collective-permute-start.1 = (f32[8,4,128]{2,1,0:T(4,128)S(1)}, f32[8,4,128]{2,1,0:T(4,128)S(1)}, u32[]{:S(2)}, u32[]{:S(2)}) collective-permute-start(f32[8,4,128]{2,1,0:T(4,128)S(1)} %get-tuple-element.15), channel_id=1, source_target_pairs={{0,1},{1,2},{2,3},{3,0},{4,5},{5,6},{6,7},{7,4},{8,9},{9,10},{10,1... | collective-permute-start | bytes 49160 | tf_op jit(solution)/shard_map/ppermute | solution.py:273
  71.0 5.8 %collective-permute-start.3 = (f32[8,12,128]{2,1,0:T(8,128)S(1)}, f32[8,12,128]{2,1,0:T(8,128)S(1)}, u32[]{:S(2)}, u32[]{:S(2)}) collective-permute-start(f32[8,12,128]{2,1,0:T(8,128)S(1)} %pad_maximum_fusion.4.mine_ref), channel_id=1, source_target_pairs={{4,0},{8,4},{12,8},{16,12},{20,16},{24,20},{28,24},{32,28},{36,32}... | collective-permute-start | bytes 147464 | tf_op jit(solution)/shard_map/ppermute | solution.py:281
  74.9 8.5 %collective-permute-start.2 = (f32[8,12,128]{2,1,0:T(8,128)S(1)}, f32[8,12,128]{2,1,0:T(8,128)S(1)}, u32[]{:S(2)}, u32[]{:S(2)}) collective-permute-start(f32[8,12,128]{2,1,0:T(8,128)S(1)} %pad_maximum_fusion.4.mine_ref), channel_id=1, source_target_pairs={{0,4},{4,8},{8,12},{12,16},{16,20},{20,24},{24,28},{28,32},{32,36}... | collective-permute-start | bytes 147464 | tf_op jit(solution)/shard_map/ppermute | solution.py:281
  133.2 1.7 %collective-permute-start.4 = (f32[8,4,128]{2,1,0:T(4,128)S(1)}, f32[8,4,128]{2,1,0:T(4,128)S(1)}, u32[]{:S(2)}, u32[]{:S(2)}) collective-permute-start(f32[8,4,128]{2,1,0:T(4,128)S(1)} %get-tuple-element.19), channel_id=1, source_target_pairs={{1,0},{2,1},{3,2},{0,3},{5,4},{6,5},{7,6},{4,7},{9,8},{10,9},{11,1... | collective-permute-start | bytes 49160 | tf_op jit(solution)/shard_map/ppermute | solution.py:274
  133.5 4.7 %collective-permute-start.5 = (f32[8,4,128]{2,1,0:T(4,128)S(1)}, f32[8,4,128]{2,1,0:T(4,128)S(1)}, u32[]{:S(2)}, u32[]{:S(2)}) collective-permute-start(f32[8,4,128]{2,1,0:T(4,128)S(1)} %get-tuple-element.20), channel_id=1, source_target_pairs={{0,1},{1,2},{2,3},{3,0},{4,5},{5,6},{6,7},{7,4},{8,9},{9,10},{10,1... | collective-permute-start | bytes 49160 | tf_op jit(solution)/shard_map/ppermute | solution.py:273
  138.2 5.8 %collective-permute-start.7 = (f32[8,12,128]{2,1,0:T(8,128)S(1)}, f32[8,12,128]{2,1,0:T(8,128)S(1)}, u32[]{:S(2)}, u32[]{:S(2)}) collective-permute-start(f32[8,12,128]{2,1,0:T(8,128)S(1)} %pad_maximum_fusion.5.mine_ref), channel_id=1, source_target_pairs={{4,0},{8,4},{12,8},{16,12},{20,16},{24,20},{28,24},{32,28},{36,32}... | collective-permute-start | bytes 147464 | tf_op jit(solution)/shard_map/ppermute | solution.py:281
  142.1 8.5 %collective-permute-start.6 = (f32[8,12,128]{2,1,0:T(8,128)S(1)}, f32[8,12,128]{2,1,0:T(8,128)S(1)}, u32[]{:S(2)}, u32[]{:S(2)}) collective-permute-start(f32[8,12,128]{2,1,0:T(8,128)S(1)} %pad_maximum_fusion.5.mine_ref), channel_id=1, source_target_pairs={{0,4},{4,8},{8,12},{12,16},{16,20},{20,24},{24,28},{28,32},{32,36}... | collective-permute-start | bytes 147464 | tf_op jit(solution)/shard_map/ppermute | solution.py:281

commit v3 on v2

--- a/solution.py
+++ b/solution.py
@@ -3,6 +3,7 @@
 
 import jax
 import jax.numpy as jnp
+import numpy as np
 from jax import lax
 from jax.experimental import pallas as pl
 from jax.experimental.pallas import tpu as pltpu
@@ -15,22 +16,21 @@
 TV_EPS = 0.01
 
 LEN = 128
-GROUP = 8
+GROUP = 16
+LIMIT = 4096.0
 
 def dft_tables(length):
-    index = jnp.arange(length, dtype=jnp.int32)
-    phase = index[:, None] * index[None, :] % length
-    angle = phase.astype(jnp.float32) * (-2.0 * math.pi / length)
+    index = np.arange(length)
+    angle = (index[:, None] * index[None, :] % length) * (-2.0 * math.pi / length)
     scale = 1.0 / math.sqrt(length)
-    return (
-        (jnp.cos(angle) * scale).astype(jnp.bfloat16),
-        (jnp.sin(angle) * scale).astype(jnp.bfloat16),
-    )
+    return tuple((wave(angle) * scale).astype(np.float32).astype(jnp.bfloat16) for wave in (np.cos, np.sin))
+
 
 def dft_blocks(fr, fi):
-    ahead = jnp.concatenate([jnp.concatenate([fr, fi], 1), jnp.concatenate([-fi, fr], 1)], 0)
-    back = jnp.concatenate([jnp.concatenate([fr, -fi], 1), jnp.concatenate([fi, fr], 1)], 0)
-    return ahead, back
+    ahead = np.block([[fr, fi], [-fi, fr]])
+    back = np.block([[fr, -fi], [fi, fr]])
+    return jnp.asarray(ahead), jnp.asarray(back)
+
 
 def dot(left, right):
     return jnp.dot(left, right, preferred_element_type=jnp.float32)
@@ -41,32 +41,85 @@
         jnp.concatenate([one[:, :LEN], two[:, :LEN]], 1),
         jnp.concatenate([one[:, LEN:], two[:, LEN:]], 1)], 0)
 
-def patch_kernel(group, spots, z_ref, probe_ref, counts_hbm, ahead_ref, back_ref, out_ref, wave, total, counts, sem):
-    copy = pltpu.make_async_copy(counts_hbm, counts, sem)
-    copy.start()
+def sine_cosine(angle):
+    turns = jnp.floor(angle * (2.0 / math.pi) + 0.5)
+    rest = ((angle - turns * 1.5703125) - turns * 4.837512969970703125e-4) - turns * 7.54978995489188216e-8
+    quadrant = turns.astype(jnp.int32)
+    square = rest * rest
+    sine = ((-1.9515295891e-4 * square + 8.3321608736e-3) * square - 1.6666654611e-1) * square * rest + rest
+    cosine = ((2.443315711809948e-5 * square - 1.388731625493765e-3) * square + 4.166664568298827e-2) * square * square
+    cosine = cosine - 0.5 * square + 1.0
+    odd = (quadrant & 1) == 1
+    first = jnp.where(odd, cosine, sine)
+    second = jnp.where(odd, sine, cosine)
+    return (
+        jnp.where((quadrant & 2) == 2, -first, first),
+        jnp.where(((quadrant + 1) & 2) == 2, -second, second),
+    )
+
+
+def patch_kernel(
+    group, z_ref, spots_hbm, counts_hbm, probe_hbm, ahead_hbm, back_hbm, out_ref,
+    wave, total, spots, counts, probe_ref, ahead_ref, back_ref, sems
+):
+    copies = [
+        pltpu.make_async_copy(source, target, sems.at[i])
+        for i, (source, target) in enumerate(
+            (
+                (spots_hbm, spots),
+                (counts_hbm, counts),
+                (probe_hbm, probe_ref),
+                (ahead_hbm, ahead_ref),
+                (back_hbm, back_ref),
+            )
+        )
+    ]
+    for copy in copies:
+        copy.start()
     patches = counts.shape[0]
     blocks = z_ref.shape[0]
     step = 4
     upper = lax.broadcasted_iota(jnp.int32, (step, 8, LEN), 1) < 4
 
-    def expand(i, carry):
+    def parts(i, half):
         at = pl.multiple_of(i * step, step)
         rows = pl.ds(pl.multiple_of(i * step * 8, step * 8), step * 8)
+
+        def part(c):
+            low = z_ref[pl.ds(at, step), 8 * c + 4 * half : 8 * c + 4 * half + 8, :]
+            high = z_ref[pl.ds(at, step), 8 * c + 4 * half + 12 : 8 * c + 4 * half + 20, :]
+            return jnp.where(upper, low, high).reshape(step * 8, LEN)
+
+        return rows, part(0), part(1)
+
+    def expand(i, largest):
         for half in range(2):
-            def part(c):
-                low = z_ref[pl.ds(at, step), 8 * c + 4 * half : 8 * c + 4 * half + 8, :]
-                high = z_ref[pl.ds(at, step), 8 * c + 4 * half + 12 : 8 * c + 4 * half + 20, :]
-                return jnp.where(upper, low, high).reshape(step * 8, LEN)
-            growth = jnp.exp(part(0))
-            angle = part(1)
-            wave[half, rows, :] = growth * jnp.cos(angle)
-            wave[2 + half, rows, :] = growth * jnp.sin(angle)
+            rows, size, angle = parts(i, half)
+            growth = jnp.exp(size)
+            sine, cosine = sine_cosine(angle)
+            wave[half, rows, :] = growth * cosine
+            wave[2 + half, rows, :] = growth * sine
             total[half, rows, :] = jnp.zeros((step * 8, LEN), jnp.float32)
             total[2 + half, rows, :] = jnp.zeros((step * 8, LEN), jnp.float32)
-        return carry
-
-    lax.fori_loop(0, blocks // step, expand, 0)
-    copy.wait()
+            largest = jnp.maximum(largest, jnp.abs(angle))
+        return largest
+
+    largest = lax.fori_loop(0, blocks // step, expand, jnp.zeros((step * 8, LEN), jnp.float32))
+
+    @pl.when(jnp.max(largest) > LIMIT)
+    def _():
+        def again(i, carry):
+            for half in range(2):
+                rows, size, angle = parts(i, half)
+                growth = jnp.exp(size)
+                wave[half, rows, :] = growth * jnp.cos(angle)
+                wave[2 + half, rows, :] = growth * jnp.sin(angle)
+            return carry
+
+        lax.fori_loop(0, blocks // step, again, 0)
+
+    for copy in copies:
+        copy.wait()
     lane = lax.broadcasted_iota(jnp.int32, (LEN, LEN), 1)
 
     def one_group(g, carry):
@@ -133,22 +186,31 @@
     lax.fori_loop(0, blocks // step, finish, 0)
 
 
+def stay(array):
+    return pltpu.with_memory_space_constraint(array, pltpu.HBM)
+
+
 def patch_gradient(z, probe, spots, counts, tables, group=GROUP):
     strips = z.shape[0]
     vmem = pl.BlockSpec(memory_space=pltpu.VMEM)
+    hbm = pl.BlockSpec(memory_space=pltpu.HBM)
     out = pl.pallas_call(
         functools.partial(patch_kernel, group),
         out_shape=jax.ShapeDtypeStruct((strips // 2, 32, LEN), jnp.float32),
-        in_specs=[pl.BlockSpec(memory_space=pltpu.SMEM), vmem, vmem, pl.BlockSpec(memory_space=pl.ANY), vmem, vmem],
+        in_specs=[vmem] + [hbm] * 5,
         out_specs=vmem,
         scratch_shapes=[
             pltpu.VMEM((4, 4 * strips, LEN), jnp.float32),
             pltpu.VMEM((4, 4 * strips, LEN), jnp.float32),
+            pltpu.SMEM(spots.shape, jnp.int32),
             pltpu.VMEM(counts.shape, jnp.float32),
-            pltpu.SemaphoreType.DMA,
+            pltpu.VMEM(probe.shape, jnp.float32),
+            pltpu.VMEM((2 * LEN, 2 * LEN), jnp.bfloat16),
+            pltpu.VMEM((2 * LEN, 2 * LEN), jnp.bfloat16),
+            pltpu.SemaphoreType.DMA((5,)),
         ],
         compiler_params=pltpu.CompilerParams(vmem_limit_bytes=16 << 20),
-    )(spots, z.reshape(strips // 2, 32, LEN), probe, counts, *tables)
+    )(z.reshape(strips // 2, 32, LEN), *[stay(x) for x in (spots, counts, probe, *tables)])
     return out.reshape(z.shape)
 
 
@@ -170,9 +232,17 @@
     lax.fori_loop(0, out_ref.shape[0], one, 0, unroll=8)
 
 
-def mix_kernel(spectra, maps_ref, out_ref, rows_ref):
+def mix_kernel(spectra_hbm, maps_hbm, out_ref, maps, rows_ref, spectra, sems):
+    copies = [
+        pltpu.make_async_copy(spectra_hbm, spectra, sems.at[0]),
+        pltpu.make_async_copy(maps_hbm, maps, sems.at[1]),
+    ]
+    for copy in copies:
+        copy.start()
+    for copy in copies:
+        copy.wait()
     for half in range(2):
-        rows_ref[:, 4 * half : 4 * half + 4, :] = maps_ref[:, :, half * LEN : (half + 1) * LEN]
+        rows_ref[:, 4 * half : 4 * half + 4, :] = maps[:, :, half * LEN : (half + 1) * LEN]
     mixed([rows_ref[p] for p in range(rows_ref.shape[0])], spectra, out_ref)
 
 
@@ -300,7 +370,20 @@
     field = pltpu.VMEM((planes, 16, 3 * LEN), jnp.float32)
     maps = material_maps.reshape(planes, rows, columns)
     current = maps.reshape(planes, rows, 2, LEN).transpose(0, 2, 1, 3).reshape(planes, 2 * rows, LEN)
-    mixes = on_chip(mix_kernel, spread, (weights,), (maps,), [pltpu.VMEM((planes, 2 * rows, LEN), jnp.float32)])
+    hbm = pl.BlockSpec(memory_space=pltpu.HBM)
+    mixes = pl.pallas_call(
+        mix_kernel,
+        out_shape=spread,
+        in_specs=[hbm, hbm],
+        out_specs=pl.BlockSpec(memory_space=pltpu.VMEM),
+        scratch_shapes=[
+            pltpu.VMEM(maps.shape, jnp.float32),
+            pltpu.VMEM(strip.shape, jnp.float32),
+            pltpu.SMEM(weights.shape, jnp.float32),
+            pltpu.SemaphoreType.DMA((2,)),
+        ],
+        compiler_params=pltpu.CompilerParams(vmem_limit_bytes=8 << 20),
+    )(stay(weights), stay(maps))
     for repeat in range(ITERS):
         tile = lax.all_to_all(mixes, "energy", split_axis=0, concat_axis=0, tiled=True)
         grads = patch_gradient(tile, probe, spots, counts, tables)

time: 153 us -> 146 us (0.954)
  blocking collectives: 63.2 us -> 92.3 us
  waiting for transfers between devices: 41 us -> 25.4 us
  starting transfers between devices: 22.1 us -> 8.86 us
  local copies, waits for them, and re-layouts: 3.77 us -> 0.01 us
  Pallas kernels: 21.4 us -> 18.7 us
    all_to_all x1 -> x2, blocking collectives: 19.1 us -> 48.1 us  [shards(): lax.all_to_all(mixes, 'energy', split_axis=0, concat_axis=0, tiled=True)]
    all_to_all x1 -> x0, waiting for transfers between devices: 15.7 us -> none  [shards(): lax.all_to_all(mixes, 'energy', split_axis=0, concat_axis=0, tiled=True)]
    all_to_all x1 -> x0, starting transfers between devices: 13 us -> none  [shards(): lax.all_to_all(mixes, 'energy', split_axis=0, concat_axis=0, tiled=True)]
    unnamed x18 -> x4, local copies, waits for them, and re-layouts: 3.77 us -> 0.01 us
    pallas_call x2, Pallas kernels: 13.8 us -> 11.8 us  [patch_gradient(): pl.pallas_call(functools.partial(patch_kernel, group), out_shape=jax.Shap...]
    pallas_call x5 -> x4, Pallas kernels: 7.58 us -> 5.67 us  [on_chip(): pl.pallas_call(kernel, out_shape=out_shape, in_specs=[smem] * len(scalars...]
  transfers between devices with their start and end apart: 9 -> 8, of which waited for: 9 -> 8; matrix products, arithmetic and copies ran while one was open for 0% -> 0% of each run, Pallas kernels for 0% -> 0%
where the time goes in v3:
time: 146 us; the launch traced here: 145 us
  blocking collectives  92.3 us (63%)
  waiting for transfers between devices  25.4 us (17%)
  Pallas kernels  18.7 us (13%)
  starting transfers between devices  8.86 us (6%)
    all_to_all x2, blocking collectives, shards(): lax.all_to_all(mixes, 'energy', split_axis=0, concat_axis=0, tiled=True)  48.1 us
    all_to_all x2, blocking collectives, shards(): lax.all_to_all(grads, 'energy', split_axis=0, concat_axis=0, tiled=True)  44.2 us
    ppermute x2, waiting for transfers between devices, from_neighbours(): lax.ppermute(strip, 'energy', ahead)  13.2 us
    pallas_call x2, Pallas kernels, patch_gradient(): pl.pallas_call(functools.partial(patch_kernel, group), out_shape=jax.Shap...  11.8 us
    ppermute x2, starting transfers between devices, from_neighbours(): lax.ppermute(strip, 'energy', back)  7.69 us
    ppermute x2, waiting for transfers between devices, with_edges(): from_left = lax.ppermute(high, 'tile', ahead)  6.62 us
    pallas_call x4, Pallas kernels, on_chip(): pl.pallas_call(kernel, out_shape=out_shape, in_specs=[smem] * len(scalars...  5.67 us
    ppermute x2, waiting for transfers between devices, from_neighbours(): lax.ppermute(strip, 'energy', back)  3.73 us
  transfers between devices with their start and end apart: 8, of which 8 were waited for; matrix products, arithmetic and copies ran while one was open for 0% of the time, Pallas kernels for 0%

profile of v3, /device:TPU:8, one launch (start us, length us, event | category | flops | bytes accessed | tf_op | source)
XLA Modules:
  0.0 145.5 jit_solution(10809484262349157330)
XLA Ops:
  0.0 1.3 shard_map.73
  1.3 29.1 %all_to_all.20 = f32[64,16,128]{2,1,0:T(8,128)S(1)} all-to-all(f32[64,16,128]{2,1,0:T(8,128)S(1)} %shard_map.73), channel_id=1, replica_groups=mesh['energy'=64,'tile'=4] {'energy'}, dimensions={0} | all-to-all | bytes 1048576 | tf_op jit(solution)/shard_map/all_to_all | solution.py:388
  30.4 0.0 copy-start
  30.4 0.0 copy-start.1
  30.4 5.9 %shard_map.74 = f32[32,32,128]{2,1,0:T(8,128)S(1)} custom-call(f32[32,32,128]{2,1,0:T(8,128)S(1)} %bitcast.23, s32[2,32]{1,0:T(2,128)} %bitcast.35, f32[32,128,128]{2,1,0:T(8,128)} %bitcast.31, f32[128,256]{1,0:T(8,128)} %bitcast.33, bf16[256,256]{1,0:T(8,128)(2,1)} %constant.15.clone.ahead_hbm, bf16[256,256]{1,0:T(8,128)(2,1)} %constant.16.clone.back_hbm), custom_call_target="tpu_custom_call" | custom-call | tf_op jit(solution)/shard_map/pallas_call | solution.py:197
  36.3 23.0 %all_to_all.21.grads_ref = f32[64,16,128]{2,1,0:T(8,128)S(1)} all-to-all(f32[64,16,128]{2,1,0:T(8,128)S(1)} %bitcast.24), channel_id=1, replica_groups=mesh['energy'=64,'tile'=4] {'energy'}, dimensions={0} | all-to-all | bytes 1048576 | tf_op jit(solution)/shard_map/all_to_all | solution.py:390
  59.3 0.0 copy-done
  59.3 0.0 copy-done.1
  59.3 1.1 shard_map.75
  60.4 0.1 collective-permute-start
  60.5 0.5 collective-permute-start.1
  61.0 0.9 collective-permute-done
  61.9 3.3 %collective-permute-done.1 = f32[8,4,128]{2,1,0:T(4,128)S(1)} collective-permute-done((f32[8,4,128]{2,1,0:T(4,128)S(1)}, f32[8,4,128]{2,1,0:T(4,128)S(1)}, u32[]{:S(2)}, u32[]{:S(2)}) %collective-permute-start.1) | collective-permute-done | bytes 16416 | tf_op jit(solution)/shard_map/ppermute | solution.py:343
  65.3 3.9 %collective-permute-start.3 = (f32[8,12,128]{2,1,0:T(8,128)S(1)}, f32[8,12,128]{2,1,0:T(8,128)S(1)}, u32[]{:S(2)}, u32[]{:S(2)}) collective-permute-start(f32[8,12,128]{2,1,0:T(8,128)S(1)} %pad_maximum_fusion.mine_ref), channel_id=1, source_target_pairs={{4,0},{8,4},{12,8},{16,12},{20,16},{24,20},{28,24},{32,28},{36,32}... | collective-permute-start | bytes 147464 | tf_op jit(solution)/shard_map/ppermute | solution.py:351
  69.1 0.0 collective-permute-start.2
  69.1 0.1 pad_add_fusion.place
  69.2 1.8 %collective-permute-done.3.after_ref = f32[8,12,128]{2,1,0:T(8,128)S(1)} collective-permute-done((f32[8,12,128]{2,1,0:T(8,128)S(1)}, f32[8,12,128]{2,1,0:T(8,128)S(1)}, u32[]{:S(2)}, u32[]{:S(2)}) %collective-permute-start.3) | collective-permute-done | bytes 49184 | tf_op jit(solution)/shard_map/ppermute | solution.py:351
  71.0 6.6 %collective-permute-done.2.before_ref = f32[8,12,128]{2,1,0:T(8,128)S(1)} collective-permute-done((f32[8,12,128]{2,1,0:T(8,128)S(1)}, f32[8,12,128]{2,1,0:T(8,128)S(1)}, u32[]{:S(2)}, u32[]{:S(2)}) %collective-permute-start.2) | collective-permute-done | bytes 49184 | tf_op jit(solution)/shard_map/ppermute | solution.py:351
  77.6 1.7 %shard_map.76 = (f32[8,8,128]{2,1,0:T(8,128)S(1)}, f32[64,16,128]{2,1,0:T(8,128)S(1)}) custom-call(s32[2]{0:T(128)S(1)} %pad_add_fusion.place, f32[8,64]{1,0:T(8,128)S(1)} %bitcast.29, f32[8,12,128]{2,1,0:T(8,128)S(1)} %pad_maximum_fusion.mine_ref, f32[8,12,128]{2,1,0:T(8,128)S(1)} %collective-permute-done.2.before_ref, ...), custom_call_target="tpu_custom_call" | custom-call | tf_op jit(solution)/shard_map/pallas_call | solution.py:325
  79.3 19.0 %all_to_all.22 = f32[64,16,128]{2,1,0:T(8,128)S(1)} all-to-all(f32[64,16,128]{2,1,0:T(8,128)S(1)} %get-tuple-element.16), channel_id=1, replica_groups=mesh['energy'=64,'tile'=4] {'energy'}, dimensions={0} | all-to-all | bytes 1048576 | tf_op jit(solution)/shard_map/all_to_all | solution.py:388
  98.3 5.9 %shard_map.77 = f32[32,32,128]{2,1,0:T(8,128)S(1)} custom-call(f32[32,32,128]{2,1,0:T(8,128)S(1)} %bitcast.21, s32[2,32]{1,0:T(2,128)} %bitcast.36, f32[32,128,128]{2,1,0:T(8,128)} %bitcast.32, f32[128,256]{1,0:T(8,128)} %bitcast.34, bf16[256,256]{1,0:T(8,128)(2,1)} %constant.15.clone.ahead_hbm, bf16[256,256]{1,0:T(8,128)(2,1)} %constant.16.clone.back_hbm), custom_call_target="tpu_custom_call" | custom-call | tf_op jit(solution)/shard_map/pallas_call | solution.py:197
  104.2 21.2 %all_to_all.23.grads_ref = f32[64,16,128]{2,1,0:T(8,128)S(1)} all-to-all(f32[64,16,128]{2,1,0:T(8,128)S(1)} %bitcast.22), channel_id=1, replica_groups=mesh['energy'=64,'tile'=4] {'energy'}, dimensions={0} | all-to-all | bytes 1048576 | tf_op jit(solution)/shard_map/all_to_all | solution.py:390
  125.4 1.1 shard_map.78
  126.5 0.1 collective-permute-start.4
  126.6 0.5 collective-permute-start.5
  127.1 0.9 collective-permute-done.4
  128.1 3.3 %collective-permute-done.5 = f32[8,4,128]{2,1,0:T(4,128)S(1)} collective-permute-done((f32[8,4,128]{2,1,0:T(4,128)S(1)}, f32[8,4,128]{2,1,0:T(4,128)S(1)}, u32[]{:S(2)}, u32[]{:S(2)}) %collective-permute-start.5) | collective-permute-done | bytes 16416 | tf_op jit(solution)/shard_map/ppermute | solution.py:343
  131.4 3.8 %collective-permute-start.7 = (f32[8,12,128]{2,1,0:T(8,128)S(1)}, f32[8,12,128]{2,1,0:T(8,128)S(1)}, u32[]{:S(2)}, u32[]{:S(2)}) collective-permute-start(f32[8,12,128]{2,1,0:T(8,128)S(1)} %pad_maximum_fusion.1.mine_ref), channel_id=1, source_target_pairs={{4,0},{8,4},{12,8},{16,12},{20,16},{24,20},{28,24},{32,28},{36,32}... | collective-permute-start | bytes 147464 | tf_op jit(solution)/shard_map/ppermute | solution.py:351
  135.2 0.0 collective-permute-start.6
  135.2 1.9 %collective-permute-done.7.after_ref = f32[8,12,128]{2,1,0:T(8,128)S(1)} collective-permute-done((f32[8,12,128]{2,1,0:T(8,128)S(1)}, f32[8,12,128]{2,1,0:T(8,128)S(1)}, u32[]{:S(2)}, u32[]{:S(2)}) %collective-permute-start.7) | collective-permute-done | bytes 49184 | tf_op jit(solution)/shard_map/ppermute | solution.py:351
  137.1 6.6 %collective-permute-done.6.before_ref = f32[8,12,128]{2,1,0:T(8,128)S(1)} collective-permute-done((f32[8,12,128]{2,1,0:T(8,128)S(1)}, f32[8,12,128]{2,1,0:T(8,128)S(1)}, u32[]{:S(2)}, u32[]{:S(2)}) %collective-permute-start.6) | collective-permute-done | bytes 49184 | tf_op jit(solution)/shard_map/ppermute | solution.py:351
  143.7 1.8 %shard_map.79 = f32[8,4,256]{2,1,0:T(4,128)} custom-call(s32[2]{0:T(128)S(1)} %pad_add_fusion.place, f32[8,12,128]{2,1,0:T(8,128)S(1)} %pad_maximum_fusion.1.mine_ref, f32[8,12,128]{2,1,0:T(8,128)S(1)} %collective-permute-done.6.before_ref, f32[8,12,128]{2,1,0:T(8,128)S(1)} %collective-permute-done.7.after_ref), custom_call_target="tpu_custom_call" | custom-call | tf_op jit(solution)/shard_map/pallas_call | solution.py:325
  (5 shorter events, 0.0 us)
Async XLA Ops:
  30.4 28.9 %copy-start = (f32[2,4,4,256]{3,2,1,0:T(4,128)S(1)}, f32[2,4,4,256]{3,2,1,0:T(4,128)}, u32[]{:S(2)}) copy-start(f32[2,4,4,256]{3,2,1,0:T(4,128)} %param.7) | copy-start | bytes 98308
  30.4 28.9 %copy-start.1 = (f32[64,4,2]{0,2,1:T(2,128)S(1)}, f32[64,4,2]{0,2,1:T(2,128)}, u32[]{:S(2)}) copy-start(f32[64,4,2]{0,2,1:T(2,128)} %param.8) | copy-start | bytes 6148
  60.4 1.5 %collective-permute-start = (f32[8,4,128]{2,1,0:T(4,128)S(1)}, f32[8,4,128]{2,1,0:T(4,128)S(1)}, u32[]{:S(2)}, u32[]{:S(2)}) collective-permute-start(f32[8,4,128]{2,1,0:T(4,128)S(1)} %get-tuple-element.14), channel_id=1, source_target_pairs={{1,0},{2,1},{3,2},{0,3},{5,4},{6,5},{7,6},{4,7},{9,8},{10,9},{11,1... | collective-permute-start | bytes 49160 | tf_op jit(solution)/shard_map/ppermute | solution.py:344
  60.5 4.7 %collective-permute-start.1 = (f32[8,4,128]{2,1,0:T(4,128)S(1)}, f32[8,4,128]{2,1,0:T(4,128)S(1)}, u32[]{:S(2)}, u32[]{:S(2)}) collective-permute-start(f32[8,4,128]{2,1,0:T(4,128)S(1)} %get-tuple-element.15), channel_id=1, source_target_pairs={{0,1},{1,2},{2,3},{3,0},{4,5},{5,6},{6,7},{7,4},{8,9},{9,10},{10,1... | collective-permute-start | bytes 49160 | tf_op jit(solution)/shard_map/ppermute | solution.py:343
  65.3 5.8 %collective-permute-start.3 = (f32[8,12,128]{2,1,0:T(8,128)S(1)}, f32[8,12,128]{2,1,0:T(8,128)S(1)}, u32[]{:S(2)}, u32[]{:S(2)}) collective-permute-start(f32[8,12,128]{2,1,0:T(8,128)S(1)} %pad_maximum_fusion.mine_ref), channel_id=1, source_target_pairs={{4,0},{8,4},{12,8},{16,12},{20,16},{24,20},{28,24},{32,28},{36,32}... | collective-permute-start | bytes 147464 | tf_op jit(solution)/shard_map/ppermute | solution.py:351
  69.1 8.5 %collective-permute-start.2 = (f32[8,12,128]{2,1,0:T(8,128)S(1)}, f32[8,12,128]{2,1,0:T(8,128)S(1)}, u32[]{:S(2)}, u32[]{:S(2)}) collective-permute-start(f32[8,12,128]{2,1,0:T(8,128)S(1)} %pad_maximum_fusion.mine_ref), channel_id=1, source_target_pairs={{0,4},{4,8},{8,12},{12,16},{16,20},{20,24},{24,28},{28,32},{32,36}... | collective-permute-start | bytes 147464 | tf_op jit(solution)/shard_map/ppermute | solution.py:351
  126.5 1.5 %collective-permute-start.4 = (f32[8,4,128]{2,1,0:T(4,128)S(1)}, f32[8,4,128]{2,1,0:T(4,128)S(1)}, u32[]{:S(2)}, u32[]{:S(2)}) collective-permute-start(f32[8,4,128]{2,1,0:T(4,128)S(1)} %get-tuple-element.19), channel_id=1, source_target_pairs={{1,0},{2,1},{3,2},{0,3},{5,4},{6,5},{7,6},{4,7},{9,8},{10,9},{11,1... | collective-permute-start | bytes 49160 | tf_op jit(solution)/shard_map/ppermute | solution.py:344
  126.6 4.7 %collective-permute-start.5 = (f32[8,4,128]{2,1,0:T(4,128)S(1)}, f32[8,4,128]{2,1,0:T(4,128)S(1)}, u32[]{:S(2)}, u32[]{:S(2)}) collective-permute-start(f32[8,4,128]{2,1,0:T(4,128)S(1)} %get-tuple-element.20), channel_id=1, source_target_pairs={{0,1},{1,2},{2,3},{3,0},{4,5},{5,6},{6,7},{7,4},{8,9},{9,10},{10,1... | collective-permute-start | bytes 49160 | tf_op jit(solution)/shard_map/ppermute | solution.py:343
  131.4 5.7 %collective-permute-start.7 = (f32[8,12,128]{2,1,0:T(8,128)S(1)}, f32[8,12,128]{2,1,0:T(8,128)S(1)}, u32[]{:S(2)}, u32[]{:S(2)}) collective-permute-start(f32[8,12,128]{2,1,0:T(8,128)S(1)} %pad_maximum_fusion.1.mine_ref), channel_id=1, source_target_pairs={{4,0},{8,4},{12,8},{16,12},{20,16},{24,20},{28,24},{32,28},{36,32}... | collective-permute-start | bytes 147464 | tf_op jit(solution)/shard_map/ppermute | solution.py:351
  135.2 8.5 %collective-permute-start.6 = (f32[8,12,128]{2,1,0:T(8,128)S(1)}, f32[8,12,128]{2,1,0:T(8,128)S(1)}, u32[]{:S(2)}, u32[]{:S(2)}) collective-permute-start(f32[8,12,128]{2,1,0:T(8,128)S(1)} %pad_maximum_fusion.1.mine_ref), channel_id=1, source_target_pairs={{0,4},{4,8},{8,12},{12,16},{16,20},{20,24},{24,28},{28,32},{32,36}... | collective-permute-start | bytes 147464 | tf_op jit(solution)/shard_map/ppermute | solution.py:351

commit v4 on v3

--- a/solution.py
+++ b/solution.py
@@ -59,21 +59,13 @@
 
 
 def patch_kernel(
-    group, z_ref, spots_hbm, counts_hbm, probe_hbm, ahead_hbm, back_hbm, out_ref,
-    wave, total, spots, counts, probe_ref, ahead_ref, back_ref, sems
+    group, z_ref, spots_hbm, counts_from, probe_from, ahead_from, back_from, out_ref, wave, total, spots, *rest
 ):
-    copies = [
-        pltpu.make_async_copy(source, target, sems.at[i])
-        for i, (source, target) in enumerate(
-            (
-                (spots_hbm, spots),
-                (counts_hbm, counts),
-                (probe_hbm, probe_ref),
-                (ahead_hbm, ahead_ref),
-                (back_hbm, back_ref),
-            )
-        )
-    ]
+    *buffers, sems = rest
+    sources = (counts_from, probe_from, ahead_from, back_from)
+    counts, probe_ref, ahead_ref, back_ref = buffers or sources
+    moves = [(spots_hbm, spots), *zip(sources, buffers)]
+    copies = [pltpu.make_async_copy(source, target, sems.at[i]) for i, (source, target) in enumerate(moves)]
     for copy in copies:
         copy.start()
     patches = counts.shape[0]
@@ -190,27 +182,25 @@
     return pltpu.with_memory_space_constraint(array, pltpu.HBM)
 
 
-def patch_gradient(z, probe, spots, counts, tables, group=GROUP):
+def patch_gradient(z, probe, spots, counts, tables, resident, group=GROUP):
     strips = z.shape[0]
     vmem = pl.BlockSpec(memory_space=pltpu.VMEM)
     hbm = pl.BlockSpec(memory_space=pltpu.HBM)
+    inputs = (counts, probe, *tables)
     out = pl.pallas_call(
         functools.partial(patch_kernel, group),
         out_shape=jax.ShapeDtypeStruct((strips // 2, 32, LEN), jnp.float32),
-        in_specs=[vmem] + [hbm] * 5,
+        in_specs=[vmem, hbm] + [vmem if resident else hbm] * len(inputs),
         out_specs=vmem,
         scratch_shapes=[
             pltpu.VMEM((4, 4 * strips, LEN), jnp.float32),
             pltpu.VMEM((4, 4 * strips, LEN), jnp.float32),
             pltpu.SMEM(spots.shape, jnp.int32),
-            pltpu.VMEM(counts.shape, jnp.float32),
-            pltpu.VMEM(probe.shape, jnp.float32),
-            pltpu.VMEM((2 * LEN, 2 * LEN), jnp.bfloat16),
-            pltpu.VMEM((2 * LEN, 2 * LEN), jnp.bfloat16),
+            *([] if resident else [pltpu.VMEM(x.shape, x.dtype) for x in inputs]),
             pltpu.SemaphoreType.DMA((5,)),
         ],
         compiler_params=pltpu.CompilerParams(vmem_limit_bytes=16 << 20),
-    )(z.reshape(strips // 2, 32, LEN), *[stay(x) for x in (spots, counts, probe, *tables)])
+    )(z.reshape(strips // 2, 32, LEN), stay(spots), *(inputs if resident else [stay(x) for x in inputs]))
     return out.reshape(z.shape)
 
 
@@ -246,7 +236,7 @@
     mixed([rows_ref[p] for p in range(rows_ref.shape[0])], spectra, out_ref)
 
 
-def unmix_kernel(factor, spectra, grads_ref, rows_ref, out_ref, low_ref, high_ref):
+def unmix_kernel(factor, place, spectra, grads_ref, rows_ref, out_ref, near_ref, far_ref):
     materials = rows_ref.shape[0] // 2
 
     def one(e, sums):
@@ -260,22 +250,26 @@
             imags.append(sums[materials + m] + cr * gi - ci * gr)
         return tuple(reals + imags)
 
+    even = place[1] % 2 == 0
     zero = jnp.zeros(rows_ref.shape[1:], jnp.float32)
     sums = lax.fori_loop(0, grads_ref.shape[0], one, (zero,) * (2 * materials), unroll=8)
     for p in range(2 * materials):
         value = rows_ref[p] - factor * sums[p]
         out_ref[p] = value
-        low_ref[p] = value[:4]
-        high_ref[p] = value[4:]
-
-
-def smooth(place, last, mine_ref, before_ref, after_ref, field):
+        near_ref[p] = jnp.where(even, value[4:], value[:4])
+        far_ref[p] = jnp.where(even, value[:4], value[4:])
+
+
+def smooth(place, last, mine_ref, near_ref, far_ref, field):
     planes = mine_ref.shape[0]
+    even = place[0] % 2 == 0
     for j in range(3):
         lanes = slice(j * LEN, (j + 1) * LEN)
-        field[:, 0:4, lanes] = before_ref[:, 4 * j : 4 * j + 4, :]
+        near = near_ref[:, 4 * j : 4 * j + 4, :]
+        far = far_ref[:, 4 * j : 4 * j + 4, :]
+        field[:, 0:4, lanes] = jnp.where(even, far, near)
         field[:, 4:8, lanes] = mine_ref[:, 4 * j : 4 * j + 4, :]
-        field[:, 8:12, lanes] = after_ref[:, 4 * j : 4 * j + 4, :]
+        field[:, 8:12, lanes] = jnp.where(even, near, far)
         field[:, 12:16, lanes] = jnp.zeros((planes, 4, LEN), jnp.float32)
     shape = (16, 3 * LEN)
     row = lax.broadcasted_iota(jnp.int32, shape, 0)
@@ -305,16 +299,16 @@
     return results
 
 
-def smooth_mix_kernel(last, place, spectra, mine_ref, before_ref, after_ref, rows_ref, out_ref, field):
-    results = smooth(place, last, mine_ref, before_ref, after_ref, field)
+def smooth_mix_kernel(last, place, spectra, mine_ref, near_ref, far_ref, rows_ref, out_ref, field):
+    results = smooth(place, last, mine_ref, near_ref, far_ref, field)
     for p, value in enumerate(results):
         rows_ref[p, 0:4, :] = value[4:8, :LEN]
         rows_ref[p, 4:8, :] = value[4:8, LEN : 2 * LEN]
     mixed([rows_ref[p] for p in range(rows_ref.shape[0])], spectra, out_ref)
 
 
-def smooth_kernel(last, place, mine_ref, before_ref, after_ref, out_ref, field):
-    results = smooth(place, last, mine_ref, before_ref, after_ref, field)
+def smooth_kernel(last, place, mine_ref, near_ref, far_ref, out_ref, field):
+    results = smooth(place, last, mine_ref, near_ref, far_ref, field)
     for p, value in enumerate(results):
         out_ref[p] = value[4:8, : 2 * LEN]
 
@@ -332,23 +326,23 @@
     )(*scalars, *arrays)
 
 
-def ring(axis):
+def swaps(axis):
     count = lax.axis_size(axis)
-    ahead = [(i, (i + 1) % count) for i in range(count)]
-    return ahead, [(b, a) for a, b in ahead]
-
-
-def with_edges(rows, low, high):
-    ahead, back = ring("tile")
-    from_left = lax.ppermute(high, "tile", ahead)
-    from_right = lax.ppermute(low, "tile", back)
-    lane = lax.broadcasted_iota(jnp.int32, from_left.shape, 2)
-    return jnp.concatenate([rows, jnp.where(lane < LEN // 2, from_right, from_left)], 1)
+    near = [(i, i ^ 1) for i in range(count)]
+    return near, [((i + 1) % count, (k + 1) % count) for i, k in near]
+
+
+def with_edges(rows, to_near, to_far, even):
+    near, far = swaps("tile")
+    from_near = lax.ppermute(to_near, "tile", near)
+    from_far = lax.ppermute(to_far, "tile", far)
+    lane = lax.broadcasted_iota(jnp.int32, from_near.shape, 2)
+    return jnp.concatenate([rows, jnp.where((lane < LEN // 2) == even, from_near, from_far)], 1)
 
 
 def from_neighbours(strip):
-    ahead, back = ring("energy")
-    return lax.ppermute(strip, "energy", ahead), lax.ppermute(strip, "energy", back)
+    near, far = swaps("energy")
+    return lax.ppermute(strip, "energy", near), lax.ppermute(strip, "energy", far)
 
 
 def shards(material_maps, spectra, probes, offsets, measured):
@@ -368,7 +362,8 @@
     part = jax.ShapeDtypeStruct((planes, rows, LEN), jnp.float32)
     spread = jax.ShapeDtypeStruct((energies, 4 * rows, LEN), jnp.float32)
     field = pltpu.VMEM((planes, 16, 3 * LEN), jnp.float32)
-    maps = material_maps.reshape(planes, rows, columns)
+    even = place[1] % 2 == 0
+    maps, place, even = lax.optimization_barrier((material_maps.reshape(planes, rows, columns), place, even))
     current = maps.reshape(planes, rows, 2, LEN).transpose(0, 2, 1, 3).reshape(planes, 2 * rows, LEN)
     hbm = pl.BlockSpec(memory_space=pltpu.HBM)
     mixes = pl.pallas_call(
@@ -386,19 +381,19 @@
     )(stay(weights), stay(maps))
     for repeat in range(ITERS):
         tile = lax.all_to_all(mixes, "energy", split_axis=0, concat_axis=0, tiled=True)
-        grads = patch_gradient(tile, probe, spots, counts, tables)
+        grads = patch_gradient(tile, probe, spots, counts, tables, repeat > 0)
         grads = lax.all_to_all(grads, "energy", split_axis=0, concat_axis=0, tiled=True)
-        current, low, high = on_chip(
-            functools.partial(unmix_kernel, factor), (strip, part, part), (weights,), (grads, current)
+        current, to_near, to_far = on_chip(
+            functools.partial(unmix_kernel, factor), (strip, part, part), (place, weights), (grads, current)
         )
-        mine = with_edges(current, low, high)
-        before, after = from_neighbours(mine)
+        mine = with_edges(current, to_near, to_far, even)
+        near, far = from_neighbours(mine)
         if repeat < ITERS - 1:
             current, mixes = on_chip(
-                functools.partial(smooth_mix_kernel, last), (strip, spread), (place, weights), (mine, before, after), [field]
+                functools.partial(smooth_mix_kernel, last), (strip, spread), (place, weights), (mine, near, far), [field]
             )
     result = jax.ShapeDtypeStruct((planes, rows, columns), jnp.float32)
-    out = on_chip(functools.partial(smooth_kernel, last), result, (place,), (mine, before, after), [field])
+    out = on_chip(functools.partial(smooth_kernel, last), result, (place,), (mine, near, far), [field])
     return out.reshape(material_maps.shape)
 
 

time: 146 us -> 144 us (0.986)
  waiting for transfers between devices: 25.4 us -> 14.4 us
  blocking collectives: 92.3 us -> 97 us
  starting transfers between devices: 8.86 us -> 12.7 us
    ppermute x8, waiting for transfers between devices: 25.4 us -> 14.4 us  [the longest x2 9.75 us: from_neighbours(): lax.ppermute(strip, 'energy', far)]
    ppermute x8, starting transfers between devices: 8.86 us -> 12.7 us  [the longest x2 7.68 us: from_neighbours(): lax.ppermute(strip, 'energy', far)]
    all_to_all x2, blocking collectives: 48.1 us -> 51.2 us  [shards(): lax.all_to_all(mixes, 'energy', split_axis=0, concat_axis=0, tiled=True)]
    all_to_all x2, blocking collectives: 44.2 us -> 45.8 us  [shards(): lax.all_to_all(grads, 'energy', split_axis=0, concat_axis=0, tiled=True)]
  transfers between devices with their start and end apart: 8 -> 8, of which waited for: 8 -> 4; matrix products, arithmetic and copies ran while one was open for 0% -> 0% of each run, Pallas kernels for 0% -> 0%
where the time goes in v4:
time: 144 us; the launch traced here: 142 us
  blocking collectives  97 us (67%)
  Pallas kernels  17.7 us (12%)
  waiting for transfers between devices  14.4 us (10%)
  starting transfers between devices  12.7 us (9%)
    all_to_all x2, blocking collectives, shards(): lax.all_to_all(mixes, 'energy', split_axis=0, concat_axis=0, tiled=True)  51.2 us
    all_to_all x2, blocking collectives, shards(): lax.all_to_all(grads, 'energy', split_axis=0, concat_axis=0, tiled=True)  45.8 us
    pallas_call x2, Pallas kernels, patch_gradient(): pl.pallas_call(functools.partial(patch_kernel, group), out_shape=jax.Shap...  10.8 us
    ppermute x2, waiting for transfers between devices, from_neighbours(): lax.ppermute(strip, 'energy', far)  9.75 us
    ppermute x2, starting transfers between devices, from_neighbours(): lax.ppermute(strip, 'energy', far)  7.68 us
    pallas_call x4, Pallas kernels, on_chip(): pl.pallas_call(kernel, out_shape=out_shape, in_specs=[smem] * len(scalars...  5.63 us
    ppermute x2, starting transfers between devices, with_edges(): from_far = lax.ppermute(to_far, 'tile', far)  4.8 us
    ppermute x2, waiting for transfers between devices, with_edges(): from_far = lax.ppermute(to_far, 'tile', far)  4.69 us
  transfers between devices with their start and end apart: 8, of which 4 were waited for; matrix products, arithmetic and copies ran while one was open for 0% of the time, Pallas kernels for 0%

profile of v4, /device:TPU:8, one launch (start us, length us, event | category | flops | bytes accessed | tf_op | source)
XLA Modules:
  0.0 142.1 jit_solution(16802972853596548110)
XLA Ops:
  0.0 0.1 pad_add_fusion.place
  0.1 1.3 shard_map.73
  1.4 29.1 %all_to_all.20 = f32[64,16,128]{2,1,0:T(8,128)S(1)} all-to-all(f32[64,16,128]{2,1,0:T(8,128)S(1)} %shard_map.73), channel_id=1, replica_groups=mesh['energy'=64,'tile'=4] {'energy'}, dimensions={0} | all-to-all | bytes 1048576 | tf_op jit(solution)/shard_map/all_to_all | solution.py:383
  30.5 0.0 copy-start.4
  30.5 0.0 copy-start.5
  30.5 5.9 %shard_map.74 = f32[32,32,128]{2,1,0:T(8,128)S(1)} custom-call(f32[32,32,128]{2,1,0:T(8,128)S(1)} %bitcast.25, s32[2,32]{1,0:T(2,128)} %bitcast.35, f32[32,128,128]{2,1,0:T(8,128)} %bitcast.21, f32[128,256]{1,0:T(8,128)} %bitcast.27, bf16[256,256]{1,0:T(8,128)(2,1)} %constant.29.clone.ahead_from, bf16[256,256]{1,0:T(8,128)(2,1)} %constant.30.clone.back_from), custom_call_target="tpu_custom_call" | custom-call | tf_op jit(solution)/shard_map/pallas_call | solution.py:190
  36.4 0.0 copy-start
  36.4 0.0 copy-start.1
  36.4 0.0 copy-start.2
  36.4 0.0 copy-start.3
  36.4 23.2 %all_to_all.21.grads_ref = f32[64,16,128]{2,1,0:T(8,128)S(1)} all-to-all(f32[64,16,128]{2,1,0:T(8,128)S(1)} %bitcast.26), channel_id=1, replica_groups=mesh['energy'=64,'tile'=4] {'energy'}, dimensions={0} | all-to-all | bytes 1048576 | tf_op jit(solution)/shard_map/all_to_all | solution.py:385
  59.6 0.0 copy-done.4
  59.6 0.0 copy-done.5
  59.6 1.1 shard_map.75
  60.7 0.1 collective-permute-start
  60.8 2.4 %collective-permute-start.1 = (f32[8,4,128]{2,1,0:T(4,128)S(1)}, f32[8,4,128]{2,1,0:T(4,128)S(1)}, u32[]{:S(2)}, u32[]{:S(2)}) collective-permute-start(f32[8,4,128]{2,1,0:T(4,128)S(1)} %get-tuple-element.21), channel_id=1, source_target_pairs={{1,2},{2,1},{3,0},{0,3},{5,6},{6,5},{7,4},{4,7},{9,10},{10,9},{11,... | collective-permute-start | bytes 49160 | tf_op jit(solution)/shard_map/ppermute | solution.py:338
  63.2 0.0 collective-permute-done
  63.2 2.3 %collective-permute-done.1 = f32[8,4,128]{2,1,0:T(4,128)S(1)} collective-permute-done((f32[8,4,128]{2,1,0:T(4,128)S(1)}, f32[8,4,128]{2,1,0:T(4,128)S(1)}, u32[]{:S(2)}, u32[]{:S(2)}) %collective-permute-start.1) | collective-permute-done | bytes 16416 | tf_op jit(solution)/shard_map/ppermute | solution.py:338
  65.6 3.8 %collective-permute-start.3 = (f32[8,12,128]{2,1,0:T(8,128)S(1)}, f32[8,12,128]{2,1,0:T(8,128)S(1)}, u32[]{:S(2)}, u32[]{:S(2)}) collective-permute-start(f32[8,12,128]{2,1,0:T(8,128)S(1)} %pad_maximum_fusion.mine_ref), channel_id=1, source_target_pairs={{4,8},{8,4},{12,16},{16,12},{20,24},{24,20},{28,32},{32,28},{36,40... | collective-permute-start | bytes 147464 | tf_op jit(solution)/shard_map/ppermute | solution.py:345
  69.4 0.0 collective-permute-start.2
  69.4 4.9 %collective-permute-done.3.far_ref = f32[8,12,128]{2,1,0:T(8,128)S(1)} collective-permute-done((f32[8,12,128]{2,1,0:T(8,128)S(1)}, f32[8,12,128]{2,1,0:T(8,128)S(1)}, u32[]{:S(2)}, u32[]{:S(2)}) %collective-permute-start.3) | collective-permute-done | bytes 49184 | tf_op jit(solution)/shard_map/ppermute | solution.py:345
  74.3 0.0 collective-permute-done.2.near_ref
  74.3 1.7 %shard_map.76 = (f32[8,8,128]{2,1,0:T(8,128)S(1)}, f32[64,16,128]{2,1,0:T(8,128)S(1)}) custom-call(s32[2]{0:T(128)S(1)} %pad_add_fusion.place, f32[8,64]{1,0:T(8,128)S(1)} %bitcast.33, f32[8,12,128]{2,1,0:T(8,128)S(1)} %pad_maximum_fusion.mine_ref, f32[8,12,128]{2,1,0:T(8,128)S(1)} %collective-permute-done.2.near_ref, ...), custom_call_target="tpu_custom_call" | custom-call | tf_op jit(solution)/shard_map/pallas_call | solution.py:319
  76.0 22.1 %all_to_all.22 = f32[64,16,128]{2,1,0:T(8,128)S(1)} all-to-all(f32[64,16,128]{2,1,0:T(8,128)S(1)} %get-tuple-element.22), channel_id=1, replica_groups=mesh['energy'=64,'tile'=4] {'energy'}, dimensions={0} | all-to-all | bytes 1048576 | tf_op jit(solution)/shard_map/all_to_all | solution.py:383
  98.1 0.0 copy-done
  98.1 0.0 copy-done.1
  98.1 0.0 copy-done.2
  98.1 0.0 copy-done.3
  98.1 4.9 %shard_map.77 = f32[32,32,128]{2,1,0:T(8,128)S(1)} custom-call(f32[32,32,128]{2,1,0:T(8,128)S(1)} %bitcast.23, s32[2,32]{1,0:T(2,128)} %bitcast.36, f32[32,128,128]{2,1,0:T(8,128)S(1)} %bitcast.22, f32[128,256]{1,0:T(8,128)S(1)} %bitcast.28, bf16[256,256]{1,0:T(8,128)(2,1)S(1)} %copy-done.3, bf16[256,256]{1,0:T(8,128)(2,1)S(1)} %copy-done.2), custom_call_target="tpu_custom_call" | custom-call | tf_op jit(solution)/shard_map/pallas_call | solution.py:190
  103.0 22.6 %all_to_all.23.grads_ref = f32[64,16,128]{2,1,0:T(8,128)S(1)} all-to-all(f32[64,16,128]{2,1,0:T(8,128)S(1)} %bitcast.24), channel_id=1, replica_groups=mesh['energy'=64,'tile'=4] {'energy'}, dimensions={0} | all-to-all | bytes 1048576 | tf_op jit(solution)/shard_map/all_to_all | solution.py:385
  125.6 1.1 shard_map.78
  126.7 0.1 collective-permute-start.4
  126.8 2.4 %collective-permute-start.5 = (f32[8,4,128]{2,1,0:T(4,128)S(1)}, f32[8,4,128]{2,1,0:T(4,128)S(1)}, u32[]{:S(2)}, u32[]{:S(2)}) collective-permute-start(f32[8,4,128]{2,1,0:T(4,128)S(1)} %get-tuple-element.26), channel_id=1, source_target_pairs={{1,2},{2,1},{3,0},{0,3},{5,6},{6,5},{7,4},{4,7},{9,10},{10,9},{11,... | collective-permute-start | bytes 49160 | tf_op jit(solution)/shard_map/ppermute | solution.py:338
  129.3 0.0 collective-permute-done.4
  129.3 2.3 %collective-permute-done.5 = f32[8,4,128]{2,1,0:T(4,128)S(1)} collective-permute-done((f32[8,4,128]{2,1,0:T(4,128)S(1)}, f32[8,4,128]{2,1,0:T(4,128)S(1)}, u32[]{:S(2)}, u32[]{:S(2)}) %collective-permute-start.5) | collective-permute-done | bytes 16416 | tf_op jit(solution)/shard_map/ppermute | solution.py:338
  131.6 3.8 %collective-permute-start.7 = (f32[8,12,128]{2,1,0:T(8,128)S(1)}, f32[8,12,128]{2,1,0:T(8,128)S(1)}, u32[]{:S(2)}, u32[]{:S(2)}) collective-permute-start(f32[8,12,128]{2,1,0:T(8,128)S(1)} %pad_maximum_fusion.1.mine_ref), channel_id=1, source_target_pairs={{4,8},{8,4},{12,16},{16,12},{20,24},{24,20},{28,32},{32,28},{36,40... | collective-permute-start | bytes 147464 | tf_op jit(solution)/shard_map/ppermute | solution.py:345
  135.5 0.0 collective-permute-start.6
  135.5 4.9 %collective-permute-done.7.far_ref = f32[8,12,128]{2,1,0:T(8,128)S(1)} collective-permute-done((f32[8,12,128]{2,1,0:T(8,128)S(1)}, f32[8,12,128]{2,1,0:T(8,128)S(1)}, u32[]{:S(2)}, u32[]{:S(2)}) %collective-permute-start.7) | collective-permute-done | bytes 49184 | tf_op jit(solution)/shard_map/ppermute | solution.py:345
  140.3 0.0 collective-permute-done.6.near_ref
  140.3 1.7 %shard_map.79 = f32[8,4,256]{2,1,0:T(4,128)} custom-call(s32[2]{0:T(128)S(1)} %pad_add_fusion.place, f32[8,12,128]{2,1,0:T(8,128)S(1)} %pad_maximum_fusion.1.mine_ref, f32[8,12,128]{2,1,0:T(8,128)S(1)} %collective-permute-done.6.near_ref, f32[8,12,128]{2,1,0:T(8,128)S(1)} %collective-permute-done.7.far_ref), custom_call_target="tpu_custom_call" | custom-call | tf_op jit(solution)/shard_map/pallas_call | solution.py:319
  (5 shorter events, 0.0 us)
Async XLA Ops:
  30.5 29.1 %copy-start.4 = (f32[2,4,4,256]{3,2,1,0:T(4,128)S(1)}, f32[2,4,4,256]{3,2,1,0:T(4,128)}, u32[]{:S(2)}) copy-start(f32[2,4,4,256]{3,2,1,0:T(4,128)} %param.7) | copy-start | bytes 98308
  30.5 29.1 %copy-start.5 = (f32[64,4,2]{0,2,1:T(2,128)S(1)}, f32[64,4,2]{0,2,1:T(2,128)}, u32[]{:S(2)}) copy-start(f32[64,4,2]{0,2,1:T(2,128)} %param.8) | copy-start | bytes 6148
  36.4 61.7 %copy-start = (f32[1,1,32,128,128]{4,3,2,1,0:T(8,128)S(1)}, f32[1,1,32,128,128]{4,3,2,1,0:T(8,128)}, u32[]{:S(2)}) copy-start(f32[1,1,32,128,128]{4,3,2,1,0:T(8,128)} %param.11) | copy-start | bytes 6291460
  36.4 61.7 %copy-start.1 = (f32[1,128,256]{2,1,0:T(8,128)S(1)}, f32[1,128,256]{2,1,0:T(8,128)}, u32[]{:S(2)}) copy-start(f32[1,128,256]{2,1,0:T(8,128)} %param.9) | copy-start | bytes 393220
  36.4 61.7 %copy-start.2 = (bf16[256,256]{1,0:T(8,128)(2,1)S(1)}, bf16[256,256]{1,0:T(8,128)(2,1)}, u32[]{:S(2)}) copy-start(bf16[256,256]{1,0:T(8,128)(2,1)} %constant.30.clone.back_from) | copy-start | bytes 393220
  36.4 61.7 %copy-start.3 = (bf16[256,256]{1,0:T(8,128)(2,1)S(1)}, bf16[256,256]{1,0:T(8,128)(2,1)}, u32[]{:S(2)}) copy-start(bf16[256,256]{1,0:T(8,128)(2,1)} %constant.29.clone.ahead_from) | copy-start | bytes 393220
  60.7 2.5 %collective-permute-start = (f32[8,4,128]{2,1,0:T(4,128)S(1)}, f32[8,4,128]{2,1,0:T(4,128)S(1)}, u32[]{:S(2)}, u32[]{:S(2)}) collective-permute-start(f32[8,4,128]{2,1,0:T(4,128)S(1)} %get-tuple-element.20), channel_id=1, source_target_pairs={{0,1},{1,0},{2,3},{3,2},{4,5},{5,4},{6,7},{7,6},{8,9},{9,8},{10,11... | collective-permute-start | bytes 49160 | tf_op jit(solution)/shard_map/ppermute | solution.py:337
  60.8 4.8 %collective-permute-start.1 = (f32[8,4,128]{2,1,0:T(4,128)S(1)}, f32[8,4,128]{2,1,0:T(4,128)S(1)}, u32[]{:S(2)}, u32[]{:S(2)}) collective-permute-start(f32[8,4,128]{2,1,0:T(4,128)S(1)} %get-tuple-element.21), channel_id=1, source_target_pairs={{1,2},{2,1},{3,0},{0,3},{5,6},{6,5},{7,4},{4,7},{9,10},{10,9},{11,... | collective-permute-start | bytes 49160 | tf_op jit(solution)/shard_map/ppermute | solution.py:338
  65.6 8.7 %collective-permute-start.3 = (f32[8,12,128]{2,1,0:T(8,128)S(1)}, f32[8,12,128]{2,1,0:T(8,128)S(1)}, u32[]{:S(2)}, u32[]{:S(2)}) collective-permute-start(f32[8,12,128]{2,1,0:T(8,128)S(1)} %pad_maximum_fusion.mine_ref), channel_id=1, source_target_pairs={{4,8},{8,4},{12,16},{16,12},{20,24},{24,20},{28,32},{32,28},{36,40... | collective-permute-start | bytes 147464 | tf_op jit(solution)/shard_map/ppermute | solution.py:345
  69.4 4.9 %collective-permute-start.2 = (f32[8,12,128]{2,1,0:T(8,128)S(1)}, f32[8,12,128]{2,1,0:T(8,128)S(1)}, u32[]{:S(2)}, u32[]{:S(2)}) collective-permute-start(f32[8,12,128]{2,1,0:T(8,128)S(1)} %pad_maximum_fusion.mine_ref), channel_id=1, source_target_pairs={{0,4},{4,0},{8,12},{12,8},{16,20},{20,16},{24,28},{28,24},{32,36},... | collective-permute-start | bytes 147464 | tf_op jit(solution)/shard_map/ppermute | solution.py:345
  126.7 2.5 %collective-permute-start.4 = (f32[8,4,128]{2,1,0:T(4,128)S(1)}, f32[8,4,128]{2,1,0:T(4,128)S(1)}, u32[]{:S(2)}, u32[]{:S(2)}) collective-permute-start(f32[8,4,128]{2,1,0:T(4,128)S(1)} %get-tuple-element.25), channel_id=1, source_target_pairs={{0,1},{1,0},{2,3},{3,2},{4,5},{5,4},{6,7},{7,6},{8,9},{9,8},{10,11... | collective-permute-start | bytes 49160 | tf_op jit(solution)/shard_map/ppermute | solution.py:337
  126.8 4.8 %collective-permute-start.5 = (f32[8,4,128]{2,1,0:T(4,128)S(1)}, f32[8,4,128]{2,1,0:T(4,128)S(1)}, u32[]{:S(2)}, u32[]{:S(2)}) collective-permute-start(f32[8,4,128]{2,1,0:T(4,128)S(1)} %get-tuple-element.26), channel_id=1, source_target_pairs={{1,2},{2,1},{3,0},{0,3},{5,6},{6,5},{7,4},{4,7},{9,10},{10,9},{11,... | collective-permute-start | bytes 49160 | tf_op jit(solution)/shard_map/ppermute | solution.py:338
  131.6 8.7 %collective-permute-start.7 = (f32[8,12,128]{2,1,0:T(8,128)S(1)}, f32[8,12,128]{2,1,0:T(8,128)S(1)}, u32[]{:S(2)}, u32[]{:S(2)}) collective-permute-start(f32[8,12,128]{2,1,0:T(8,128)S(1)} %pad_maximum_fusion.1.mine_ref), channel_id=1, source_target_pairs={{4,8},{8,4},{12,16},{16,12},{20,24},{24,20},{28,32},{32,28},{36,40... | collective-permute-start | bytes 147464 | tf_op jit(solution)/shard_map/ppermute | solution.py:345
  135.5 4.9 %collective-permute-start.6 = (f32[8,12,128]{2,1,0:T(8,128)S(1)}, f32[8,12,128]{2,1,0:T(8,128)S(1)}, u32[]{:S(2)}, u32[]{:S(2)}) collective-permute-start(f32[8,12,128]{2,1,0:T(8,128)S(1)} %pad_maximum_fusion.1.mine_ref), channel_id=1, source_target_pairs={{0,4},{4,0},{8,12},{12,8},{16,20},{20,16},{24,28},{28,24},{32,36},... | collective-permute-start | bytes 147464 | tf_op jit(solution)/shard_map/ppermute | solution.py:345

commit v5 on v4

--- a/solution.py
+++ b/solution.py
@@ -59,15 +59,10 @@
 
 
 def patch_kernel(
-    group, z_ref, spots_hbm, counts_from, probe_from, ahead_from, back_from, out_ref, wave, total, spots, *rest
+    group, z_ref, spots_hbm, counts, probe_ref, ahead_ref, back_ref, out_ref, wave, total, spots, sem
 ):
-    *buffers, sems = rest
-    sources = (counts_from, probe_from, ahead_from, back_from)
-    counts, probe_ref, ahead_ref, back_ref = buffers or sources
-    moves = [(spots_hbm, spots), *zip(sources, buffers)]
-    copies = [pltpu.make_async_copy(source, target, sems.at[i]) for i, (source, target) in enumerate(moves)]
-    for copy in copies:
-        copy.start()
+    copy = pltpu.make_async_copy(spots_hbm, spots, sem)
+    copy.start()
     patches = counts.shape[0]
     blocks = z_ref.shape[0]
     step = 4
@@ -110,8 +105,7 @@
 
         lax.fori_loop(0, blocks // step, again, 0)
 
-    for copy in copies:
-        copy.wait()
+    copy.wait()
     lane = lax.broadcasted_iota(jnp.int32, (LEN, LEN), 1)
 
     def one_group(g, carry):
@@ -182,7 +176,7 @@
     return pltpu.with_memory_space_constraint(array, pltpu.HBM)
 
 
-def patch_gradient(z, probe, spots, counts, tables, resident, group=GROUP):
+def patch_gradient(z, probe, spots, counts, tables, group=GROUP):
     strips = z.shape[0]
     vmem = pl.BlockSpec(memory_space=pltpu.VMEM)
     hbm = pl.BlockSpec(memory_space=pltpu.HBM)
@@ -190,17 +184,16 @@
     out = pl.pallas_call(
         functools.partial(patch_kernel, group),
         out_shape=jax.ShapeDtypeStruct((strips // 2, 32, LEN), jnp.float32),
-        in_specs=[vmem, hbm] + [vmem if resident else hbm] * len(inputs),
+        in_specs=[vmem, hbm] + [vmem] * len(inputs),
         out_specs=vmem,
         scratch_shapes=[
             pltpu.VMEM((4, 4 * strips, LEN), jnp.float32),
             pltpu.VMEM((4, 4 * strips, LEN), jnp.float32),
             pltpu.SMEM(spots.shape, jnp.int32),
-            *([] if resident else [pltpu.VMEM(x.shape, x.dtype) for x in inputs]),
-            pltpu.SemaphoreType.DMA((5,)),
+            pltpu.SemaphoreType.DMA,
         ],
         compiler_params=pltpu.CompilerParams(vmem_limit_bytes=16 << 20),
-    )(z.reshape(strips // 2, 32, LEN), stay(spots), *(inputs if resident else [stay(x) for x in inputs]))
+    )(z.reshape(strips // 2, 32, LEN), stay(spots), *inputs)
     return out.reshape(z.shape)
 
 
@@ -222,7 +215,8 @@
     lax.fori_loop(0, out_ref.shape[0], one, 0, unroll=8)
 
 
-def mix_kernel(spectra_hbm, maps_hbm, out_ref, maps, rows_ref, spectra, sems):
+def mix_kernel(spectra_hbm, maps_hbm, *rest):
+    out_ref, maps, rows_ref, spectra, sems = rest[-5:]
     copies = [
         pltpu.make_async_copy(spectra_hbm, spectra, sems.at[0]),
         pltpu.make_async_copy(maps_hbm, maps, sems.at[1]),
@@ -366,10 +360,11 @@
     maps, place, even = lax.optimization_barrier((material_maps.reshape(planes, rows, columns), place, even))
     current = maps.reshape(planes, rows, 2, LEN).transpose(0, 2, 1, 3).reshape(planes, 2 * rows, LEN)
     hbm = pl.BlockSpec(memory_space=pltpu.HBM)
+    later = (counts, probe, *tables)
     mixes = pl.pallas_call(
         mix_kernel,
         out_shape=spread,
-        in_specs=[hbm, hbm],
+        in_specs=[hbm] * (2 + len(later)),
         out_specs=pl.BlockSpec(memory_space=pltpu.VMEM),
         scratch_shapes=[
             pltpu.VMEM(maps.shape, jnp.float32),
@@ -378,10 +373,10 @@
             pltpu.SemaphoreType.DMA((2,)),
         ],
         compiler_params=pltpu.CompilerParams(vmem_limit_bytes=8 << 20),
-    )(stay(weights), stay(maps))
+    )(*[stay(x) for x in (weights, maps, *later)])
     for repeat in range(ITERS):
         tile = lax.all_to_all(mixes, "energy", split_axis=0, concat_axis=0, tiled=True)
-        grads = patch_gradient(tile, probe, spots, counts, tables, repeat > 0)
+        grads = patch_gradient(tile, probe, spots, counts, tables)
         grads = lax.all_to_all(grads, "energy", split_axis=0, concat_axis=0, tiled=True)
         current, to_near, to_far = on_chip(
             functools.partial(unmix_kernel, factor), (strip, part, part), (place, weights), (grads, current)

time: 144 us -> 143 us (level)
  no operation moved by 1% of the time
where the time goes in v5:
time: 143 us; the launch traced here: 141 us
  blocking collectives  96.8 us (68%)
  Pallas kernels  16.9 us (12%)
  waiting for transfers between devices  14.5 us (10%)
  starting transfers between devices  12.6 us (9%)
    all_to_all x2, blocking collectives, shards(): lax.all_to_all(mixes, 'energy', split_axis=0, concat_axis=0, tiled=True)  51.2 us
    all_to_all x2, blocking collectives, shards(): lax.all_to_all(grads, 'energy', split_axis=0, concat_axis=0, tiled=True)  45.7 us
    pallas_call x2, Pallas kernels, patch_gradient(): pl.pallas_call(functools.partial(patch_kernel, group), out_shape=jax.Shap...  9.86 us
    ppermute x2, waiting for transfers between devices, from_neighbours(): lax.ppermute(strip, 'energy', far)  9.75 us
    ppermute x2, starting transfers between devices, from_neighbours(): lax.ppermute(strip, 'energy', far)  7.68 us
    pallas_call x4, Pallas kernels, on_chip(): pl.pallas_call(kernel, out_shape=out_shape, in_specs=[smem] * len(scalars...  5.63 us
    ppermute x2, starting transfers between devices, with_edges(): from_far = lax.ppermute(to_far, 'tile', far)  4.78 us
    ppermute x2, waiting for transfers between devices, with_edges(): from_far = lax.ppermute(to_far, 'tile', far)  4.71 us
  transfers between devices with their start and end apart: 8, of which 4 were waited for; matrix products, arithmetic and copies ran while one was open for 0% of the time, Pallas kernels for 0%

profile of v5, /device:TPU:8, one launch (start us, length us, event | category | flops | bytes accessed | tf_op | source)
XLA Modules:
  0.0 141.1 jit_solution(15708360390306730264)
XLA Ops:
  0.0 0.0 copy-start.2
  0.0 0.0 copy-start.3
  0.0 0.0 copy-start
  0.0 0.0 copy-start.1
  0.0 0.1 pad_add_fusion.place
  0.1 1.4 %shard_map.73 = f32[64,16,128]{2,1,0:T(8,128)S(1)} custom-call(f32[8,64]{1,0:T(8,128)} %bitcast.33, f32[8,4,256]{2,1,0:T(4,128)} %bitcast.31, f32[32,128,128]{2,1,0:T(8,128)} %bitcast.21, f32[128,256]{1,0:T(8,128)} %bitcast.28, bf16[256,256]{1,0:T(8,128)(2,1)} %constant.29.clone.rest_2_.ahead_ref, bf16[256,256]{1,0:T(8,128)(2,1)} %constant.30.clone.rest_3_.back_ref), custom_call_target="tpu_custom_call" | custom-call | tf_op jit(solution)/shard_map/pallas_call | solution.py:364
  1.5 29.1 %all_to_all.20 = f32[64,16,128]{2,1,0:T(8,128)S(1)} all-to-all(f32[64,16,128]{2,1,0:T(8,128)S(1)} %shard_map.73), channel_id=1, replica_groups=mesh['energy'=64,'tile'=4] {'energy'}, dimensions={0} | all-to-all | bytes 1048576 | tf_op jit(solution)/shard_map/all_to_all | solution.py:378
  30.6 0.0 copy-done.2
  30.6 0.0 copy-done.3
  30.6 0.0 copy-done
  30.6 0.0 copy-done.1
  30.7 0.0 copy-start.4
  30.7 0.0 copy-start.5
  30.7 5.0 %shard_map.74 = f32[32,32,128]{2,1,0:T(8,128)S(1)} custom-call(f32[32,32,128]{2,1,0:T(8,128)S(1)} %bitcast.26, s32[2,32]{1,0:T(2,128)} %bitcast.37, f32[32,128,128]{2,1,0:T(8,128)S(1)} %bitcast.22, f32[128,256]{1,0:T(8,128)S(1)} %bitcast.29, bf16[256,256]{1,0:T(8,128)(2,1)S(1)} %copy-done.3, bf16[256,256]{1,0:T(8,128)(2,1)S(1)} %copy-done.2), custom_call_target="tpu_custom_call" | custom-call | tf_op jit(solution)/shard_map/pallas_call | solution.py:184
  35.7 23.0 %all_to_all.21.grads_ref = f32[64,16,128]{2,1,0:T(8,128)S(1)} all-to-all(f32[64,16,128]{2,1,0:T(8,128)S(1)} %bitcast.27), channel_id=1, replica_groups=mesh['energy'=64,'tile'=4] {'energy'}, dimensions={0} | all-to-all | bytes 1048576 | tf_op jit(solution)/shard_map/all_to_all | solution.py:380
  58.7 0.0 copy-done.4
  58.7 0.0 copy-done.5
  58.7 1.1 shard_map.75
  59.9 0.1 collective-permute-start
  60.0 2.4 %collective-permute-start.1 = (f32[8,4,128]{2,1,0:T(4,128)S(1)}, f32[8,4,128]{2,1,0:T(4,128)S(1)}, u32[]{:S(2)}, u32[]{:S(2)}) collective-permute-start(f32[8,4,128]{2,1,0:T(4,128)S(1)} %get-tuple-element.21), channel_id=1, source_target_pairs={{1,2},{2,1},{3,0},{0,3},{5,6},{6,5},{7,4},{4,7},{9,10},{10,9},{11,... | collective-permute-start | bytes 49160 | tf_op jit(solution)/shard_map/ppermute | solution.py:332
  62.4 0.0 collective-permute-done
  62.4 2.4 %collective-permute-done.1 = f32[8,4,128]{2,1,0:T(4,128)S(1)} collective-permute-done((f32[8,4,128]{2,1,0:T(4,128)S(1)}, f32[8,4,128]{2,1,0:T(4,128)S(1)}, u32[]{:S(2)}, u32[]{:S(2)}) %collective-permute-start.1) | collective-permute-done | bytes 16416 | tf_op jit(solution)/shard_map/ppermute | solution.py:332
  64.7 3.8 %collective-permute-start.3 = (f32[8,12,128]{2,1,0:T(8,128)S(1)}, f32[8,12,128]{2,1,0:T(8,128)S(1)}, u32[]{:S(2)}, u32[]{:S(2)}) collective-permute-start(f32[8,12,128]{2,1,0:T(8,128)S(1)} %pad_maximum_fusion.mine_ref), channel_id=1, source_target_pairs={{4,8},{8,4},{12,16},{16,12},{20,24},{24,20},{28,32},{32,28},{36,40... | collective-permute-start | bytes 147464 | tf_op jit(solution)/shard_map/ppermute | solution.py:339
  68.6 0.0 collective-permute-start.2
  68.6 4.9 %collective-permute-done.3.far_ref = f32[8,12,128]{2,1,0:T(8,128)S(1)} collective-permute-done((f32[8,12,128]{2,1,0:T(8,128)S(1)}, f32[8,12,128]{2,1,0:T(8,128)S(1)}, u32[]{:S(2)}, u32[]{:S(2)}) %collective-permute-start.3) | collective-permute-done | bytes 49184 | tf_op jit(solution)/shard_map/ppermute | solution.py:339
  73.4 0.0 collective-permute-done.2.near_ref
  73.5 1.7 %shard_map.76 = (f32[8,8,128]{2,1,0:T(8,128)S(1)}, f32[64,16,128]{2,1,0:T(8,128)S(1)}) custom-call(s32[2]{0:T(128)S(1)} %pad_add_fusion.place, f32[8,64]{1,0:T(8,128)S(1)} %bitcast.35, f32[8,12,128]{2,1,0:T(8,128)S(1)} %pad_maximum_fusion.mine_ref, f32[8,12,128]{2,1,0:T(8,128)S(1)} %collective-permute-done.2.near_ref, ...), custom_call_target="tpu_custom_call" | custom-call | tf_op jit(solution)/shard_map/pallas_call | solution.py:313
  75.1 22.1 %all_to_all.22 = f32[64,16,128]{2,1,0:T(8,128)S(1)} all-to-all(f32[64,16,128]{2,1,0:T(8,128)S(1)} %get-tuple-element.22), channel_id=1, replica_groups=mesh['energy'=64,'tile'=4] {'energy'}, dimensions={0} | all-to-all | bytes 1048576 | tf_op jit(solution)/shard_map/all_to_all | solution.py:378
  97.2 4.9 %shard_map.77 = f32[32,32,128]{2,1,0:T(8,128)S(1)} custom-call(f32[32,32,128]{2,1,0:T(8,128)S(1)} %bitcast.24, s32[2,32]{1,0:T(2,128)} %bitcast.38, f32[32,128,128]{2,1,0:T(8,128)S(1)} %bitcast.23, f32[128,256]{1,0:T(8,128)S(1)} %bitcast.30, bf16[256,256]{1,0:T(8,128)(2,1)S(1)} %copy-done.3, bf16[256,256]{1,0:T(8,128)(2,1)S(1)} %copy-done.2), custom_call_target="tpu_custom_call" | custom-call | tf_op jit(solution)/shard_map/pallas_call | solution.py:184
  102.1 22.6 %all_to_all.23.grads_ref = f32[64,16,128]{2,1,0:T(8,128)S(1)} all-to-all(f32[64,16,128]{2,1,0:T(8,128)S(1)} %bitcast.25), channel_id=1, replica_groups=mesh['energy'=64,'tile'=4] {'energy'}, dimensions={0} | all-to-all | bytes 1048576 | tf_op jit(solution)/shard_map/all_to_all | solution.py:380
  124.7 1.1 shard_map.78
  125.8 0.1 collective-permute-start.4
  125.9 2.4 %collective-permute-start.5 = (f32[8,4,128]{2,1,0:T(4,128)S(1)}, f32[8,4,128]{2,1,0:T(4,128)S(1)}, u32[]{:S(2)}, u32[]{:S(2)}) collective-permute-start(f32[8,4,128]{2,1,0:T(4,128)S(1)} %get-tuple-element.26), channel_id=1, source_target_pairs={{1,2},{2,1},{3,0},{0,3},{5,6},{6,5},{7,4},{4,7},{9,10},{10,9},{11,... | collective-permute-start | bytes 49160 | tf_op jit(solution)/shard_map/ppermute | solution.py:332
  128.3 0.0 collective-permute-done.4
  128.3 2.4 %collective-permute-done.5 = f32[8,4,128]{2,1,0:T(4,128)S(1)} collective-permute-done((f32[8,4,128]{2,1,0:T(4,128)S(1)}, f32[8,4,128]{2,1,0:T(4,128)S(1)}, u32[]{:S(2)}, u32[]{:S(2)}) %collective-permute-start.5) | collective-permute-done | bytes 16416 | tf_op jit(solution)/shard_map/ppermute | solution.py:332
  130.7 3.8 %collective-permute-start.7 = (f32[8,12,128]{2,1,0:T(8,128)S(1)}, f32[8,12,128]{2,1,0:T(8,128)S(1)}, u32[]{:S(2)}, u32[]{:S(2)}) collective-permute-start(f32[8,12,128]{2,1,0:T(8,128)S(1)} %pad_maximum_fusion.1.mine_ref), channel_id=1, source_target_pairs={{4,8},{8,4},{12,16},{16,12},{20,24},{24,20},{28,32},{32,28},{36,40... | collective-permute-start | bytes 147464 | tf_op jit(solution)/shard_map/ppermute | solution.py:339
  134.5 0.0 collective-permute-start.6
  134.5 4.9 %collective-permute-done.7.far_ref = f32[8,12,128]{2,1,0:T(8,128)S(1)} collective-permute-done((f32[8,12,128]{2,1,0:T(8,128)S(1)}, f32[8,12,128]{2,1,0:T(8,128)S(1)}, u32[]{:S(2)}, u32[]{:S(2)}) %collective-permute-start.7) | collective-permute-done | bytes 49184 | tf_op jit(solution)/shard_map/ppermute | solution.py:339
  139.4 0.0 collective-permute-done.6.near_ref
  139.4 1.7 %shard_map.79 = f32[8,4,256]{2,1,0:T(4,128)} custom-call(s32[2]{0:T(128)S(1)} %pad_add_fusion.place, f32[8,12,128]{2,1,0:T(8,128)S(1)} %pad_maximum_fusion.1.mine_ref, f32[8,12,128]{2,1,0:T(8,128)S(1)} %collective-permute-done.6.near_ref, f32[8,12,128]{2,1,0:T(8,128)S(1)} %collective-permute-done.7.far_ref), custom_call_target="tpu_custom_call" | custom-call | tf_op jit(solution)/shard_map/pallas_call | solution.py:313
  (5 shorter events, 0.0 us)
Async XLA Ops:
  0.0 30.6 %copy-start.2 = (bf16[256,256]{1,0:T(8,128)(2,1)S(1)}, bf16[256,256]{1,0:T(8,128)(2,1)}, u32[]{:S(2)}) copy-start(bf16[256,256]{1,0:T(8,128)(2,1)} %constant.30.clone.rest_3_.back_ref) | copy-start | bytes 393220
  0.0 30.6 %copy-start.3 = (bf16[256,256]{1,0:T(8,128)(2,1)S(1)}, bf16[256,256]{1,0:T(8,128)(2,1)}, u32[]{:S(2)}) copy-start(bf16[256,256]{1,0:T(8,128)(2,1)} %constant.29.clone.rest_2_.ahead_ref) | copy-start | bytes 393220
  0.0 30.6 %copy-start = (f32[1,1,32,128,128]{4,3,2,1,0:T(8,128)S(1)}, f32[1,1,32,128,128]{4,3,2,1,0:T(8,128)}, u32[]{:S(2)}) copy-start(f32[1,1,32,128,128]{4,3,2,1,0:T(8,128)} %param.11) | copy-start | bytes 6291460
  0.0 30.6 %copy-start.1 = (f32[1,128,256]{2,1,0:T(8,128)S(1)}, f32[1,128,256]{2,1,0:T(8,128)}, u32[]{:S(2)}) copy-start(f32[1,128,256]{2,1,0:T(8,128)} %param.9) | copy-start | bytes 393220
  30.7 28.1 %copy-start.4 = (f32[2,4,4,256]{3,2,1,0:T(4,128)S(1)}, f32[2,4,4,256]{3,2,1,0:T(4,128)}, u32[]{:S(2)}) copy-start(f32[2,4,4,256]{3,2,1,0:T(4,128)} %param.7) | copy-start | bytes 98308
  30.7 28.1 %copy-start.5 = (f32[64,4,2]{0,2,1:T(2,128)S(1)}, f32[64,4,2]{0,2,1:T(2,128)}, u32[]{:S(2)}) copy-start(f32[64,4,2]{0,2,1:T(2,128)} %param.8) | copy-start | bytes 6148
  59.9 2.5 %collective-permute-start = (f32[8,4,128]{2,1,0:T(4,128)S(1)}, f32[8,4,128]{2,1,0:T(4,128)S(1)}, u32[]{:S(2)}, u32[]{:S(2)}) collective-permute-start(f32[8,4,128]{2,1,0:T(4,128)S(1)} %get-tuple-element.20), channel_id=1, source_target_pairs={{0,1},{1,0},{2,3},{3,2},{4,5},{5,4},{6,7},{7,6},{8,9},{9,8},{10,11... | collective-permute-start | bytes 49160 | tf_op jit(solution)/shard_map/ppermute | solution.py:331
  60.0 4.8 %collective-permute-start.1 = (f32[8,4,128]{2,1,0:T(4,128)S(1)}, f32[8,4,128]{2,1,0:T(4,128)S(1)}, u32[]{:S(2)}, u32[]{:S(2)}) collective-permute-start(f32[8,4,128]{2,1,0:T(4,128)S(1)} %get-tuple-element.21), channel_id=1, source_target_pairs={{1,2},{2,1},{3,0},{0,3},{5,6},{6,5},{7,4},{4,7},{9,10},{10,9},{11,... | collective-permute-start | bytes 49160 | tf_op jit(solution)/shard_map/ppermute | solution.py:332
  64.7 8.7 %collective-permute-start.3 = (f32[8,12,128]{2,1,0:T(8,128)S(1)}, f32[8,12,128]{2,1,0:T(8,128)S(1)}, u32[]{:S(2)}, u32[]{:S(2)}) collective-permute-start(f32[8,12,128]{2,1,0:T(8,128)S(1)} %pad_maximum_fusion.mine_ref), channel_id=1, source_target_pairs={{4,8},{8,4},{12,16},{16,12},{20,24},{24,20},{28,32},{32,28},{36,40... | collective-permute-start | bytes 147464 | tf_op jit(solution)/shard_map/ppermute | solution.py:339
  68.6 4.9 %collective-permute-start.2 = (f32[8,12,128]{2,1,0:T(8,128)S(1)}, f32[8,12,128]{2,1,0:T(8,128)S(1)}, u32[]{:S(2)}, u32[]{:S(2)}) collective-permute-start(f32[8,12,128]{2,1,0:T(8,128)S(1)} %pad_maximum_fusion.mine_ref), channel_id=1, source_target_pairs={{0,4},{4,0},{8,12},{12,8},{16,20},{20,16},{24,28},{28,24},{32,36},... | collective-permute-start | bytes 147464 | tf_op jit(solution)/shard_map/ppermute | solution.py:339
  125.8 2.5 %collective-permute-start.4 = (f32[8,4,128]{2,1,0:T(4,128)S(1)}, f32[8,4,128]{2,1,0:T(4,128)S(1)}, u32[]{:S(2)}, u32[]{:S(2)}) collective-permute-start(f32[8,4,128]{2,1,0:T(4,128)S(1)} %get-tuple-element.25), channel_id=1, source_target_pairs={{0,1},{1,0},{2,3},{3,2},{4,5},{5,4},{6,7},{7,6},{8,9},{9,8},{10,11... | collective-permute-start | bytes 49160 | tf_op jit(solution)/shard_map/ppermute | solution.py:331
  125.9 4.8 %collective-permute-start.5 = (f32[8,4,128]{2,1,0:T(4,128)S(1)}, f32[8,4,128]{2,1,0:T(4,128)S(1)}, u32[]{:S(2)}, u32[]{:S(2)}) collective-permute-start(f32[8,4,128]{2,1,0:T(4,128)S(1)} %get-tuple-element.26), channel_id=1, source_target_pairs={{1,2},{2,1},{3,0},{0,3},{5,6},{6,5},{7,4},{4,7},{9,10},{10,9},{11,... | collective-permute-start | bytes 49160 | tf_op jit(solution)/shard_map/ppermute | solution.py:332
  130.7 8.7 %collective-permute-start.7 = (f32[8,12,128]{2,1,0:T(8,128)S(1)}, f32[8,12,128]{2,1,0:T(8,128)S(1)}, u32[]{:S(2)}, u32[]{:S(2)}) collective-permute-start(f32[8,12,128]{2,1,0:T(8,128)S(1)} %pad_maximum_fusion.1.mine_ref), channel_id=1, source_target_pairs={{4,8},{8,4},{12,16},{16,12},{20,24},{24,20},{28,32},{32,28},{36,40... | collective-permute-start | bytes 147464 | tf_op jit(solution)/shard_map/ppermute | solution.py:339
  134.5 4.9 %collective-permute-start.6 = (f32[8,12,128]{2,1,0:T(8,128)S(1)}, f32[8,12,128]{2,1,0:T(8,128)S(1)}, u32[]{:S(2)}, u32[]{:S(2)}) collective-permute-start(f32[8,12,128]{2,1,0:T(8,128)S(1)} %pad_maximum_fusion.1.mine_ref), channel_id=1, source_target_pairs={{0,4},{4,0},{8,12},{12,8},{16,20},{20,16},{24,28},{28,24},{32,36},... | collective-permute-start | bytes 147464 | tf_op jit(solution)/shard_map/ppermute | solution.py:339

commit v6 on v5

--- a/solution.py
+++ b/solution.py
@@ -230,7 +230,7 @@
     mixed([rows_ref[p] for p in range(rows_ref.shape[0])], spectra, out_ref)
 
 
-def unmix_kernel(factor, place, spectra, grads_ref, rows_ref, out_ref, near_ref, far_ref):
+def unmix_kernel(factor, place, spectra, grads_ref, rows_ref, out_ref, far_ref, near_ref):
     materials = rows_ref.shape[0] // 2
 
     def one(e, sums):
@@ -255,16 +255,18 @@
 
 
 def smooth(place, last, mine_ref, near_ref, far_ref, field):
-    planes = mine_ref.shape[0]
+    planes = field.shape[0]
     even = place[0] % 2 == 0
-    for j in range(3):
-        lanes = slice(j * LEN, (j + 1) * LEN)
-        near = near_ref[:, 4 * j : 4 * j + 4, :]
-        far = far_ref[:, 4 * j : 4 * j + 4, :]
-        field[:, 0:4, lanes] = jnp.where(even, far, near)
-        field[:, 4:8, lanes] = mine_ref[:, 4 * j : 4 * j + 4, :]
-        field[:, 8:12, lanes] = jnp.where(even, near, far)
-        field[:, 12:16, lanes] = jnp.zeros((planes, 4, LEN), jnp.float32)
+    for p in range(planes):
+        for j in range(3):
+            rows = slice(8 * p + 4 * j, 8 * p + 4 * j + 4) if j < 2 else slice(8 * planes + 4 * p, 8 * planes + 4 * p + 4)
+            lanes = slice(j * LEN, (j + 1) * LEN)
+            near = near_ref[rows, :]
+            far = far_ref[rows, :]
+            field[p, 0:4, lanes] = jnp.where(even, far, near)
+            field[p, 4:8, lanes] = mine_ref[rows, :]
+            field[p, 8:12, lanes] = jnp.where(even, near, far)
+            field[p, 12:16, lanes] = jnp.zeros((4, LEN), jnp.float32)
     shape = (16, 3 * LEN)
     row = lax.broadcasted_iota(jnp.int32, shape, 0)
     lane = lax.broadcasted_iota(jnp.int32, shape, 1)
@@ -328,10 +330,11 @@
 
 def with_edges(rows, to_near, to_far, even):
     near, far = swaps("tile")
+    from_far = lax.ppermute(to_far, "tile", far)
     from_near = lax.ppermute(to_near, "tile", near)
-    from_far = lax.ppermute(to_far, "tile", far)
     lane = lax.broadcasted_iota(jnp.int32, from_near.shape, 2)
-    return jnp.concatenate([rows, jnp.where((lane < LEN // 2) == even, from_near, from_far)], 1)
+    edges = jnp.where((lane < LEN // 2) != even, from_far, from_near)
+    return jnp.concatenate([rows.reshape(-1, LEN), edges.reshape(-1, LEN)], 0)
 
 
 def from_neighbours(strip):
@@ -378,7 +381,7 @@
         tile = lax.all_to_all(mixes, "energy", split_axis=0, concat_axis=0, tiled=True)
         grads = patch_gradient(tile, probe, spots, counts, tables)
         grads = lax.all_to_all(grads, "energy", split_axis=0, concat_axis=0, tiled=True)
-        current, to_near, to_far = on_chip(
+        current, to_far, to_near = on_chip(
             functools.partial(unmix_kernel, factor), (strip, part, part), (place, weights), (grads, current)
         )
         mine = with_edges(current, to_near, to_far, even)

time: 143 us -> 140 us (0.979)
  starting transfers between devices: 12.6 us -> 10.6 us
    ppermute x2, starting transfers between devices: 4.78 us -> 0.19 us  [with_edges(): from_far = lax.ppermute(to_far, 'tile', far)]
    ppermute x2, starting transfers between devices: 0.19 us -> 2.51 us  [with_edges(): from_near = lax.ppermute(to_near, 'tile', near)]
    ppermute x2, waiting for transfers between devices: 4.71 us -> 6.78 us  [with_edges(): from_far = lax.ppermute(to_far, 'tile', far)]
where the time goes in v6:
time: 140 us; the launch traced here: 139 us
  blocking collectives  95.7 us (68%)
  Pallas kernels  16.9 us (12%)
  waiting for transfers between devices  15.7 us (11%)
  starting transfers between devices  10.6 us (8%)
    all_to_all x2, blocking collectives, shards(): lax.all_to_all(mixes, 'energy', split_axis=0, concat_axis=0, tiled=True)  50.9 us
    all_to_all x2, blocking collectives, shards(): lax.all_to_all(grads, 'energy', split_axis=0, concat_axis=0, tiled=True)  44.8 us
    pallas_call x2, Pallas kernels, patch_gradient(): pl.pallas_call(functools.partial(patch_kernel, group), out_shape=jax.Shap...  9.89 us
    ppermute x2, waiting for transfers between devices, from_neighbours(): lax.ppermute(strip, 'energy', far)  8.87 us
    ppermute x2, starting transfers between devices, from_neighbours(): lax.ppermute(strip, 'energy', far)  7.92 us
    ppermute x2, waiting for transfers between devices, with_edges(): from_far = lax.ppermute(to_far, 'tile', far)  6.78 us
    pallas_call x4, Pallas kernels, on_chip(): pl.pallas_call(kernel, out_shape=out_shape, in_specs=[smem] * len(scalars...  5.62 us
  transfers between devices with their start and end apart: 8, of which 4 were waited for; matrix products, arithmetic and copies ran while one was open for 0% of the time, Pallas kernels for 0%

profile of v6, /device:TPU:8, one launch (start us, length us, event | category | flops | bytes accessed | tf_op | source)
XLA Modules:
  0.0 139.2 jit_solution(11188111339160139177)
XLA Ops:
  0.0 0.0 copy-start.2
  0.0 0.0 copy-start.3
  0.0 0.0 copy-start
  0.0 0.0 copy-start.1
  0.0 0.1 pad_add_fusion.place
  0.1 1.4 %shard_map.73 = f32[64,16,128]{2,1,0:T(8,128)S(1)} custom-call(f32[8,64]{1,0:T(8,128)} %bitcast.37, f32[8,4,256]{2,1,0:T(4,128)} %bitcast.35, f32[32,128,128]{2,1,0:T(8,128)} %bitcast.25, f32[128,256]{1,0:T(8,128)} %bitcast.32, bf16[256,256]{1,0:T(8,128)(2,1)} %constant.29.clone.rest_2_.ahead_ref, bf16[256,256]{1,0:T(8,128)(2,1)} %constant.30.clone.rest_3_.back_ref), custom_call_target="tpu_custom_call" | custom-call | tf_op jit(solution)/shard_map/pallas_call | solution.py:367
  1.5 29.1 %all_to_all.20 = f32[64,16,128]{2,1,0:T(8,128)S(1)} all-to-all(f32[64,16,128]{2,1,0:T(8,128)S(1)} %shard_map.73), channel_id=1, replica_groups=mesh['energy'=64,'tile'=4] {'energy'}, dimensions={0} | all-to-all | bytes 1048576 | tf_op jit(solution)/shard_map/all_to_all | solution.py:381
  30.6 0.0 copy-done.2
  30.6 0.0 copy-done.3
  30.6 0.0 copy-done
  30.6 0.0 copy-done.1
  30.7 0.0 copy-start.4
  30.7 0.0 copy-start.5
  30.7 5.0 %shard_map.74 = f32[32,32,128]{2,1,0:T(8,128)S(1)} custom-call(f32[32,32,128]{2,1,0:T(8,128)S(1)} %bitcast.30, s32[2,32]{1,0:T(2,128)} %bitcast.45, f32[32,128,128]{2,1,0:T(8,128)S(1)} %bitcast.26, f32[128,256]{1,0:T(8,128)S(1)} %bitcast.33, bf16[256,256]{1,0:T(8,128)(2,1)S(1)} %copy-done.3, bf16[256,256]{1,0:T(8,128)(2,1)S(1)} %copy-done.2), custom_call_target="tpu_custom_call" | custom-call | tf_op jit(solution)/shard_map/pallas_call | solution.py:184
  35.7 23.0 %all_to_all.21.grads_ref = f32[64,16,128]{2,1,0:T(8,128)S(1)} all-to-all(f32[64,16,128]{2,1,0:T(8,128)S(1)} %bitcast.31), channel_id=1, replica_groups=mesh['energy'=64,'tile'=4] {'energy'}, dimensions={0} | all-to-all | bytes 1048576 | tf_op jit(solution)/shard_map/all_to_all | solution.py:383
  58.7 0.0 copy-done.4
  58.7 0.0 copy-done.5
  58.7 1.1 shard_map.75
  59.8 0.1 collective-permute-start
  59.9 2.4 %collective-permute-start.1 = (f32[8,4,128]{2,1,0:T(4,128)S(1)}, f32[8,4,128]{2,1,0:T(4,128)S(1)}, u32[]{:S(2)}, u32[]{:S(2)}) collective-permute-start(f32[8,4,128]{2,1,0:T(4,128)S(1)} %get-tuple-element.21), channel_id=1, source_target_pairs={{0,1},{1,0},{2,3},{3,2},{4,5},{5,4},{6,7},{7,6},{8,9},{9,8},{10,11... | collective-permute-start | bytes 49160 | tf_op jit(solution)/shard_map/ppermute | solution.py:334
  62.3 2.2 %collective-permute-done = f32[8,4,128]{2,1,0:T(4,128)S(1)} collective-permute-done((f32[8,4,128]{2,1,0:T(4,128)S(1)}, f32[8,4,128]{2,1,0:T(4,128)S(1)}, u32[]{:S(2)}, u32[]{:S(2)}) %collective-permute-start) | collective-permute-done | bytes 16416 | tf_op jit(solution)/shard_map/ppermute | solution.py:333
  64.6 0.0 collective-permute-done.1
  64.6 4.0 %collective-permute-start.3 = (f32[96,128]{1,0:T(8,128)S(1)}, f32[96,128]{1,0:T(8,128)S(1)}, u32[]{:S(2)}, u32[]{:S(2)}) collective-permute-start(f32[96,128]{1,0:T(8,128)S(1)} %pad_maximum_fusion.mine_ref), channel_id=1, source_target_pairs={{4,8},{8,4},{12,16},{16,12},{20,24},{24,20},{28,32},{32,28},{36,40... | collective-permute-start | bytes 147464 | tf_op jit(solution)/shard_map/ppermute | solution.py:342
  68.6 0.0 collective-permute-start.2
  68.6 4.4 %collective-permute-done.3.far_ref = f32[96,128]{1,0:T(8,128)S(1)} collective-permute-done((f32[96,128]{1,0:T(8,128)S(1)}, f32[96,128]{1,0:T(8,128)S(1)}, u32[]{:S(2)}, u32[]{:S(2)}) %collective-permute-start.3) | collective-permute-done | bytes 49184 | tf_op jit(solution)/shard_map/ppermute | solution.py:342
  73.0 0.0 collective-permute-done.2.near_ref
  73.0 1.7 %shard_map.76 = (f32[8,8,128]{2,1,0:T(8,128)S(1)}, f32[64,16,128]{2,1,0:T(8,128)S(1)}) custom-call(s32[2]{0:T(128)S(1)} %pad_add_fusion.place, f32[8,64]{1,0:T(8,128)S(1)} %bitcast.39, f32[96,128]{1,0:T(8,128)S(1)} %pad_maximum_fusion.mine_ref, f32[96,128]{1,0:T(8,128)S(1)} %collective-permute-done.2.near_ref, f32[96,128]{1,0:T(8,128)S(1)} %collective-permute-done.3.far_ref), custom_call_target="tpu_custom_call" | custom-call | tf_op jit(solution)/shard_map/pallas_call | solution.py:315
  74.7 21.8 %all_to_all.22 = f32[64,16,128]{2,1,0:T(8,128)S(1)} all-to-all(f32[64,16,128]{2,1,0:T(8,128)S(1)} %get-tuple-element.22), channel_id=1, replica_groups=mesh['energy'=64,'tile'=4] {'energy'}, dimensions={0} | all-to-all | bytes 1048576 | tf_op jit(solution)/shard_map/all_to_all | solution.py:381
  96.5 4.9 %shard_map.77 = f32[32,32,128]{2,1,0:T(8,128)S(1)} custom-call(f32[32,32,128]{2,1,0:T(8,128)S(1)} %bitcast.28, s32[2,32]{1,0:T(2,128)} %bitcast.46, f32[32,128,128]{2,1,0:T(8,128)S(1)} %bitcast.27, f32[128,256]{1,0:T(8,128)S(1)} %bitcast.34, bf16[256,256]{1,0:T(8,128)(2,1)S(1)} %copy-done.3, bf16[256,256]{1,0:T(8,128)(2,1)S(1)} %copy-done.2), custom_call_target="tpu_custom_call" | custom-call | tf_op jit(solution)/shard_map/pallas_call | solution.py:184
  101.4 21.8 %all_to_all.23.grads_ref = f32[64,16,128]{2,1,0:T(8,128)S(1)} all-to-all(f32[64,16,128]{2,1,0:T(8,128)S(1)} %bitcast.29), channel_id=1, replica_groups=mesh['energy'=64,'tile'=4] {'energy'}, dimensions={0} | all-to-all | bytes 1048576 | tf_op jit(solution)/shard_map/all_to_all | solution.py:383
  123.2 1.1 shard_map.78
  124.3 0.1 collective-permute-start.4
  124.4 0.1 collective-permute-start.5
  124.5 4.6 %collective-permute-done.4 = f32[8,4,128]{2,1,0:T(4,128)S(1)} collective-permute-done((f32[8,4,128]{2,1,0:T(4,128)S(1)}, f32[8,4,128]{2,1,0:T(4,128)S(1)}, u32[]{:S(2)}, u32[]{:S(2)}) %collective-permute-start.4) | collective-permute-done | bytes 16416 | tf_op jit(solution)/shard_map/ppermute | solution.py:333
  129.1 0.0 collective-permute-done.5
  129.1 3.9 %collective-permute-start.7 = (f32[96,128]{1,0:T(8,128)S(1)}, f32[96,128]{1,0:T(8,128)S(1)}, u32[]{:S(2)}, u32[]{:S(2)}) collective-permute-start(f32[96,128]{1,0:T(8,128)S(1)} %pad_maximum_fusion.1.mine_ref), channel_id=1, source_target_pairs={{4,8},{8,4},{12,16},{16,12},{20,24},{24,20},{28,32},{32,28},{36,40... | collective-permute-start | bytes 147464 | tf_op jit(solution)/shard_map/ppermute | solution.py:342
  133.0 0.0 collective-permute-start.6
  133.0 4.5 %collective-permute-done.7.far_ref = f32[96,128]{1,0:T(8,128)S(1)} collective-permute-done((f32[96,128]{1,0:T(8,128)S(1)}, f32[96,128]{1,0:T(8,128)S(1)}, u32[]{:S(2)}, u32[]{:S(2)}) %collective-permute-start.7) | collective-permute-done | bytes 49184 | tf_op jit(solution)/shard_map/ppermute | solution.py:342
  137.5 0.0 collective-permute-done.6.near_ref
  137.5 1.7 %shard_map.79 = f32[8,4,256]{2,1,0:T(4,128)} custom-call(s32[2]{0:T(128)S(1)} %pad_add_fusion.place, f32[96,128]{1,0:T(8,128)S(1)} %pad_maximum_fusion.1.mine_ref, f32[96,128]{1,0:T(8,128)S(1)} %collective-permute-done.6.near_ref, f32[96,128]{1,0:T(8,128)S(1)} %collective-permute-done.7.far_ref), custom_call_target="tpu_custom_call" | custom-call | tf_op jit(solution)/shard_map/pallas_call | solution.py:315
  (5 shorter events, 0.0 us)
Async XLA Ops:
  0.0 30.6 %copy-start.2 = (bf16[256,256]{1,0:T(8,128)(2,1)S(1)}, bf16[256,256]{1,0:T(8,128)(2,1)}, u32[]{:S(2)}) copy-start(bf16[256,256]{1,0:T(8,128)(2,1)} %constant.30.clone.rest_3_.back_ref) | copy-start | bytes 393220
  0.0 30.6 %copy-start.3 = (bf16[256,256]{1,0:T(8,128)(2,1)S(1)}, bf16[256,256]{1,0:T(8,128)(2,1)}, u32[]{:S(2)}) copy-start(bf16[256,256]{1,0:T(8,128)(2,1)} %constant.29.clone.rest_2_.ahead_ref) | copy-start | bytes 393220
  0.0 30.6 %copy-start = (f32[1,1,32,128,128]{4,3,2,1,0:T(8,128)S(1)}, f32[1,1,32,128,128]{4,3,2,1,0:T(8,128)}, u32[]{:S(2)}) copy-start(f32[1,1,32,128,128]{4,3,2,1,0:T(8,128)} %param.11) | copy-start | bytes 6291460
  0.0 30.6 %copy-start.1 = (f32[1,128,256]{2,1,0:T(8,128)S(1)}, f32[1,128,256]{2,1,0:T(8,128)}, u32[]{:S(2)}) copy-start(f32[1,128,256]{2,1,0:T(8,128)} %param.9) | copy-start | bytes 393220
  30.7 28.0 %copy-start.4 = (f32[2,4,4,256]{3,2,1,0:T(4,128)S(1)}, f32[2,4,4,256]{3,2,1,0:T(4,128)}, u32[]{:S(2)}) copy-start(f32[2,4,4,256]{3,2,1,0:T(4,128)} %param.7) | copy-start | bytes 98308
  30.7 28.0 %copy-start.5 = (f32[64,4,2]{0,2,1:T(2,128)S(1)}, f32[64,4,2]{0,2,1:T(2,128)}, u32[]{:S(2)}) copy-start(f32[64,4,2]{0,2,1:T(2,128)} %param.8) | copy-start | bytes 6148
  59.8 4.8 %collective-permute-start = (f32[8,4,128]{2,1,0:T(4,128)S(1)}, f32[8,4,128]{2,1,0:T(4,128)S(1)}, u32[]{:S(2)}, u32[]{:S(2)}) collective-permute-start(f32[8,4,128]{2,1,0:T(4,128)S(1)} %get-tuple-element.20), channel_id=1, source_target_pairs={{1,2},{2,1},{3,0},{0,3},{5,6},{6,5},{7,4},{4,7},{9,10},{10,9},{11,... | collective-permute-start | bytes 49160 | tf_op jit(solution)/shard_map/ppermute | solution.py:333
  59.9 4.7 %collective-permute-start.1 = (f32[8,4,128]{2,1,0:T(4,128)S(1)}, f32[8,4,128]{2,1,0:T(4,128)S(1)}, u32[]{:S(2)}, u32[]{:S(2)}) collective-permute-start(f32[8,4,128]{2,1,0:T(4,128)S(1)} %get-tuple-element.21), channel_id=1, source_target_pairs={{0,1},{1,0},{2,3},{3,2},{4,5},{5,4},{6,7},{7,6},{8,9},{9,8},{10,11... | collective-permute-start | bytes 49160 | tf_op jit(solution)/shard_map/ppermute | solution.py:334
  64.6 8.4 %collective-permute-start.3 = (f32[96,128]{1,0:T(8,128)S(1)}, f32[96,128]{1,0:T(8,128)S(1)}, u32[]{:S(2)}, u32[]{:S(2)}) collective-permute-start(f32[96,128]{1,0:T(8,128)S(1)} %pad_maximum_fusion.mine_ref), channel_id=1, source_target_pairs={{4,8},{8,4},{12,16},{16,12},{20,24},{24,20},{28,32},{32,28},{36,40... | collective-permute-start | bytes 147464 | tf_op jit(solution)/shard_map/ppermute | solution.py:342
  68.6 4.4 %collective-permute-start.2 = (f32[96,128]{1,0:T(8,128)S(1)}, f32[96,128]{1,0:T(8,128)S(1)}, u32[]{:S(2)}, u32[]{:S(2)}) collective-permute-start(f32[96,128]{1,0:T(8,128)S(1)} %pad_maximum_fusion.mine_ref), channel_id=1, source_target_pairs={{0,4},{4,0},{8,12},{12,8},{16,20},{20,16},{24,28},{28,24},{32,36},... | collective-permute-start | bytes 147464 | tf_op jit(solution)/shard_map/ppermute | solution.py:342
  124.3 4.8 %collective-permute-start.4 = (f32[8,4,128]{2,1,0:T(4,128)S(1)}, f32[8,4,128]{2,1,0:T(4,128)S(1)}, u32[]{:S(2)}, u32[]{:S(2)}) collective-permute-start(f32[8,4,128]{2,1,0:T(4,128)S(1)} %get-tuple-element.25), channel_id=1, source_target_pairs={{1,2},{2,1},{3,0},{0,3},{5,6},{6,5},{7,4},{4,7},{9,10},{10,9},{11,... | collective-permute-start | bytes 49160 | tf_op jit(solution)/shard_map/ppermute | solution.py:333
  124.4 4.7 %collective-permute-start.5 = (f32[8,4,128]{2,1,0:T(4,128)S(1)}, f32[8,4,128]{2,1,0:T(4,128)S(1)}, u32[]{:S(2)}, u32[]{:S(2)}) collective-permute-start(f32[8,4,128]{2,1,0:T(4,128)S(1)} %get-tuple-element.26), channel_id=1, source_target_pairs={{0,1},{1,0},{2,3},{3,2},{4,5},{5,4},{6,7},{7,6},{8,9},{9,8},{10,11... | collective-permute-start | bytes 49160 | tf_op jit(solution)/shard_map/ppermute | solution.py:334
  129.1 8.4 %collective-permute-start.7 = (f32[96,128]{1,0:T(8,128)S(1)}, f32[96,128]{1,0:T(8,128)S(1)}, u32[]{:S(2)}, u32[]{:S(2)}) collective-permute-start(f32[96,128]{1,0:T(8,128)S(1)} %pad_maximum_fusion.1.mine_ref), channel_id=1, source_target_pairs={{4,8},{8,4},{12,16},{16,12},{20,24},{24,20},{28,32},{32,28},{36,40... | collective-permute-start | bytes 147464 | tf_op jit(solution)/shard_map/ppermute | solution.py:342
  133.0 4.5 %collective-permute-start.6 = (f32[96,128]{1,0:T(8,128)S(1)}, f32[96,128]{1,0:T(8,128)S(1)}, u32[]{:S(2)}, u32[]{:S(2)}) collective-permute-start(f32[96,128]{1,0:T(8,128)S(1)} %pad_maximum_fusion.1.mine_ref), channel_id=1, source_target_pairs={{0,4},{4,0},{8,12},{12,8},{16,20},{20,16},{24,28},{28,24},{32,36},... | collective-permute-start | bytes 147464 | tf_op jit(solution)/shard_map/ppermute | solution.py:342

commit v7 on v6

--- a/solution.py
+++ b/solution.py
@@ -197,15 +197,15 @@
     return out.reshape(z.shape)
 
 
-def mixed(planes, spectra, out_ref):
+def mixed(planes, coefficient, out_ref):
     materials = len(planes) // 2
 
     def one(e, carry):
         re = jnp.zeros_like(planes[0])
         im = jnp.zeros_like(planes[0])
         for m in range(materials):
-            cr = spectra[2 * m, e]
-            ci = spectra[2 * m + 1, e]
+            cr = coefficient(2 * m, e)
+            ci = coefficient(2 * m + 1, e)
             re = re + cr * planes[m] - ci * planes[materials + m]
             im = im + cr * planes[materials + m] + ci * planes[m]
         out_ref[e, 0:8, :] = re
@@ -227,10 +227,10 @@
         copy.wait()
     for half in range(2):
         rows_ref[:, 4 * half : 4 * half + 4, :] = maps[:, :, half * LEN : (half + 1) * LEN]
-    mixed([rows_ref[p] for p in range(rows_ref.shape[0])], spectra, out_ref)
-
-
-def unmix_kernel(factor, place, spectra, grads_ref, rows_ref, out_ref, far_ref, near_ref):
+    mixed([rows_ref[p] for p in range(rows_ref.shape[0])], lambda k, e: spectra[k, e], out_ref)
+
+
+def unmix_kernel(factor, grads_ref, rows_ref, spectra, out_ref, far_ref, near_ref):
     materials = rows_ref.shape[0] // 2
 
     def one(e, sums):
@@ -238,13 +238,13 @@
         gi = grads_ref[e, 8:16, :]
         reals, imags = [], []
         for m in range(materials):
-            cr = spectra[2 * m, e]
-            ci = spectra[2 * m + 1, e]
+            cr = spectra[2 * m, pl.ds(e, 1), :]
+            ci = spectra[2 * m + 1, pl.ds(e, 1), :]
             reals.append(sums[m] + cr * gr + ci * gi)
             imags.append(sums[materials + m] + cr * gi - ci * gr)
         return tuple(reals + imags)
 
-    even = place[1] % 2 == 0
+    even = lax.axis_index("tile") % 2 == 0
     zero = jnp.zeros(rows_ref.shape[1:], jnp.float32)
     sums = lax.fori_loop(0, grads_ref.shape[0], one, (zero,) * (2 * materials), unroll=8)
     for p in range(2 * materials):
@@ -254,8 +254,9 @@
         far_ref[p] = jnp.where(even, value[:4], value[4:])
 
 
-def smooth(place, last, mine_ref, near_ref, far_ref, field):
+def smooth(last, mine_ref, near_ref, far_ref, field):
     planes = field.shape[0]
+    place = (lax.axis_index("energy"), lax.axis_index("tile"))
     even = place[0] % 2 == 0
     for p in range(planes):
         for j in range(3):
@@ -295,31 +296,30 @@
     return results
 
 
-def smooth_mix_kernel(last, place, spectra, mine_ref, near_ref, far_ref, rows_ref, out_ref, field):
-    results = smooth(place, last, mine_ref, near_ref, far_ref, field)
+def smooth_mix_kernel(last, mine_ref, near_ref, far_ref, spectra, rows_ref, out_ref, field):
+    results = smooth(last, mine_ref, near_ref, far_ref, field)
     for p, value in enumerate(results):
         rows_ref[p, 0:4, :] = value[4:8, :LEN]
         rows_ref[p, 4:8, :] = value[4:8, LEN : 2 * LEN]
-    mixed([rows_ref[p] for p in range(rows_ref.shape[0])], spectra, out_ref)
-
-
-def smooth_kernel(last, place, mine_ref, near_ref, far_ref, out_ref, field):
-    results = smooth(place, last, mine_ref, near_ref, far_ref, field)
+    mixed([rows_ref[p] for p in range(rows_ref.shape[0])], lambda k, e: spectra[k, pl.ds(e, 1), :], out_ref)
+
+
+def smooth_kernel(last, mine_ref, near_ref, far_ref, out_ref, field):
+    results = smooth(last, mine_ref, near_ref, far_ref, field)
     for p, value in enumerate(results):
         out_ref[p] = value[4:8, : 2 * LEN]
 
 
-def on_chip(kernel, out_shape, scalars, arrays, scratch=()):
+def on_chip(kernel, out_shape, arrays, scratch=()):
     vmem = pl.BlockSpec(memory_space=pltpu.VMEM)
-    smem = pl.BlockSpec(memory_space=pltpu.SMEM)
     return pl.pallas_call(
         kernel,
         out_shape=out_shape,
-        in_specs=[smem] * len(scalars) + [vmem] * len(arrays),
+        in_specs=[vmem] * len(arrays),
         out_specs=jax.tree.map(lambda _: vmem, out_shape),
         scratch_shapes=list(scratch),
         compiler_params=pltpu.CompilerParams(vmem_limit_bytes=8 << 20),
-    )(*scalars, *arrays)
+    )(*arrays)
 
 
 def swaps(axis):
@@ -353,14 +353,16 @@
     tables = dft_blocks(*dft_tables(LEN))
     weights = spectra.transpose(1, 2, 0).reshape(2 * materials, energies)
     factor = DATA_STEP / math.sqrt(energies)
-    place = jnp.stack([lax.axis_index("energy"), lax.axis_index("tile")]).astype(jnp.int32)
+    spread_weights = jnp.broadcast_to(weights[:, :, None], (*weights.shape, LEN))
     last = (lax.axis_size("energy") - 1, lax.axis_size("tile") - 1)
     strip = jax.ShapeDtypeStruct((planes, 2 * rows, LEN), jnp.float32)
     part = jax.ShapeDtypeStruct((planes, rows, LEN), jnp.float32)
     spread = jax.ShapeDtypeStruct((energies, 4 * rows, LEN), jnp.float32)
     field = pltpu.VMEM((planes, 16, 3 * LEN), jnp.float32)
-    even = place[1] % 2 == 0
-    maps, place, even = lax.optimization_barrier((material_maps.reshape(planes, rows, columns), place, even))
+    even = lax.axis_index("tile") % 2 == 0
+    maps, even, spread_weights = lax.optimization_barrier(
+        (material_maps.reshape(planes, rows, columns), even, spread_weights)
+    )
     current = maps.reshape(planes, rows, 2, LEN).transpose(0, 2, 1, 3).reshape(planes, 2 * rows, LEN)
     hbm = pl.BlockSpec(memory_space=pltpu.HBM)
     later = (counts, probe, *tables)
@@ -382,16 +384,16 @@
         grads = patch_gradient(tile, probe, spots, counts, tables)
         grads = lax.all_to_all(grads, "energy", split_axis=0, concat_axis=0, tiled=True)
         current, to_far, to_near = on_chip(
-            functools.partial(unmix_kernel, factor), (strip, part, part), (place, weights), (grads, current)
+            functools.partial(unmix_kernel, factor), (strip, part, part), (grads, current, spread_weights)
         )
         mine = with_edges(current, to_near, to_far, even)
         near, far = from_neighbours(mine)
         if repeat < ITERS - 1:
             current, mixes = on_chip(
-                functools.partial(smooth_mix_kernel, last), (strip, spread), (place, weights), (mine, near, far), [field]
+                functools.partial(smooth_mix_kernel, last), (strip, spread), (mine, near, far, spread_weights), [field]
             )
     result = jax.ShapeDtypeStruct((planes, rows, columns), jnp.float32)
-    out = on_chip(functools.partial(smooth_kernel, last), result, (place,), (mine, near, far), [field])
+    out = on_chip(functools.partial(smooth_kernel, last), result, (mine, near, far), [field])
     return out.reshape(material_maps.shape)
 
 

time: 140 us -> 137 us (0.979)
  Pallas kernels: 16.9 us -> 14 us
    pallas_call x4, Pallas kernels: 5.62 us -> 2.7 us  [on_chip(): pl.pallas_call(kernel, out_shape=out_shape, in_specs=[vmem] * len(arrays)...]
where the time goes in v7:
time: 137 us
  blocking collectives  95.7 us (70%)
  waiting for transfers between devices  15.8 us (12%)
  Pallas kernels  14 us (10%)
  starting transfers between devices  10.5 us (8%)
    all_to_all x2, blocking collectives, shards(): lax.all_to_all(mixes, 'energy', split_axis=0, concat_axis=0, tiled=True)  50.9 us
    all_to_all x2, blocking collectives, shards(): lax.all_to_all(grads, 'energy', split_axis=0, concat_axis=0, tiled=True)  44.9 us
    pallas_call x2, Pallas kernels, patch_gradient(): pl.pallas_call(functools.partial(patch_kernel, group), out_shape=jax.Shap...  9.92 us
    ppermute x2, waiting for transfers between devices, from_neighbours(): lax.ppermute(strip, 'energy', far)  8.91 us
    ppermute x2, starting transfers between devices, from_neighbours(): lax.ppermute(strip, 'energy', far)  7.88 us
    ppermute x2, waiting for transfers between devices, with_edges(): from_far = lax.ppermute(to_far, 'tile', far)  6.84 us
  transfers between devices with their start and end apart: 8, of which 4 were waited for; matrix products, arithmetic and copies ran while one was open for 0% of the time, Pallas kernels for 0%

profile of v7, /device:TPU:8, one launch (start us, length us, event | category | flops | bytes accessed | tf_op | source)
XLA Modules:
  0.0 137.1 jit_solution(12267380959841819711)
XLA Ops:
  0.0 0.8 broadcast_in_dim.2.spectra
  0.8 0.0 copy-start
  0.8 0.0 copy-start.1
  0.8 0.0 copy-start.2
  0.9 0.0 copy-start.3
  0.9 1.4 %shard_map.73 = f32[64,16,128]{2,1,0:T(8,128)S(1)} custom-call(f32[8,64]{1,0:T(8,128)} %bitcast.40, f32[8,4,256]{2,1,0:T(4,128)} %bitcast.33, f32[32,128,128]{2,1,0:T(8,128)} %bitcast.23, f32[128,256]{1,0:T(8,128)} %bitcast.30, bf16[256,256]{1,0:T(8,128)(2,1)} %constant.24.clone.rest_2_.ahead_ref, bf16[256,256]{1,0:T(8,128)(2,1)} %constant.25.clone.rest_3_.back_ref), custom_call_target="tpu_custom_call" | custom-call | tf_op jit(solution)/shard_map/pallas_call | solution.py:369
  2.3 29.1 %all_to_all.20 = f32[64,16,128]{2,1,0:T(8,128)S(1)} all-to-all(f32[64,16,128]{2,1,0:T(8,128)S(1)} %shard_map.73), channel_id=1, replica_groups=mesh['energy'=64,'tile'=4] {'energy'}, dimensions={0} | all-to-all | bytes 1048576 | tf_op jit(solution)/shard_map/all_to_all | solution.py:383
  31.4 0.0 copy-done
  31.4 0.0 copy-done.1
  31.4 0.0 copy-done.2
  31.4 0.0 copy-done.3
  31.4 0.0 copy-start.4
  31.4 5.0 %shard_map.74 = f32[32,32,128]{2,1,0:T(8,128)S(1)} custom-call(f32[32,32,128]{2,1,0:T(8,128)S(1)} %bitcast.28, s32[2,32]{1,0:T(2,128)} %bitcast.41, f32[32,128,128]{2,1,0:T(8,128)S(1)} %bitcast.24, f32[128,256]{1,0:T(8,128)S(1)} %bitcast.31, bf16[256,256]{1,0:T(8,128)(2,1)S(1)} %copy-done.3, bf16[256,256]{1,0:T(8,128)(2,1)S(1)} %copy-done.2), custom_call_target="tpu_custom_call" | custom-call | tf_op jit(solution)/shard_map/pallas_call | solution.py:184
  36.5 23.0 %all_to_all.21.grads_ref = f32[64,16,128]{2,1,0:T(8,128)S(1)} all-to-all(f32[64,16,128]{2,1,0:T(8,128)S(1)} %bitcast.29), channel_id=1, replica_groups=mesh['energy'=64,'tile'=4] {'energy'}, dimensions={0} | all-to-all | bytes 1048576 | tf_op jit(solution)/shard_map/all_to_all | solution.py:385
  59.5 0.0 copy-done.4
  59.5 0.3 shard_map.75
  59.8 0.1 collective-permute-start
  59.9 2.4 %collective-permute-start.1 = (f32[8,4,128]{2,1,0:T(4,128)S(1)}, f32[8,4,128]{2,1,0:T(4,128)S(1)}, u32[]{:S(2)}, u32[]{:S(2)}) collective-permute-start(f32[8,4,128]{2,1,0:T(4,128)S(1)} %get-tuple-element.21), channel_id=1, source_target_pairs={{0,1},{1,0},{2,3},{3,2},{4,5},{5,4},{6,7},{7,6},{8,9},{9,8},{10,11... | collective-permute-start | bytes 49160 | tf_op jit(solution)/shard_map/ppermute | solution.py:334
  62.3 2.3 %collective-permute-done = f32[8,4,128]{2,1,0:T(4,128)S(1)} collective-permute-done((f32[8,4,128]{2,1,0:T(4,128)S(1)}, f32[8,4,128]{2,1,0:T(4,128)S(1)}, u32[]{:S(2)}, u32[]{:S(2)}) %collective-permute-start) | collective-permute-done | bytes 16416 | tf_op jit(solution)/shard_map/ppermute | solution.py:333
  64.6 0.0 collective-permute-done.1
  64.6 4.0 %collective-permute-start.3 = (f32[96,128]{1,0:T(8,128)S(1)}, f32[96,128]{1,0:T(8,128)S(1)}, u32[]{:S(2)}, u32[]{:S(2)}) collective-permute-start(f32[96,128]{1,0:T(8,128)S(1)} %pad_maximum_fusion.mine_ref), channel_id=1, source_target_pairs={{4,8},{8,4},{12,16},{16,12},{20,24},{24,20},{28,32},{32,28},{36,40... | collective-permute-start | bytes 147464 | tf_op jit(solution)/shard_map/ppermute | solution.py:342
  68.5 0.0 collective-permute-start.2
  68.5 4.4 %collective-permute-done.3.far_ref = f32[96,128]{1,0:T(8,128)S(1)} collective-permute-done((f32[96,128]{1,0:T(8,128)S(1)}, f32[96,128]{1,0:T(8,128)S(1)}, u32[]{:S(2)}, u32[]{:S(2)}) %collective-permute-start.3) | collective-permute-done | bytes 49184 | tf_op jit(solution)/shard_map/ppermute | solution.py:342
  73.0 0.0 collective-permute-done.2.near_ref
  73.0 0.9 shard_map.76
  73.9 21.8 %all_to_all.22 = f32[64,16,128]{2,1,0:T(8,128)S(1)} all-to-all(f32[64,16,128]{2,1,0:T(8,128)S(1)} %get-tuple-element.22), channel_id=1, replica_groups=mesh['energy'=64,'tile'=4] {'energy'}, dimensions={0} | all-to-all | bytes 1048576 | tf_op jit(solution)/shard_map/all_to_all | solution.py:383
  95.6 4.9 %shard_map.77 = f32[32,32,128]{2,1,0:T(8,128)S(1)} custom-call(f32[32,32,128]{2,1,0:T(8,128)S(1)} %bitcast.26, s32[2,32]{1,0:T(2,128)} %bitcast.42, f32[32,128,128]{2,1,0:T(8,128)S(1)} %bitcast.25, f32[128,256]{1,0:T(8,128)S(1)} %bitcast.32, bf16[256,256]{1,0:T(8,128)(2,1)S(1)} %copy-done.3, bf16[256,256]{1,0:T(8,128)(2,1)S(1)} %copy-done.2), custom_call_target="tpu_custom_call" | custom-call | tf_op jit(solution)/shard_map/pallas_call | solution.py:184
  100.5 21.9 %all_to_all.23.grads_ref = f32[64,16,128]{2,1,0:T(8,128)S(1)} all-to-all(f32[64,16,128]{2,1,0:T(8,128)S(1)} %bitcast.27), channel_id=1, replica_groups=mesh['energy'=64,'tile'=4] {'energy'}, dimensions={0} | all-to-all | bytes 1048576 | tf_op jit(solution)/shard_map/all_to_all | solution.py:385
  122.4 0.3 shard_map.78
  122.7 0.1 collective-permute-start.4
  122.8 0.1 collective-permute-start.5
  122.9 4.6 %collective-permute-done.4 = f32[8,4,128]{2,1,0:T(4,128)S(1)} collective-permute-done((f32[8,4,128]{2,1,0:T(4,128)S(1)}, f32[8,4,128]{2,1,0:T(4,128)S(1)}, u32[]{:S(2)}, u32[]{:S(2)}) %collective-permute-start.4) | collective-permute-done | bytes 16416 | tf_op jit(solution)/shard_map/ppermute | solution.py:333
  127.5 0.0 collective-permute-done.5
  127.5 3.9 %collective-permute-start.7 = (f32[96,128]{1,0:T(8,128)S(1)}, f32[96,128]{1,0:T(8,128)S(1)}, u32[]{:S(2)}, u32[]{:S(2)}) collective-permute-start(f32[96,128]{1,0:T(8,128)S(1)} %pad_maximum_fusion.1.mine_ref), channel_id=1, source_target_pairs={{4,8},{8,4},{12,16},{16,12},{20,24},{24,20},{28,32},{32,28},{36,40... | collective-permute-start | bytes 147464 | tf_op jit(solution)/shard_map/ppermute | solution.py:342
  131.4 0.0 collective-permute-start.6
  131.4 4.5 %collective-permute-done.7.far_ref = f32[96,128]{1,0:T(8,128)S(1)} collective-permute-done((f32[96,128]{1,0:T(8,128)S(1)}, f32[96,128]{1,0:T(8,128)S(1)}, u32[]{:S(2)}, u32[]{:S(2)}) %collective-permute-start.7) | collective-permute-done | bytes 49184 | tf_op jit(solution)/shard_map/ppermute | solution.py:342
  135.9 0.0 collective-permute-done.6.near_ref
  135.9 1.2 shard_map.79
  (5 shorter events, 0.0 us)
Async XLA Ops:
  0.8 30.6 %copy-start = (f32[1,1,32,128,128]{4,3,2,1,0:T(8,128)S(1)}, f32[1,1,32,128,128]{4,3,2,1,0:T(8,128)}, u32[]{:S(2)}) copy-start(f32[1,1,32,128,128]{4,3,2,1,0:T(8,128)} %param.11) | copy-start | bytes 6291460
  0.8 30.6 %copy-start.1 = (f32[1,128,256]{2,1,0:T(8,128)S(1)}, f32[1,128,256]{2,1,0:T(8,128)}, u32[]{:S(2)}) copy-start(f32[1,128,256]{2,1,0:T(8,128)} %param.9) | copy-start | bytes 393220
  0.8 30.6 %copy-start.2 = (bf16[256,256]{1,0:T(8,128)(2,1)S(1)}, bf16[256,256]{1,0:T(8,128)(2,1)}, u32[]{:S(2)}) copy-start(bf16[256,256]{1,0:T(8,128)(2,1)} %constant.25.clone.rest_3_.back_ref) | copy-start | bytes 393220
  0.9 30.6 %copy-start.3 = (bf16[256,256]{1,0:T(8,128)(2,1)S(1)}, bf16[256,256]{1,0:T(8,128)(2,1)}, u32[]{:S(2)}) copy-start(bf16[256,256]{1,0:T(8,128)(2,1)} %constant.24.clone.rest_2_.ahead_ref) | copy-start | bytes 393220
  31.4 28.1 %copy-start.4 = (f32[2,4,4,256]{3,2,1,0:T(4,128)S(1)}, f32[2,4,4,256]{3,2,1,0:T(4,128)}, u32[]{:S(2)}) copy-start(f32[2,4,4,256]{3,2,1,0:T(4,128)} %param.7) | copy-start | bytes 98308
  59.8 4.8 %collective-permute-start = (f32[8,4,128]{2,1,0:T(4,128)S(1)}, f32[8,4,128]{2,1,0:T(4,128)S(1)}, u32[]{:S(2)}, u32[]{:S(2)}) collective-permute-start(f32[8,4,128]{2,1,0:T(4,128)S(1)} %get-tuple-element.20), channel_id=1, source_target_pairs={{1,2},{2,1},{3,0},{0,3},{5,6},{6,5},{7,4},{4,7},{9,10},{10,9},{11,... | collective-permute-start | bytes 49160 | tf_op jit(solution)/shard_map/ppermute | solution.py:333
  59.9 4.7 %collective-permute-start.1 = (f32[8,4,128]{2,1,0:T(4,128)S(1)}, f32[8,4,128]{2,1,0:T(4,128)S(1)}, u32[]{:S(2)}, u32[]{:S(2)}) collective-permute-start(f32[8,4,128]{2,1,0:T(4,128)S(1)} %get-tuple-element.21), channel_id=1, source_target_pairs={{0,1},{1,0},{2,3},{3,2},{4,5},{5,4},{6,7},{7,6},{8,9},{9,8},{10,11... | collective-permute-start | bytes 49160 | tf_op jit(solution)/shard_map/ppermute | solution.py:334
  64.6 8.4 %collective-permute-start.3 = (f32[96,128]{1,0:T(8,128)S(1)}, f32[96,128]{1,0:T(8,128)S(1)}, u32[]{:S(2)}, u32[]{:S(2)}) collective-permute-start(f32[96,128]{1,0:T(8,128)S(1)} %pad_maximum_fusion.mine_ref), channel_id=1, source_target_pairs={{4,8},{8,4},{12,16},{16,12},{20,24},{24,20},{28,32},{32,28},{36,40... | collective-permute-start | bytes 147464 | tf_op jit(solution)/shard_map/ppermute | solution.py:342
  68.5 4.4 %collective-permute-start.2 = (f32[96,128]{1,0:T(8,128)S(1)}, f32[96,128]{1,0:T(8,128)S(1)}, u32[]{:S(2)}, u32[]{:S(2)}) collective-permute-start(f32[96,128]{1,0:T(8,128)S(1)} %pad_maximum_fusion.mine_ref), channel_id=1, source_target_pairs={{0,4},{4,0},{8,12},{12,8},{16,20},{20,16},{24,28},{28,24},{32,36},... | collective-permute-start | bytes 147464 | tf_op jit(solution)/shard_map/ppermute | solution.py:342
  122.7 4.8 %collective-permute-start.4 = (f32[8,4,128]{2,1,0:T(4,128)S(1)}, f32[8,4,128]{2,1,0:T(4,128)S(1)}, u32[]{:S(2)}, u32[]{:S(2)}) collective-permute-start(f32[8,4,128]{2,1,0:T(4,128)S(1)} %get-tuple-element.25), channel_id=1, source_target_pairs={{1,2},{2,1},{3,0},{0,3},{5,6},{6,5},{7,4},{4,7},{9,10},{10,9},{11,... | collective-permute-start | bytes 49160 | tf_op jit(solution)/shard_map/ppermute | solution.py:333
  122.8 4.7 %collective-permute-start.5 = (f32[8,4,128]{2,1,0:T(4,128)S(1)}, f32[8,4,128]{2,1,0:T(4,128)S(1)}, u32[]{:S(2)}, u32[]{:S(2)}) collective-permute-start(f32[8,4,128]{2,1,0:T(4,128)S(1)} %get-tuple-element.26), channel_id=1, source_target_pairs={{0,1},{1,0},{2,3},{3,2},{4,5},{5,4},{6,7},{7,6},{8,9},{9,8},{10,11... | collective-permute-start | bytes 49160 | tf_op jit(solution)/shard_map/ppermute | solution.py:334
  127.5 8.4 %collective-permute-start.7 = (f32[96,128]{1,0:T(8,128)S(1)}, f32[96,128]{1,0:T(8,128)S(1)}, u32[]{:S(2)}, u32[]{:S(2)}) collective-permute-start(f32[96,128]{1,0:T(8,128)S(1)} %pad_maximum_fusion.1.mine_ref), channel_id=1, source_target_pairs={{4,8},{8,4},{12,16},{16,12},{20,24},{24,20},{28,32},{32,28},{36,40... | collective-permute-start | bytes 147464 | tf_op jit(solution)/shard_map/ppermute | solution.py:342
  131.4 4.5 %collective-permute-start.6 = (f32[96,128]{1,0:T(8,128)S(1)}, f32[96,128]{1,0:T(8,128)S(1)}, u32[]{:S(2)}, u32[]{:S(2)}) collective-permute-start(f32[96,128]{1,0:T(8,128)S(1)} %pad_maximum_fusion.1.mine_ref), channel_id=1, source_target_pairs={{0,4},{4,0},{8,12},{12,8},{16,20},{20,16},{24,28},{28,24},{32,36},... | collective-permute-start | bytes 147464 | tf_op jit(solution)/shard_map/ppermute | solution.py:342

commit v8 on v7

--- a/solution.py
+++ b/solution.py
@@ -216,7 +216,7 @@
 
 
 def mix_kernel(spectra_hbm, maps_hbm, *rest):
-    out_ref, maps, rows_ref, spectra, sems = rest[-5:]
+    out_ref, rows_of, maps, rows_ref, spectra, sems = rest[-6:]
     copies = [
         pltpu.make_async_copy(spectra_hbm, spectra, sems.at[0]),
         pltpu.make_async_copy(maps_hbm, maps, sems.at[1]),
@@ -227,6 +227,13 @@
         copy.wait()
     for half in range(2):
         rows_ref[:, 4 * half : 4 * half + 4, :] = maps[:, :, half * LEN : (half + 1) * LEN]
+
+    def spread(e, carry):
+        for k in range(spectra.shape[0]):
+            rows_of[k, pl.ds(e, 1), :] = jnp.full((1, LEN), spectra[k, e])
+        return carry
+
+    lax.fori_loop(0, out_ref.shape[0], spread, 0, unroll=8)
     mixed([rows_ref[p] for p in range(rows_ref.shape[0])], lambda k, e: spectra[k, e], out_ref)
 
 
@@ -353,24 +360,21 @@
     tables = dft_blocks(*dft_tables(LEN))
     weights = spectra.transpose(1, 2, 0).reshape(2 * materials, energies)
     factor = DATA_STEP / math.sqrt(energies)
-    spread_weights = jnp.broadcast_to(weights[:, :, None], (*weights.shape, LEN))
     last = (lax.axis_size("energy") - 1, lax.axis_size("tile") - 1)
     strip = jax.ShapeDtypeStruct((planes, 2 * rows, LEN), jnp.float32)
     part = jax.ShapeDtypeStruct((planes, rows, LEN), jnp.float32)
     spread = jax.ShapeDtypeStruct((energies, 4 * rows, LEN), jnp.float32)
     field = pltpu.VMEM((planes, 16, 3 * LEN), jnp.float32)
     even = lax.axis_index("tile") % 2 == 0
-    maps, even, spread_weights = lax.optimization_barrier(
-        (material_maps.reshape(planes, rows, columns), even, spread_weights)
-    )
+    maps, even = lax.optimization_barrier((material_maps.reshape(planes, rows, columns), even))
     current = maps.reshape(planes, rows, 2, LEN).transpose(0, 2, 1, 3).reshape(planes, 2 * rows, LEN)
     hbm = pl.BlockSpec(memory_space=pltpu.HBM)
     later = (counts, probe, *tables)
-    mixes = pl.pallas_call(
+    mixes, spread_weights = pl.pallas_call(
         mix_kernel,
-        out_shape=spread,
+        out_shape=(spread, jax.ShapeDtypeStruct((*weights.shape, LEN), jnp.float32)),
         in_specs=[hbm] * (2 + len(later)),
-        out_specs=pl.BlockSpec(memory_space=pltpu.VMEM),
+        out_specs=(pl.BlockSpec(memory_space=pltpu.VMEM),) * 2,
         scratch_shapes=[
             pltpu.VMEM(maps.shape, jnp.float32),
             pltpu.VMEM(strip.shape, jnp.float32),

time: 137 us -> 137 us (level)
  no operation moved by 1% of the time
where the time goes in v8:
time: 137 us
  blocking collectives  95.7 us (70%)
  waiting for transfers between devices  15.7 us (11%)
  Pallas kernels  14.5 us (11%)
  starting transfers between devices  10.5 us (8%)
    all_to_all x2, blocking collectives, shards(): lax.all_to_all(mixes, 'energy', split_axis=0, concat_axis=0, tiled=True)  50.8 us
    all_to_all x2, blocking collectives, shards(): lax.all_to_all(grads, 'energy', split_axis=0, concat_axis=0, tiled=True)  44.9 us
    pallas_call x2, Pallas kernels, patch_gradient(): pl.pallas_call(functools.partial(patch_kernel, group), out_shape=jax.Shap...  9.87 us
    ppermute x2, waiting for transfers between devices, from_neighbours(): lax.ppermute(strip, 'energy', far)  8.91 us
    ppermute x2, starting transfers between devices, from_neighbours(): lax.ppermute(strip, 'energy', far)  7.88 us
    ppermute x2, waiting for transfers between devices, with_edges(): from_far = lax.ppermute(to_far, 'tile', far)  6.81 us
  transfers between devices with their start and end apart: 8, of which 4 were waited for; matrix products, arithmetic and copies ran while one was open for 0% of the time, Pallas kernels for 0%

profile of v8, /device:TPU:8, one launch (start us, length us, event | category | flops | bytes accessed | tf_op | source)
XLA Modules:
  0.0 136.7 jit_solution(14011536604030876031)
XLA Ops:
  0.0 0.0 copy-start.2
  0.0 0.0 copy-start.3
  0.0 0.0 copy-start
  0.0 0.0 copy-start.1
  0.0 1.9 %shard_map.73 = (f32[64,16,128]{2,1,0:T(8,128)S(1)}, f32[8,64,128]{2,1,0:T(8,128)S(1)}) custom-call(f32[8,64]{1,0:T(8,128)} %bitcast.39, f32[8,4,256]{2,1,0:T(4,128)} %bitcast.33, f32[32,128,128]{2,1,0:T(8,128)} %bitcast.23, f32[128,256]{1,0:T(8,128)} %bitcast.30, bf16[256,256]{1,0:T(8,128)(2,1)} %constant.24.clone.rest_2_.ahead_ref, ...), custom_call_target="tpu_custom_call" | custom-call | tf_op jit(solution)/shard_map/pallas_call | solution.py:373
  1.9 29.1 %all_to_all.20 = f32[64,16,128]{2,1,0:T(8,128)S(1)} all-to-all(f32[64,16,128]{2,1,0:T(8,128)S(1)} %get-tuple-element.18), channel_id=1, replica_groups=mesh['energy'=64,'tile'=4] {'energy'}, dimensions={0} | all-to-all | bytes 1048576 | tf_op jit(solution)/shard_map/all_to_all | solution.py:387
  31.0 0.0 copy-done.2
  31.0 0.0 copy-done.3
  31.0 0.0 copy-done
  31.0 0.0 copy-done.1
  31.1 0.0 copy-start.4
  31.1 5.0 %shard_map.74 = f32[32,32,128]{2,1,0:T(8,128)S(1)} custom-call(f32[32,32,128]{2,1,0:T(8,128)S(1)} %bitcast.28, s32[2,32]{1,0:T(2,128)} %bitcast.40, f32[32,128,128]{2,1,0:T(8,128)S(1)} %bitcast.24, f32[128,256]{1,0:T(8,128)S(1)} %bitcast.31, bf16[256,256]{1,0:T(8,128)(2,1)S(1)} %copy-done.3, bf16[256,256]{1,0:T(8,128)(2,1)S(1)} %copy-done.2), custom_call_target="tpu_custom_call" | custom-call | tf_op jit(solution)/shard_map/pallas_call | solution.py:184
  36.1 23.0 %all_to_all.21.grads_ref = f32[64,16,128]{2,1,0:T(8,128)S(1)} all-to-all(f32[64,16,128]{2,1,0:T(8,128)S(1)} %bitcast.29), channel_id=1, replica_groups=mesh['energy'=64,'tile'=4] {'energy'}, dimensions={0} | all-to-all | bytes 1048576 | tf_op jit(solution)/shard_map/all_to_all | solution.py:389
  59.1 0.0 copy-done.4
  59.1 0.3 shard_map.75
  59.4 0.1 collective-permute-start
  59.5 2.4 %collective-permute-start.1 = (f32[8,4,128]{2,1,0:T(4,128)S(1)}, f32[8,4,128]{2,1,0:T(4,128)S(1)}, u32[]{:S(2)}, u32[]{:S(2)}) collective-permute-start(f32[8,4,128]{2,1,0:T(4,128)S(1)} %get-tuple-element.23), channel_id=1, source_target_pairs={{0,1},{1,0},{2,3},{3,2},{4,5},{5,4},{6,7},{7,6},{8,9},{9,8},{10,11... | collective-permute-start | bytes 49160 | tf_op jit(solution)/shard_map/ppermute | solution.py:341
  61.9 2.3 %collective-permute-done = f32[8,4,128]{2,1,0:T(4,128)S(1)} collective-permute-done((f32[8,4,128]{2,1,0:T(4,128)S(1)}, f32[8,4,128]{2,1,0:T(4,128)S(1)}, u32[]{:S(2)}, u32[]{:S(2)}) %collective-permute-start) | collective-permute-done | bytes 16416 | tf_op jit(solution)/shard_map/ppermute | solution.py:340
  64.2 0.0 collective-permute-done.1
  64.2 4.0 %collective-permute-start.3 = (f32[96,128]{1,0:T(8,128)S(1)}, f32[96,128]{1,0:T(8,128)S(1)}, u32[]{:S(2)}, u32[]{:S(2)}) collective-permute-start(f32[96,128]{1,0:T(8,128)S(1)} %pad_maximum_fusion.mine_ref), channel_id=1, source_target_pairs={{4,8},{8,4},{12,16},{16,12},{20,24},{24,20},{28,32},{32,28},{36,40... | collective-permute-start | bytes 147464 | tf_op jit(solution)/shard_map/ppermute | solution.py:349
  68.2 0.0 collective-permute-start.2
  68.2 4.4 %collective-permute-done.3.far_ref = f32[96,128]{1,0:T(8,128)S(1)} collective-permute-done((f32[96,128]{1,0:T(8,128)S(1)}, f32[96,128]{1,0:T(8,128)S(1)}, u32[]{:S(2)}, u32[]{:S(2)}) %collective-permute-start.3) | collective-permute-done | bytes 49184 | tf_op jit(solution)/shard_map/ppermute | solution.py:349
  72.6 0.0 collective-permute-done.2.near_ref
  72.6 0.9 shard_map.76
  73.5 21.7 %all_to_all.22 = f32[64,16,128]{2,1,0:T(8,128)S(1)} all-to-all(f32[64,16,128]{2,1,0:T(8,128)S(1)} %get-tuple-element.24), channel_id=1, replica_groups=mesh['energy'=64,'tile'=4] {'energy'}, dimensions={0} | all-to-all | bytes 1048576 | tf_op jit(solution)/shard_map/all_to_all | solution.py:387
  95.2 4.9 %shard_map.77 = f32[32,32,128]{2,1,0:T(8,128)S(1)} custom-call(f32[32,32,128]{2,1,0:T(8,128)S(1)} %bitcast.26, s32[2,32]{1,0:T(2,128)} %bitcast.41, f32[32,128,128]{2,1,0:T(8,128)S(1)} %bitcast.25, f32[128,256]{1,0:T(8,128)S(1)} %bitcast.32, bf16[256,256]{1,0:T(8,128)(2,1)S(1)} %copy-done.3, bf16[256,256]{1,0:T(8,128)(2,1)S(1)} %copy-done.2), custom_call_target="tpu_custom_call" | custom-call | tf_op jit(solution)/shard_map/pallas_call | solution.py:184
  100.1 21.9 %all_to_all.23.grads_ref = f32[64,16,128]{2,1,0:T(8,128)S(1)} all-to-all(f32[64,16,128]{2,1,0:T(8,128)S(1)} %bitcast.27), channel_id=1, replica_groups=mesh['energy'=64,'tile'=4] {'energy'}, dimensions={0} | all-to-all | bytes 1048576 | tf_op jit(solution)/shard_map/all_to_all | solution.py:389
  122.0 0.3 shard_map.78
  122.3 0.1 collective-permute-start.4
  122.4 0.1 collective-permute-start.5
  122.5 4.6 %collective-permute-done.4 = f32[8,4,128]{2,1,0:T(4,128)S(1)} collective-permute-done((f32[8,4,128]{2,1,0:T(4,128)S(1)}, f32[8,4,128]{2,1,0:T(4,128)S(1)}, u32[]{:S(2)}, u32[]{:S(2)}) %collective-permute-start.4) | collective-permute-done | bytes 16416 | tf_op jit(solution)/shard_map/ppermute | solution.py:340
  127.0 0.0 collective-permute-done.5
  127.1 3.9 %collective-permute-start.7 = (f32[96,128]{1,0:T(8,128)S(1)}, f32[96,128]{1,0:T(8,128)S(1)}, u32[]{:S(2)}, u32[]{:S(2)}) collective-permute-start(f32[96,128]{1,0:T(8,128)S(1)} %pad_maximum_fusion.1.mine_ref), channel_id=1, source_target_pairs={{4,8},{8,4},{12,16},{16,12},{20,24},{24,20},{28,32},{32,28},{36,40... | collective-permute-start | bytes 147464 | tf_op jit(solution)/shard_map/ppermute | solution.py:349
  131.0 0.0 collective-permute-start.6
  131.0 4.5 %collective-permute-done.7.far_ref = f32[96,128]{1,0:T(8,128)S(1)} collective-permute-done((f32[96,128]{1,0:T(8,128)S(1)}, f32[96,128]{1,0:T(8,128)S(1)}, u32[]{:S(2)}, u32[]{:S(2)}) %collective-permute-start.7) | collective-permute-done | bytes 49184 | tf_op jit(solution)/shard_map/ppermute | solution.py:349
  135.5 0.0 collective-permute-done.6.near_ref
  135.5 1.2 shard_map.79
  (5 shorter events, 0.0 us)
Async XLA Ops:
  0.0 31.0 %copy-start.2 = (bf16[256,256]{1,0:T(8,128)(2,1)S(1)}, bf16[256,256]{1,0:T(8,128)(2,1)}, u32[]{:S(2)}) copy-start(bf16[256,256]{1,0:T(8,128)(2,1)} %constant.25.clone.rest_3_.back_ref) | copy-start | bytes 393220
  0.0 31.0 %copy-start.3 = (bf16[256,256]{1,0:T(8,128)(2,1)S(1)}, bf16[256,256]{1,0:T(8,128)(2,1)}, u32[]{:S(2)}) copy-start(bf16[256,256]{1,0:T(8,128)(2,1)} %constant.24.clone.rest_2_.ahead_ref) | copy-start | bytes 393220
  0.0 31.0 %copy-start = (f32[1,1,32,128,128]{4,3,2,1,0:T(8,128)S(1)}, f32[1,1,32,128,128]{4,3,2,1,0:T(8,128)}, u32[]{:S(2)}) copy-start(f32[1,1,32,128,128]{4,3,2,1,0:T(8,128)} %param.11) | copy-start | bytes 6291460
  0.0 31.0 %copy-start.1 = (f32[1,128,256]{2,1,0:T(8,128)S(1)}, f32[1,128,256]{2,1,0:T(8,128)}, u32[]{:S(2)}) copy-start(f32[1,128,256]{2,1,0:T(8,128)} %param.9) | copy-start | bytes 393220
  31.1 28.0 %copy-start.4 = (f32[2,4,4,256]{3,2,1,0:T(4,128)S(1)}, f32[2,4,4,256]{3,2,1,0:T(4,128)}, u32[]{:S(2)}) copy-start(f32[2,4,4,256]{3,2,1,0:T(4,128)} %param.7) | copy-start | bytes 98308
  59.4 4.8 %collective-permute-start = (f32[8,4,128]{2,1,0:T(4,128)S(1)}, f32[8,4,128]{2,1,0:T(4,128)S(1)}, u32[]{:S(2)}, u32[]{:S(2)}) collective-permute-start(f32[8,4,128]{2,1,0:T(4,128)S(1)} %get-tuple-element.22), channel_id=1, source_target_pairs={{1,2},{2,1},{3,0},{0,3},{5,6},{6,5},{7,4},{4,7},{9,10},{10,9},{11,... | collective-permute-start | bytes 49160 | tf_op jit(solution)/shard_map/ppermute | solution.py:340
  59.5 4.7 %collective-permute-start.1 = (f32[8,4,128]{2,1,0:T(4,128)S(1)}, f32[8,4,128]{2,1,0:T(4,128)S(1)}, u32[]{:S(2)}, u32[]{:S(2)}) collective-permute-start(f32[8,4,128]{2,1,0:T(4,128)S(1)} %get-tuple-element.23), channel_id=1, source_target_pairs={{0,1},{1,0},{2,3},{3,2},{4,5},{5,4},{6,7},{7,6},{8,9},{9,8},{10,11... | collective-permute-start | bytes 49160 | tf_op jit(solution)/shard_map/ppermute | solution.py:341
  64.2 8.4 %collective-permute-start.3 = (f32[96,128]{1,0:T(8,128)S(1)}, f32[96,128]{1,0:T(8,128)S(1)}, u32[]{:S(2)}, u32[]{:S(2)}) collective-permute-start(f32[96,128]{1,0:T(8,128)S(1)} %pad_maximum_fusion.mine_ref), channel_id=1, source_target_pairs={{4,8},{8,4},{12,16},{16,12},{20,24},{24,20},{28,32},{32,28},{36,40... | collective-permute-start | bytes 147464 | tf_op jit(solution)/shard_map/ppermute | solution.py:349
  68.2 4.4 %collective-permute-start.2 = (f32[96,128]{1,0:T(8,128)S(1)}, f32[96,128]{1,0:T(8,128)S(1)}, u32[]{:S(2)}, u32[]{:S(2)}) collective-permute-start(f32[96,128]{1,0:T(8,128)S(1)} %pad_maximum_fusion.mine_ref), channel_id=1, source_target_pairs={{0,4},{4,0},{8,12},{12,8},{16,20},{20,16},{24,28},{28,24},{32,36},... | collective-permute-start | bytes 147464 | tf_op jit(solution)/shard_map/ppermute | solution.py:349
  122.3 4.8 %collective-permute-start.4 = (f32[8,4,128]{2,1,0:T(4,128)S(1)}, f32[8,4,128]{2,1,0:T(4,128)S(1)}, u32[]{:S(2)}, u32[]{:S(2)}) collective-permute-start(f32[8,4,128]{2,1,0:T(4,128)S(1)} %get-tuple-element.27), channel_id=1, source_target_pairs={{1,2},{2,1},{3,0},{0,3},{5,6},{6,5},{7,4},{4,7},{9,10},{10,9},{11,... | collective-permute-start | bytes 49160 | tf_op jit(solution)/shard_map/ppermute | solution.py:340
  122.4 4.7 %collective-permute-start.5 = (f32[8,4,128]{2,1,0:T(4,128)S(1)}, f32[8,4,128]{2,1,0:T(4,128)S(1)}, u32[]{:S(2)}, u32[]{:S(2)}) collective-permute-start(f32[8,4,128]{2,1,0:T(4,128)S(1)} %get-tuple-element.28), channel_id=1, source_target_pairs={{0,1},{1,0},{2,3},{3,2},{4,5},{5,4},{6,7},{7,6},{8,9},{9,8},{10,11... | collective-permute-start | bytes 49160 | tf_op jit(solution)/shard_map/ppermute | solution.py:341
  127.1 8.4 %collective-permute-start.7 = (f32[96,128]{1,0:T(8,128)S(1)}, f32[96,128]{1,0:T(8,128)S(1)}, u32[]{:S(2)}, u32[]{:S(2)}) collective-permute-start(f32[96,128]{1,0:T(8,128)S(1)} %pad_maximum_fusion.1.mine_ref), channel_id=1, source_target_pairs={{4,8},{8,4},{12,16},{16,12},{20,24},{24,20},{28,32},{32,28},{36,40... | collective-permute-start | bytes 147464 | tf_op jit(solution)/shard_map/ppermute | solution.py:349
  131.0 4.5 %collective-permute-start.6 = (f32[96,128]{1,0:T(8,128)S(1)}, f32[96,128]{1,0:T(8,128)S(1)}, u32[]{:S(2)}, u32[]{:S(2)}) collective-permute-start(f32[96,128]{1,0:T(8,128)S(1)} %pad_maximum_fusion.1.mine_ref), channel_id=1, source_target_pairs={{0,4},{4,0},{8,12},{12,8},{16,20},{20,16},{24,28},{28,24},{32,36},... | collective-permute-start | bytes 147464 | tf_op jit(solution)/shard_map/ppermute | solution.py:349

commit v9 on v8

--- a/solution.py
+++ b/solution.py
@@ -228,13 +228,12 @@
     for half in range(2):
         rows_ref[:, 4 * half : 4 * half + 4, :] = maps[:, :, half * LEN : (half + 1) * LEN]
 
-    def spread(e, carry):
-        for k in range(spectra.shape[0]):
-            rows_of[k, pl.ds(e, 1), :] = jnp.full((1, LEN), spectra[k, e])
-        return carry
-
-    lax.fori_loop(0, out_ref.shape[0], spread, 0, unroll=8)
-    mixed([rows_ref[p] for p in range(rows_ref.shape[0])], lambda k, e: spectra[k, e], out_ref)
+    def coefficient(k, e):
+        value = jnp.full((1, LEN), spectra[k, e])
+        rows_of[k, pl.ds(e, 1), :] = value
+        return value
+
+    mixed([rows_ref[p] for p in range(rows_ref.shape[0])], coefficient, out_ref)
 
 
 def unmix_kernel(factor, grads_ref, rows_ref, spectra, out_ref, far_ref, near_ref):

time: 137 us -> 137 us (level)
  no operation moved by 1% of the time
where the time goes in v9:
time: 137 us; the launch traced here: 136 us
  blocking collectives  95.9 us (70%)
  waiting for transfers between devices  15.6 us (11%)
  Pallas kernels  13.9 us (10%)
  starting transfers between devices  10.7 us (8%)
    all_to_all x2, blocking collectives, shards(): lax.all_to_all(mixes, 'energy', split_axis=0, concat_axis=0, tiled=True)  50.9 us
    all_to_all x2, blocking collectives, shards(): lax.all_to_all(grads, 'energy', split_axis=0, concat_axis=0, tiled=True)  45 us
    pallas_call x2, Pallas kernels, patch_gradient(): pl.pallas_call(functools.partial(patch_kernel, group), out_shape=jax.Shap...  9.78 us
    ppermute x2, waiting for transfers between devices, from_neighbours(): lax.ppermute(strip, 'energy', far)  8.86 us
    ppermute x2, starting transfers between devices, from_neighbours(): lax.ppermute(strip, 'energy', far)  7.92 us
    ppermute x2, waiting for transfers between devices, with_edges(): from_far = lax.ppermute(to_far, 'tile', far)  6.75 us
  transfers between devices with their start and end apart: 8, of which 4 were waited for; matrix products, arithmetic and copies ran while one was open for 0% of the time, Pallas kernels for 0%

profile of v9, /device:TPU:8, one launch (start us, length us, event | category | flops | bytes accessed | tf_op | source)
XLA Modules:
  0.0 136.3 jit_solution(2222813016529916062)
XLA Ops:
  0.0 0.0 copy-start.2
  0.0 0.0 copy-start.3
  0.0 0.0 copy-start
  0.0 0.0 copy-start.1
  0.0 1.4 %shard_map.73 = (f32[64,16,128]{2,1,0:T(8,128)S(1)}, f32[8,64,128]{2,1,0:T(8,128)S(1)}) custom-call(f32[8,64]{1,0:T(8,128)} %bitcast.39, f32[8,4,256]{2,1,0:T(4,128)} %bitcast.33, f32[32,128,128]{2,1,0:T(8,128)} %bitcast.23, f32[128,256]{1,0:T(8,128)} %bitcast.30, bf16[256,256]{1,0:T(8,128)(2,1)} %constant.24.clone.rest_2_.ahead_ref, ...), custom_call_target="tpu_custom_call" | custom-call | tf_op jit(solution)/shard_map/pallas_call | solution.py:372
  1.5 29.1 %all_to_all.20 = f32[64,16,128]{2,1,0:T(8,128)S(1)} all-to-all(f32[64,16,128]{2,1,0:T(8,128)S(1)} %get-tuple-element.18), channel_id=1, replica_groups=mesh['energy'=64,'tile'=4] {'energy'}, dimensions={0} | all-to-all | bytes 1048576 | tf_op jit(solution)/shard_map/all_to_all | solution.py:386
  30.6 0.0 copy-done.2
  30.6 0.0 copy-done.3
  30.6 0.0 copy-done
  30.6 0.0 copy-done.1
  30.6 0.0 copy-start.4
  30.6 5.0 %shard_map.74 = f32[32,32,128]{2,1,0:T(8,128)S(1)} custom-call(f32[32,32,128]{2,1,0:T(8,128)S(1)} %bitcast.28, s32[2,32]{1,0:T(2,128)} %bitcast.40, f32[32,128,128]{2,1,0:T(8,128)S(1)} %bitcast.24, f32[128,256]{1,0:T(8,128)S(1)} %bitcast.31, bf16[256,256]{1,0:T(8,128)(2,1)S(1)} %copy-done.3, bf16[256,256]{1,0:T(8,128)(2,1)S(1)} %copy-done.2), custom_call_target="tpu_custom_call" | custom-call | tf_op jit(solution)/shard_map/pallas_call | solution.py:184
  35.6 23.0 %all_to_all.21.grads_ref = f32[64,16,128]{2,1,0:T(8,128)S(1)} all-to-all(f32[64,16,128]{2,1,0:T(8,128)S(1)} %bitcast.29), channel_id=1, replica_groups=mesh['energy'=64,'tile'=4] {'energy'}, dimensions={0} | all-to-all | bytes 1048576 | tf_op jit(solution)/shard_map/all_to_all | solution.py:388
  58.6 0.0 copy-done.4
  58.6 0.3 shard_map.75
  58.9 0.1 collective-permute-start
  59.0 2.5 %collective-permute-start.1 = (f32[8,4,128]{2,1,0:T(4,128)S(1)}, f32[8,4,128]{2,1,0:T(4,128)S(1)}, u32[]{:S(2)}, u32[]{:S(2)}) collective-permute-start(f32[8,4,128]{2,1,0:T(4,128)S(1)} %get-tuple-element.23), channel_id=1, source_target_pairs={{0,1},{1,0},{2,3},{3,2},{4,5},{5,4},{6,7},{7,6},{8,9},{9,8},{10,11... | collective-permute-start | bytes 49160 | tf_op jit(solution)/shard_map/ppermute | solution.py:340
  61.5 2.2 %collective-permute-done = f32[8,4,128]{2,1,0:T(4,128)S(1)} collective-permute-done((f32[8,4,128]{2,1,0:T(4,128)S(1)}, f32[8,4,128]{2,1,0:T(4,128)S(1)}, u32[]{:S(2)}, u32[]{:S(2)}) %collective-permute-start) | collective-permute-done | bytes 16416 | tf_op jit(solution)/shard_map/ppermute | solution.py:339
  63.7 0.0 collective-permute-done.1
  63.7 4.0 %collective-permute-start.3 = (f32[96,128]{1,0:T(8,128)S(1)}, f32[96,128]{1,0:T(8,128)S(1)}, u32[]{:S(2)}, u32[]{:S(2)}) collective-permute-start(f32[96,128]{1,0:T(8,128)S(1)} %pad_maximum_fusion.mine_ref), channel_id=1, source_target_pairs={{4,8},{8,4},{12,16},{16,12},{20,24},{24,20},{28,32},{32,28},{36,40... | collective-permute-start | bytes 147464 | tf_op jit(solution)/shard_map/ppermute | solution.py:348
  67.7 0.0 collective-permute-start.2
  67.7 4.4 %collective-permute-done.3.far_ref = f32[96,128]{1,0:T(8,128)S(1)} collective-permute-done((f32[96,128]{1,0:T(8,128)S(1)}, f32[96,128]{1,0:T(8,128)S(1)}, u32[]{:S(2)}, u32[]{:S(2)}) %collective-permute-start.3) | collective-permute-done | bytes 49184 | tf_op jit(solution)/shard_map/ppermute | solution.py:348
  72.1 0.0 collective-permute-done.2.near_ref
  72.1 0.9 shard_map.76
  73.0 21.9 %all_to_all.22 = f32[64,16,128]{2,1,0:T(8,128)S(1)} all-to-all(f32[64,16,128]{2,1,0:T(8,128)S(1)} %get-tuple-element.24), channel_id=1, replica_groups=mesh['energy'=64,'tile'=4] {'energy'}, dimensions={0} | all-to-all | bytes 1048576 | tf_op jit(solution)/shard_map/all_to_all | solution.py:386
  94.8 4.8 %shard_map.77 = f32[32,32,128]{2,1,0:T(8,128)S(1)} custom-call(f32[32,32,128]{2,1,0:T(8,128)S(1)} %bitcast.26, s32[2,32]{1,0:T(2,128)} %bitcast.41, f32[32,128,128]{2,1,0:T(8,128)S(1)} %bitcast.25, f32[128,256]{1,0:T(8,128)S(1)} %bitcast.32, bf16[256,256]{1,0:T(8,128)(2,1)S(1)} %copy-done.3, bf16[256,256]{1,0:T(8,128)(2,1)S(1)} %copy-done.2), custom_call_target="tpu_custom_call" | custom-call | tf_op jit(solution)/shard_map/pallas_call | solution.py:184
  99.7 22.0 %all_to_all.23.grads_ref = f32[64,16,128]{2,1,0:T(8,128)S(1)} all-to-all(f32[64,16,128]{2,1,0:T(8,128)S(1)} %bitcast.27), channel_id=1, replica_groups=mesh['energy'=64,'tile'=4] {'energy'}, dimensions={0} | all-to-all | bytes 1048576 | tf_op jit(solution)/shard_map/all_to_all | solution.py:388
  121.6 0.3 shard_map.78
  122.0 0.1 collective-permute-start.4
  122.1 0.1 collective-permute-start.5
  122.2 4.6 %collective-permute-done.4 = f32[8,4,128]{2,1,0:T(4,128)S(1)} collective-permute-done((f32[8,4,128]{2,1,0:T(4,128)S(1)}, f32[8,4,128]{2,1,0:T(4,128)S(1)}, u32[]{:S(2)}, u32[]{:S(2)}) %collective-permute-start.4) | collective-permute-done | bytes 16416 | tf_op jit(solution)/shard_map/ppermute | solution.py:339
  126.7 0.0 collective-permute-done.5
  126.7 3.9 %collective-permute-start.7 = (f32[96,128]{1,0:T(8,128)S(1)}, f32[96,128]{1,0:T(8,128)S(1)}, u32[]{:S(2)}, u32[]{:S(2)}) collective-permute-start(f32[96,128]{1,0:T(8,128)S(1)} %pad_maximum_fusion.1.mine_ref), channel_id=1, source_target_pairs={{4,8},{8,4},{12,16},{16,12},{20,24},{24,20},{28,32},{32,28},{36,40... | collective-permute-start | bytes 147464 | tf_op jit(solution)/shard_map/ppermute | solution.py:348
  130.7 0.0 collective-permute-start.6
  130.7 4.5 %collective-permute-done.7.far_ref = f32[96,128]{1,0:T(8,128)S(1)} collective-permute-done((f32[96,128]{1,0:T(8,128)S(1)}, f32[96,128]{1,0:T(8,128)S(1)}, u32[]{:S(2)}, u32[]{:S(2)}) %collective-permute-start.7) | collective-permute-done | bytes 49184 | tf_op jit(solution)/shard_map/ppermute | solution.py:348
  135.1 0.0 collective-permute-done.6.near_ref
  135.1 1.2 shard_map.79
  (5 shorter events, 0.0 us)
Async XLA Ops:
  0.0 30.6 %copy-start.2 = (bf16[256,256]{1,0:T(8,128)(2,1)S(1)}, bf16[256,256]{1,0:T(8,128)(2,1)}, u32[]{:S(2)}) copy-start(bf16[256,256]{1,0:T(8,128)(2,1)} %constant.25.clone.rest_3_.back_ref) | copy-start | bytes 393220
  0.0 30.6 %copy-start.3 = (bf16[256,256]{1,0:T(8,128)(2,1)S(1)}, bf16[256,256]{1,0:T(8,128)(2,1)}, u32[]{:S(2)}) copy-start(bf16[256,256]{1,0:T(8,128)(2,1)} %constant.24.clone.rest_2_.ahead_ref) | copy-start | bytes 393220
  0.0 30.6 %copy-start = (f32[1,1,32,128,128]{4,3,2,1,0:T(8,128)S(1)}, f32[1,1,32,128,128]{4,3,2,1,0:T(8,128)}, u32[]{:S(2)}) copy-start(f32[1,1,32,128,128]{4,3,2,1,0:T(8,128)} %param.11) | copy-start | bytes 6291460
  0.0 30.6 %copy-start.1 = (f32[1,128,256]{2,1,0:T(8,128)S(1)}, f32[1,128,256]{2,1,0:T(8,128)}, u32[]{:S(2)}) copy-start(f32[1,128,256]{2,1,0:T(8,128)} %param.9) | copy-start | bytes 393220
  30.6 28.0 %copy-start.4 = (f32[2,4,4,256]{3,2,1,0:T(4,128)S(1)}, f32[2,4,4,256]{3,2,1,0:T(4,128)}, u32[]{:S(2)}) copy-start(f32[2,4,4,256]{3,2,1,0:T(4,128)} %param.7) | copy-start | bytes 98308
  58.9 4.8 %collective-permute-start = (f32[8,4,128]{2,1,0:T(4,128)S(1)}, f32[8,4,128]{2,1,0:T(4,128)S(1)}, u32[]{:S(2)}, u32[]{:S(2)}) collective-permute-start(f32[8,4,128]{2,1,0:T(4,128)S(1)} %get-tuple-element.22), channel_id=1, source_target_pairs={{1,2},{2,1},{3,0},{0,3},{5,6},{6,5},{7,4},{4,7},{9,10},{10,9},{11,... | collective-permute-start | bytes 49160 | tf_op jit(solution)/shard_map/ppermute | solution.py:339
  59.0 4.7 %collective-permute-start.1 = (f32[8,4,128]{2,1,0:T(4,128)S(1)}, f32[8,4,128]{2,1,0:T(4,128)S(1)}, u32[]{:S(2)}, u32[]{:S(2)}) collective-permute-start(f32[8,4,128]{2,1,0:T(4,128)S(1)} %get-tuple-element.23), channel_id=1, source_target_pairs={{0,1},{1,0},{2,3},{3,2},{4,5},{5,4},{6,7},{7,6},{8,9},{9,8},{10,11... | collective-permute-start | bytes 49160 | tf_op jit(solution)/shard_map/ppermute | solution.py:340
  63.7 8.4 %collective-permute-start.3 = (f32[96,128]{1,0:T(8,128)S(1)}, f32[96,128]{1,0:T(8,128)S(1)}, u32[]{:S(2)}, u32[]{:S(2)}) collective-permute-start(f32[96,128]{1,0:T(8,128)S(1)} %pad_maximum_fusion.mine_ref), channel_id=1, source_target_pairs={{4,8},{8,4},{12,16},{16,12},{20,24},{24,20},{28,32},{32,28},{36,40... | collective-permute-start | bytes 147464 | tf_op jit(solution)/shard_map/ppermute | solution.py:348
  67.7 4.4 %collective-permute-start.2 = (f32[96,128]{1,0:T(8,128)S(1)}, f32[96,128]{1,0:T(8,128)S(1)}, u32[]{:S(2)}, u32[]{:S(2)}) collective-permute-start(f32[96,128]{1,0:T(8,128)S(1)} %pad_maximum_fusion.mine_ref), channel_id=1, source_target_pairs={{0,4},{4,0},{8,12},{12,8},{16,20},{20,16},{24,28},{28,24},{32,36},... | collective-permute-start | bytes 147464 | tf_op jit(solution)/shard_map/ppermute | solution.py:348
  122.0 4.8 %collective-permute-start.4 = (f32[8,4,128]{2,1,0:T(4,128)S(1)}, f32[8,4,128]{2,1,0:T(4,128)S(1)}, u32[]{:S(2)}, u32[]{:S(2)}) collective-permute-start(f32[8,4,128]{2,1,0:T(4,128)S(1)} %get-tuple-element.27), channel_id=1, source_target_pairs={{1,2},{2,1},{3,0},{0,3},{5,6},{6,5},{7,4},{4,7},{9,10},{10,9},{11,... | collective-permute-start | bytes 49160 | tf_op jit(solution)/shard_map/ppermute | solution.py:339
  122.1 4.7 %collective-permute-start.5 = (f32[8,4,128]{2,1,0:T(4,128)S(1)}, f32[8,4,128]{2,1,0:T(4,128)S(1)}, u32[]{:S(2)}, u32[]{:S(2)}) collective-permute-start(f32[8,4,128]{2,1,0:T(4,128)S(1)} %get-tuple-element.28), channel_id=1, source_target_pairs={{0,1},{1,0},{2,3},{3,2},{4,5},{5,4},{6,7},{7,6},{8,9},{9,8},{10,11... | collective-permute-start | bytes 49160 | tf_op jit(solution)/shard_map/ppermute | solution.py:340
  126.7 8.4 %collective-permute-start.7 = (f32[96,128]{1,0:T(8,128)S(1)}, f32[96,128]{1,0:T(8,128)S(1)}, u32[]{:S(2)}, u32[]{:S(2)}) collective-permute-start(f32[96,128]{1,0:T(8,128)S(1)} %pad_maximum_fusion.1.mine_ref), channel_id=1, source_target_pairs={{4,8},{8,4},{12,16},{16,12},{20,24},{24,20},{28,32},{32,28},{36,40... | collective-permute-start | bytes 147464 | tf_op jit(solution)/shard_map/ppermute | solution.py:348
  130.7 4.5 %collective-permute-start.6 = (f32[96,128]{1,0:T(8,128)S(1)}, f32[96,128]{1,0:T(8,128)S(1)}, u32[]{:S(2)}, u32[]{:S(2)}) collective-permute-start(f32[96,128]{1,0:T(8,128)S(1)} %pad_maximum_fusion.1.mine_ref), channel_id=1, source_target_pairs={{0,4},{4,0},{8,12},{12,8},{16,20},{20,16},{24,28},{28,24},{32,36},... | collective-permute-start | bytes 147464 | tf_op jit(solution)/shard_map/ppermute | solution.py:348
